TPU v7x, 32 devices: a whole 2x2x4 slice. The times are simulated.
32 devices in a mesh: groups: 2 (over y), exp: 4 (over z), patch: 2 (over x), band: 2 (over core).
Axes of the slice: x: 2, y: 2, z: 4, core: 2. Of those that a mesh axis runs over, the one named last changes fastest.
Arguments:
- templates: bfloat16 [8, 8, 256, 256], P(('groups', 'exp'), 'patch', None, 'band'), parts along dimension 0, may hold values from -6 to 6
- exposures: bfloat16 [8, 4, 4, 256, 256], P(('groups', 'exp'), 'patch', None, None, 'band'), parts along dimension 0, may hold values from -6 to 6
- variance: float32 [8, 4, 4, 256, 256], P(('groups', 'exp'), 'patch', None, None, 'band'), parts along dimension 0, may hold values from 0.5 to 4
- coefficients: float32 [8, 4, 4, 27], P(('groups', 'exp'), 'patch'), parts along dimension 0, may hold values from -1.2 to 1.2
- psf_width: float32 [8, 4, 4, 2], P(('groups', 'exp'), 'patch'), parts along dimension 0, may hold values from 1 to 2.5
- patch_ids: int32 [8, 4, 4], P(('groups', 'exp'), 'patch'), parts along dimension 0, may hold values from 0 to 23
- live_count: int32 [8, 4], P(('groups', 'exp'), 'patch'), parts along dimension 0, may hold values from 1 to 4
Outputs:
- coadd_diff: float32 [8, 8, 256, 256], P(('groups', 'exp'), 'patch', None, 'band'), parts along dimension 0
- score: float32 [8, 4, 4, 256, 256], P(('groups', 'exp'), 'patch', None, None, 'band'), parts along dimension 0
There are 2 independent parts, one for each index of `groups`. A program takes and returns all parts, laid end to end along the dimension named above; each array names one. Nothing has to cross between parts.
Inputs may be any that keep to these rules, and one draw needn't show every extreme that they name: `patch_ids`: an id names patch id % 8 of the grid row id // 8 - 1 relative to the exposure's own row. `live_count`: sub-tiles at slots below the count are live.
All inputs are finite; a program needn't handle non-finite values.
Results may differ from a plain program's by a relative error of at most 0.0049.
Values may be sent and summed in bfloat16 or wider, within the bound.
No kernel may reach another device: no remote copies, remote signals or barrier semaphores. Data moves between devices by JAX's collectives and lax.ppermute only.
A program may use at most 64 MiB of HBM per device.

v0:
```python
import jax
import jax.numpy as jnp
import numpy as np
from jax import lax
from jax.sharding import PartitionSpec as P

NB = 27
HW = 10
PW = 7


sigmas = (0.75, 1.5, 3.0)
degrees = (4, 2, 2)


def with_halo(value, sides, width):
    for axis, dim in sides:
        devices, length = (lax.axis_size(axis), value.shape[dim])
        up = [(i, (i + 1) % devices) for i in range(devices - 1)]
        down = [(j, i) for i, j in up]
        last = lax.slice_in_dim(value, length - width, length, axis=dim)
        first = lax.slice_in_dim(value, 0, width, axis=dim)
        before = lax.ppermute(last, axis, up)
        after = lax.ppermute(first, axis, down)
        value = jnp.concatenate([before, value, after], axis=dim)
    return value


def shifted(block, axis, distance):
    devices = range(lax.axis_size(axis))
    route = [(i - distance, i) for i in devices if i - distance in devices]
    return lax.ppermute(block, axis, route)


def basis_terms():
    terms = []
    offset = 0
    for group in range(3):
        for first in range(degrees[group] + 1):
            for second in range(degrees[group] + 1 - first):
                terms.append((group, first, second, offset + first))
        offset = offset + degrees[group] + 1
    return terms


def membership():
    table = np.zeros((27, 11), np.float32)
    for index, term in enumerate(basis_terms()):
        table[index, term[3]] = 1.0
    return table


def profile(offset, sigma, power, reach):
    grid = jnp.arange(-reach, reach + 1).astype(jnp.float32)
    base = jnp.exp(-grid * grid / (2.0 * sigma * sigma)) * (grid / reach) ** power
    scale = jnp.sqrt(jnp.sum(base * base))
    spot = offset.astype(jnp.float32)
    value = jnp.exp(-spot * spot / (2.0 * sigma * sigma)) * (spot / reach) ** power / scale
    return jnp.where(jnp.abs(offset) <= reach, value, jnp.zeros_like(value))


def row_tables(count, reach):
    index = jnp.arange(count, dtype=jnp.int32)
    offset = index[:, None] - index[None, :]
    tables = []
    for group in range(3):
        for first in range(degrees[group] + 1):
            tables.append(profile(offset, sigmas[group], first, reach))
    return jnp.stack(tables).astype(jnp.bfloat16)


def column_tables(cols_in, cols_out, shift, reach):
    inner = jnp.arange(cols_in, dtype=jnp.int32)[:, None]
    outer = jnp.arange(cols_out, dtype=jnp.int32)[None, :]
    offset = outer + shift - inner
    return jnp.stack([profile(offset, sigmas[term[0]], term[2], reach) for term in basis_terms()])


def psf_table(offset, width, reach):
    grid = jnp.arange(-reach, reach + 1).astype(jnp.float32)
    total = jnp.sum(jnp.exp(-grid * grid / (2.0 * width * width)))
    spot = offset.astype(jnp.float32)
    value = jnp.exp(-spot * spot / (2.0 * width * width)) / total
    return jnp.where(jnp.abs(offset) <= reach, value, jnp.zeros_like(value))


def on_device(templates, exposures, variance, coefficients, psf_width, patch_ids, live_count):
    size = templates.shape[2]
    cols = templates.shape[3]
    owned = templates.shape[1]
    slots = patch_ids.shape[2]
    grid_row = lax.all_gather(templates, "patch", axis=1, tiled=True)
    window = with_halo(grid_row, (("exp", 0),), 1)
    patches_row = window.shape[1]
    flat_window = window.reshape(3 * patches_row, size, cols)
    ids = patch_ids.reshape(-1)
    chosen = jnp.take(flat_window, ids, axis=0)
    padded = with_halo(chosen, (("band", 2),), HW)
    gr_flat = row_tables(size, HW).reshape(-1, size)
    col_tab = column_tables(cols + 2 * HW, cols, HW, HW)
    member = jnp.asarray(membership())
    live = (
        (jnp.arange(slots, dtype=jnp.int32)[None, None, :] < live_count[:, :, None])
        .astype(jnp.float32)
        .reshape(-1)
    )
    exp_flat = exposures.reshape(-1, size, cols)
    var_flat = variance.reshape(-1, size, cols)

    def convolve(items):
        template, coeff, exposure, var_tile = items
        rows = (
            jnp.dot(gr_flat, template, preferred_element_type=jnp.float32)
            .astype(jnp.bfloat16)
            .reshape(11, size, cols + 2 * HW)
        )
        mixing = coeff[:, None] * member
        mats = jnp.einsum("kp,kcd->pcd", mixing, col_tab, precision=lax.Precision.HIGHEST).astype(
            jnp.bfloat16
        )
        convolved = jnp.einsum("psc,pcd->sd", rows, mats, preferred_element_type=jnp.float32)
        weight = 1.0 / var_tile
        return ((exposure.astype(jnp.float32) - convolved) * weight, weight.astype(jnp.bfloat16))

    weighted, inverse_low = lax.map(
        convolve, (padded, coefficients.reshape(-1, NB), exp_flat, var_flat)
    )
    stacked = jnp.stack([weighted.astype(jnp.bfloat16), inverse_low])
    widened = with_halo(stacked, (("band", 3),), PW)
    index = jnp.arange(size, dtype=jnp.int32)
    offset_rows = index[:, None] - index[None, :]
    offset_cols = (
        jnp.arange(cols, dtype=jnp.int32)[None, :]
        + PW
        - jnp.arange(cols + 2 * PW, dtype=jnp.int32)[:, None]
    )

    def matched(items):
        weighted_pad, inverse_pad, width, alive = items
        prow = psf_table(offset_rows, width[0], PW)
        pcol = psf_table(offset_cols, width[1], PW)
        numer = jnp.dot(
            prow.astype(jnp.bfloat16), weighted_pad, preferred_element_type=jnp.float32
        ).astype(jnp.bfloat16)
        numer = jnp.dot(numer, pcol.astype(jnp.bfloat16), preferred_element_type=jnp.float32)
        denom = jnp.dot(
            (prow * prow).astype(jnp.bfloat16), inverse_pad, preferred_element_type=jnp.float32
        ).astype(jnp.bfloat16)
        denom = jnp.dot(
            denom, (pcol * pcol).astype(jnp.bfloat16), preferred_element_type=jnp.float32
        )
        return alive * numer / jnp.sqrt(denom)

    score = lax.map(matched, (widened[0], widened[1], psf_width.reshape(-1, 2), live))
    masked = weighted * live[:, None, None]
    onehot = (ids[:, None] == jnp.arange(3 * patches_row, dtype=jnp.int32)[None, :]).astype(
        jnp.float32
    )
    partial_value = jnp.einsum(
        "nq,nsc->qsc", onehot, masked, precision=lax.Precision.HIGHEST
    ).reshape(3, patches_row, size, cols)
    from_below = shifted(partial_value[2].astype(jnp.bfloat16), "exp", 1).astype(jnp.float32)
    from_above = shifted(partial_value[0].astype(jnp.bfloat16), "exp", -1).astype(jnp.float32)
    row_total = partial_value[1] + from_below + from_above
    coadd = lax.psum_scatter(row_total, "patch", scatter_dimension=0, tiled=True)
    return (coadd.reshape(1, owned, size, cols), score.reshape(exposures.shape))


def solution(mesh):
    in_specs = (
        P(("groups", "exp"), "patch", None, "band"),
        P(("groups", "exp"), "patch", None, None, "band"),
        P(("groups", "exp"), "patch", None, None, "band"),
        P(("groups", "exp"), "patch", None, None),
        P(("groups", "exp"), "patch", None, None),
        P(("groups", "exp"), "patch", None),
        P(("groups", "exp"), "patch"),
    )
    out_specs = (
        P(("groups", "exp"), "patch", None, "band"),
        P(("groups", "exp"), "patch", None, None, "band"),
    )
    return jax.shard_map(
        on_device, mesh=mesh, in_specs=in_specs, out_specs=out_specs, check_vma=False
    )
```

profile of v0, /device:TPU:0, one launch (start us, length us, event | category | flops | bytes accessed | tf_op | source)
XLA Modules:
  0.0 269.8 jit_solution(12794665926467850008)
XLA Ops:
  7.2 10.2 %all_gather.3 = bf16[1,8,256,128]{3,2,0,1:T(8,128)(2,1)S(1)} all-gather(bf16[1,4,256,128]{3,2,0,1:T(8,128)(2,1)} %bitcast.122), channel_id=1, replica_groups=mesh['groups'=2,'exp'=4,'patch'=2,'band'=2] {'patch'}, dimensions={1}, use_global_device_ids=true | all-gather | bytes 786432 | tf_op jit(solution)/shard_map/all_gather | solution.py:92
  17.4 3.7 %collective-permute-start = (bf16[1,8,256,128]{3,2,1,0:T(8,128)(2,1)S(1)}, bf16[1,8,256,128]{3,2,1,0:T(8,128)(2,1)S(1)}, u32[]{:S(2)}, u32[]{:S(2)}) collective-permute-start(bf16[1,8,256,128]{3,2,1,0:T(8,128)(2,1)S(1)} %bitcast.117), channel_id=1, source_target_pairs={{0,4},{4,8},{8,12},{1,5},{5,9},{9,13},{2,6},{6,10},{10,14},{3,7},{... | collective-permute-start | bytes 1572872 | tf_op jit(solution)/shard_map/ppermute | solution.py:23
  53.2 10.2 %stack.12 = f32[27,148,128]{2,0,1:T(8,128)S(1)} concatenate(f32[1,148,128]{2,0,1:T(1,128)S(1)} %get-tuple-element.312, f32[1,148,128]{2,0,1:T(1,128)S(1)} %get-tuple-element.313, f32[1,148,128]{2,0,1:T(1,128)S(1)} %get-tuple-element.314, f32[1,148,128]{2,0,1:T(1,128)S(1)} %get-tuple-element.305, f32[1,148,128]{2,0,1:T(1,128)} %get-tuple-element.306, ...), dimensions={0} | concatenate | bytes 4091904 | tf_op jit(solution)/shard_map/stack | solution.py:76
  67.2 82.3 %while.27 = (s32[]{:T(128)}, f32[8,256,128]{2,1,0:T(8,128)}, bf16[8,256,128]{2,1,0:T(8,128)(2,1)}, bf16[8,256,128]{2,1,0:T(8,128)(2,1)}, bf16[8,256,148]{2,1,0:T...) while((s32[]{:T(128)}, f32[8,256,128]{2,1,0:T(8,128)}, ...), condition=%wide.region_12.13_spmd.clone, body=%wide.region_11.12_spmd.sunk.clone.sunk | while | flops 388416288 | bytes 14649461 | solution.py:125
  73.1 2.9 %fusion.127 = f32[8,256,128]{2,1,0:T(8,128)} fusion(f32[8,256,128]{2,1,0:T(8,128)} %get-tuple-element.435, s32[]{:T(128)} %get-tuple-element.434, bf16[11,256,148]{1,0,2:T(8,128)(2,1)} %reshape.773, bf16[11,148,128]{2,0,1:T(8,128)(2,1)} %convolution_convert_fusion.5, bf16[8,256,128]{2,1,0:T(8,128)(2,1)} %get-tuple-element.448, ...), kind=kOutput, calls=%fused_computation.12.clone.1 | convolution fusion | flops 106823680 | bytes 2146816 | tf_op jit(solution)/shard_map/while/body/eval_jaxpr/psc,pcd->sd/dot_general | solution.py:121
  83.4 2.9 %fusion.127 = f32[8,256,128]{2,1,0:T(8,128)} fusion(f32[8,256,128]{2,1,0:T(8,128)} %get-tuple-element.435, s32[]{:T(128)} %get-tuple-element.434, bf16[11,256,148]{1,0,2:T(8,128)(2,1)} %reshape.773, bf16[11,148,128]{2,0,1:T(8,128)(2,1)} %convolution_convert_fusion.5, bf16[8,256,128]{2,1,0:T(8,128)(2,1)} %get-tuple-element.448, ...), kind=kOutput, calls=%fused_computation.12.clone.1 | convolution fusion | flops 106823680 | bytes 2146816 | tf_op jit(solution)/shard_map/while/body/eval_jaxpr/psc,pcd->sd/dot_general | solution.py:121
  93.7 2.9 %fusion.127 = f32[8,256,128]{2,1,0:T(8,128)} fusion(f32[8,256,128]{2,1,0:T(8,128)} %get-tuple-element.435, s32[]{:T(128)} %get-tuple-element.434, bf16[11,256,148]{1,0,2:T(8,128)(2,1)} %reshape.773, bf16[11,148,128]{2,0,1:T(8,128)(2,1)} %convolution_convert_fusion.5, bf16[8,256,128]{2,1,0:T(8,128)(2,1)} %get-tuple-element.448, ...), kind=kOutput, calls=%fused_computation.12.clone.1 | convolution fusion | flops 106823680 | bytes 2146816 | tf_op jit(solution)/shard_map/while/body/eval_jaxpr/psc,pcd->sd/dot_general | solution.py:121
  103.9 2.9 %fusion.127 = f32[8,256,128]{2,1,0:T(8,128)} fusion(f32[8,256,128]{2,1,0:T(8,128)} %get-tuple-element.435, s32[]{:T(128)} %get-tuple-element.434, bf16[11,256,148]{1,0,2:T(8,128)(2,1)} %reshape.773, bf16[11,148,128]{2,0,1:T(8,128)(2,1)} %convolution_convert_fusion.5, bf16[8,256,128]{2,1,0:T(8,128)(2,1)} %get-tuple-element.448, ...), kind=kOutput, calls=%fused_computation.12.clone.1 | convolution fusion | flops 106823680 | bytes 2146816 | tf_op jit(solution)/shard_map/while/body/eval_jaxpr/psc,pcd->sd/dot_general | solution.py:121
  114.2 2.9 %fusion.127 = f32[8,256,128]{2,1,0:T(8,128)} fusion(f32[8,256,128]{2,1,0:T(8,128)} %get-tuple-element.435, s32[]{:T(128)} %get-tuple-element.434, bf16[11,256,148]{1,0,2:T(8,128)(2,1)} %reshape.773, bf16[11,148,128]{2,0,1:T(8,128)(2,1)} %convolution_convert_fusion.5, bf16[8,256,128]{2,1,0:T(8,128)(2,1)} %get-tuple-element.448, ...), kind=kOutput, calls=%fused_computation.12.clone.1 | convolution fusion | flops 106823680 | bytes 2146816 | tf_op jit(solution)/shard_map/while/body/eval_jaxpr/psc,pcd->sd/dot_general | solution.py:121
  124.5 2.9 %fusion.127 = f32[8,256,128]{2,1,0:T(8,128)} fusion(f32[8,256,128]{2,1,0:T(8,128)} %get-tuple-element.435, s32[]{:T(128)} %get-tuple-element.434, bf16[11,256,148]{1,0,2:T(8,128)(2,1)} %reshape.773, bf16[11,148,128]{2,0,1:T(8,128)(2,1)} %convolution_convert_fusion.5, bf16[8,256,128]{2,1,0:T(8,128)(2,1)} %get-tuple-element.448, ...), kind=kOutput, calls=%fused_computation.12.clone.1 | convolution fusion | flops 106823680 | bytes 2146816 | tf_op jit(solution)/shard_map/while/body/eval_jaxpr/psc,pcd->sd/dot_general | solution.py:121
  134.8 2.9 %fusion.127 = f32[8,256,128]{2,1,0:T(8,128)} fusion(f32[8,256,128]{2,1,0:T(8,128)} %get-tuple-element.435, s32[]{:T(128)} %get-tuple-element.434, bf16[11,256,148]{1,0,2:T(8,128)(2,1)} %reshape.773, bf16[11,148,128]{2,0,1:T(8,128)(2,1)} %convolution_convert_fusion.5, bf16[8,256,128]{2,1,0:T(8,128)(2,1)} %get-tuple-element.448, ...), kind=kOutput, calls=%fused_computation.12.clone.1 | convolution fusion | flops 106823680 | bytes 2146816 | tf_op jit(solution)/shard_map/while/body/eval_jaxpr/psc,pcd->sd/dot_general | solution.py:121
  145.1 2.9 %fusion.127 = f32[8,256,128]{2,1,0:T(8,128)} fusion(f32[8,256,128]{2,1,0:T(8,128)} %get-tuple-element.435, s32[]{:T(128)} %get-tuple-element.434, bf16[11,256,148]{1,0,2:T(8,128)(2,1)} %reshape.773, bf16[11,148,128]{2,0,1:T(8,128)(2,1)} %convolution_convert_fusion.5, bf16[8,256,128]{2,1,0:T(8,128)(2,1)} %get-tuple-element.448, ...), kind=kOutput, calls=%fused_computation.12.clone.1 | convolution fusion | flops 106823680 | bytes 2146816 | tf_op jit(solution)/shard_map/while/body/eval_jaxpr/psc,pcd->sd/dot_general | solution.py:121
  156.1 5.4 %collective-permute-start.4 = (bf16[8,256,128]{2,0,1:T(8,128)(2,1)}, bf16[8,256,128]{2,0,1:T(8,128)(2,1)}, u32[]{:S(2)}, u32[]{:S(2)}) collective-permute-start(bf16[8,256,128]{2,0,1:T(8,128)(2,1)} %get-tuple-element.296), channel_id=1, source_target_pairs={{0,4},{4,8},{8,12},{1,5},{5,9},{9,13},{2,6},{6,10},{10,14},{3,7},{... | collective-permute-start | bytes 1572872 | tf_op jit(solution)/shard_map/ppermute | solution.py:32
  162.8 3.4 %collective-permute-start.6 = (bf16[2,8,256,7]{2,1,3,0:T(8,128)(2,1)S(1)}, bf16[2,8,256,7]{2,1,3,0:T(8,128)(2,1)S(1)}, u32[]{:S(2)}, u32[]{:S(2)}) collective-permute-start(bf16[2,8,256,7]{2,1,3,0:T(8,128)(2,1)S(1)} %get-tuple-element.300), channel_id=1, source_target_pairs={{0,1},{2,3},{4,5},{6,7},{8,9},{10,11},{12,13},{14,15},{16,17},{18,... | collective-permute-start | bytes 172040 | tf_op jit(solution)/shard_map/ppermute | solution.py:23
  175.1 2.8 %collective-permute-done.5 = bf16[8,256,128]{2,0,1:T(8,128)(2,1)} collective-permute-done((bf16[8,256,128]{2,0,1:T(8,128)(2,1)}, bf16[8,256,128]{2,0,1:T(8,128)(2,1)}, u32[]{:S(2)}, u32[]{:S(2)}) %collective-permute-start.5) | collective-permute-done | bytes 524320 | tf_op jit(solution)/shard_map/ppermute | solution.py:32
  180.6 81.4 %while.28 = (s32[]{:T(128)}, f32[8,256,128]{2,1,0:T(8,128)S(1)}, f32[8]{0:T(128)S(1)}, f32[8,2]{0,1:T(2,128)S(1)}, bf16[8,256,142]{2,1,0:T(8,128)(2,1)}, /*index...) while((s32[]{:T(128)}, f32[8,256,128]{2,1,0:T(8,128)S(1)}, ...), condition=%wide.region_17.18_spmd.clone.clone, body=%wide.region_14.17_spmd.clone.clone.sunk | while | flops 57732988 | bytes 660701 | solution.py:154
  185.0 3.2 %convolution_multiply_fusion.2 = f32[256,128]{1,0:T(8,128)S(1)} fusion(bf16[8,256,142]{2,1,0:T(8,128)(2,1)} %get-tuple-element.478, s32[]{:T(128)} %get-tuple-element.465, f32[]{:T(128)} %get-tuple-element.421, f32[]{:T(128)S(6)} %mul.999, f32[]{:T(128)} %bitcast.110, s32[128]{0:T(128)S(1)} %get-tuple-element.480, f32[]{:T(128)} %get-tuple-element.422, ...), kind=kOutput, calls=%fused_computation.29.clone.1 | convolution fusion | flops 28824576 | bytes 264712 | tf_op jit(solution)/shard_map/while/body/eval_jaxpr/dot_general | solution.py:145
  195.1 3.2 %convolution_multiply_fusion.2 = f32[256,128]{1,0:T(8,128)S(1)} fusion(bf16[8,256,142]{2,1,0:T(8,128)(2,1)} %get-tuple-element.478, s32[]{:T(128)} %get-tuple-element.465, f32[]{:T(128)} %get-tuple-element.421, f32[]{:T(128)S(6)} %mul.999, f32[]{:T(128)} %bitcast.110, s32[128]{0:T(128)S(1)} %get-tuple-element.480, f32[]{:T(128)} %get-tuple-element.422, ...), kind=kOutput, calls=%fused_computation.29.clone.1 | convolution fusion | flops 28824576 | bytes 264712 | tf_op jit(solution)/shard_map/while/body/eval_jaxpr/dot_general | solution.py:145
  205.3 3.2 %convolution_multiply_fusion.2 = f32[256,128]{1,0:T(8,128)S(1)} fusion(bf16[8,256,142]{2,1,0:T(8,128)(2,1)} %get-tuple-element.478, s32[]{:T(128)} %get-tuple-element.465, f32[]{:T(128)} %get-tuple-element.421, f32[]{:T(128)S(6)} %mul.999, f32[]{:T(128)} %bitcast.110, s32[128]{0:T(128)S(1)} %get-tuple-element.480, f32[]{:T(128)} %get-tuple-element.422, ...), kind=kOutput, calls=%fused_computation.29.clone.1 | convolution fusion | flops 28824576 | bytes 264712 | tf_op jit(solution)/shard_map/while/body/eval_jaxpr/dot_general | solution.py:145
  215.5 3.2 %convolution_multiply_fusion.2 = f32[256,128]{1,0:T(8,128)S(1)} fusion(bf16[8,256,142]{2,1,0:T(8,128)(2,1)} %get-tuple-element.478, s32[]{:T(128)} %get-tuple-element.465, f32[]{:T(128)} %get-tuple-element.421, f32[]{:T(128)S(6)} %mul.999, f32[]{:T(128)} %bitcast.110, s32[128]{0:T(128)S(1)} %get-tuple-element.480, f32[]{:T(128)} %get-tuple-element.422, ...), kind=kOutput, calls=%fused_computation.29.clone.1 | convolution fusion | flops 28824576 | bytes 264712 | tf_op jit(solution)/shard_map/while/body/eval_jaxpr/dot_general | solution.py:145
  225.7 3.2 %convolution_multiply_fusion.2 = f32[256,128]{1,0:T(8,128)S(1)} fusion(bf16[8,256,142]{2,1,0:T(8,128)(2,1)} %get-tuple-element.478, s32[]{:T(128)} %get-tuple-element.465, f32[]{:T(128)} %get-tuple-element.421, f32[]{:T(128)S(6)} %mul.999, f32[]{:T(128)} %bitcast.110, s32[128]{0:T(128)S(1)} %get-tuple-element.480, f32[]{:T(128)} %get-tuple-element.422, ...), kind=kOutput, calls=%fused_computation.29.clone.1 | convolution fusion | flops 28824576 | bytes 264712 | tf_op jit(solution)/shard_map/while/body/eval_jaxpr/dot_general | solution.py:145
  235.8 3.2 %convolution_multiply_fusion.2 = f32[256,128]{1,0:T(8,128)S(1)} fusion(bf16[8,256,142]{2,1,0:T(8,128)(2,1)} %get-tuple-element.478, s32[]{:T(128)} %get-tuple-element.465, f32[]{:T(128)} %get-tuple-element.421, f32[]{:T(128)S(6)} %mul.999, f32[]{:T(128)} %bitcast.110, s32[128]{0:T(128)S(1)} %get-tuple-element.480, f32[]{:T(128)} %get-tuple-element.422, ...), kind=kOutput, calls=%fused_computation.29.clone.1 | convolution fusion | flops 28824576 | bytes 264712 | tf_op jit(solution)/shard_map/while/body/eval_jaxpr/dot_general | solution.py:145
  246.0 3.2 %convolution_multiply_fusion.2 = f32[256,128]{1,0:T(8,128)S(1)} fusion(bf16[8,256,142]{2,1,0:T(8,128)(2,1)} %get-tuple-element.478, s32[]{:T(128)} %get-tuple-element.465, f32[]{:T(128)} %get-tuple-element.421, f32[]{:T(128)S(6)} %mul.999, f32[]{:T(128)} %bitcast.110, s32[128]{0:T(128)S(1)} %get-tuple-element.480, f32[]{:T(128)} %get-tuple-element.422, ...), kind=kOutput, calls=%fused_computation.29.clone.1 | convolution fusion | flops 28824576 | bytes 264712 | tf_op jit(solution)/shard_map/while/body/eval_jaxpr/dot_general | solution.py:145
  256.2 3.2 %convolution_multiply_fusion.2 = f32[256,128]{1,0:T(8,128)S(1)} fusion(bf16[8,256,142]{2,1,0:T(8,128)(2,1)} %get-tuple-element.478, s32[]{:T(128)} %get-tuple-element.465, f32[]{:T(128)} %get-tuple-element.421, f32[]{:T(128)S(6)} %mul.999, f32[]{:T(128)} %bitcast.110, s32[128]{0:T(128)S(1)} %get-tuple-element.480, f32[]{:T(128)} %get-tuple-element.422, ...), kind=kOutput, calls=%fused_computation.29.clone.1 | convolution fusion | flops 28824576 | bytes 264712 | tf_op jit(solution)/shard_map/while/body/eval_jaxpr/dot_general | solution.py:145
  (186 shorter events, 144.1 us)
Async XLA Ops:
  7.2 254.9 %reduce-scatter.2.cloned.1.call-start = ((), (), s32[]{:S(2)}) async-start(), calls=%async_computation.1 | async-start | bytes 1572864 | tf_op jit(solution)/shard_map/reduce_scatter | solution.py:165
  17.4 24.9 %copy-start.5 = (bf16[1,8,256,128]{3,2,0,1:T(8,128)(2,1)}, bf16[1,8,256,128]{3,2,0,1:T(8,128)(2,1)S(1)}, u32[]{:S(2)}) copy-start(bf16[1,8,256,128]{3,2,0,1:T(8,128)(2,1)S(1)} %all_gather.3) | copy-start | bytes 1572868
  17.4 24.9 %collective-permute-start = (bf16[1,8,256,128]{3,2,1,0:T(8,128)(2,1)S(1)}, bf16[1,8,256,128]{3,2,1,0:T(8,128)(2,1)S(1)}, u32[]{:S(2)}, u32[]{:S(2)}) collective-permute-start(bf16[1,8,256,128]{3,2,1,0:T(8,128)(2,1)S(1)} %bitcast.117), channel_id=1, source_target_pairs={{0,4},{4,8},{8,12},{1,5},{5,9},{9,13},{2,6},{6,10},{10,14},{3,7},{... | collective-permute-start | bytes 1572872 | tf_op jit(solution)/shard_map/ppermute | solution.py:23
  21.1 22.0 %collective-permute-start.1 = (bf16[1,8,256,128]{3,2,1,0:T(8,128)(2,1)S(1)}, bf16[1,8,256,128]{3,2,1,0:T(8,128)(2,1)}, u32[]{:S(2)}, u32[]{:S(2)}) collective-permute-start(bf16[1,8,256,128]{3,2,1,0:T(8,128)(2,1)S(1)} %bitcast.118), channel_id=1, source_target_pairs={{4,0},{8,4},{12,8},{5,1},{9,5},{13,9},{6,2},{10,6},{14,10},{7,3},{... | collective-permute-start | bytes 1572872 | tf_op jit(solution)/shard_map/ppermute | solution.py:24
  46.0 6.0 %copy-start.9 = (f32[1,2,4,2]{2,3,1,0:T(2,128)S(1)}, f32[1,2,4,2]{2,3,1,0:T(2,128)}, u32[]{:S(2)}) copy-start(f32[1,2,4,2]{2,3,1,0:T(2,128)} %param.16) | copy-start | bytes 196
  48.4 15.0 %collective-permute-start.2 = (bf16[8,256,10]{2,1,0:T(8,128)(2,1)}, bf16[8,256,10]{2,1,0:T(8,128)(2,1)}, u32[]{:S(2)}, u32[]{:S(2)}) collective-permute-start(bf16[8,256,10]{2,1,0:T(8,128)(2,1)} %get-tuple-element.302), channel_id=1, source_target_pairs={{0,1},{2,3},{4,5},{6,7},{8,9},{10,11},{12,13},{14,15},{16,17},{18,... | collective-permute-start | bytes 122888 | tf_op jit(solution)/shard_map/ppermute | solution.py:23
  50.5 12.9 %collective-permute-start.3 = (bf16[8,256,10]{2,1,0:T(8,128)(2,1)}, bf16[8,256,10]{2,1,0:T(8,128)(2,1)}, u32[]{:S(2)}, u32[]{:S(2)}) collective-permute-start(bf16[8,256,10]{2,1,0:T(8,128)(2,1)} %get-tuple-element.303), channel_id=1, source_target_pairs={{1,0},{3,2},{5,4},{7,6},{9,8},{11,10},{13,12},{15,14},{17,16},{19,... | collective-permute-start | bytes 122888 | tf_op jit(solution)/shard_map/ppermute | solution.py:24
  52.0 1.1 copy-start
  63.3 3.9 %copy-start.8 = (f32[27,11]{0,1:T(8,128)S(1)}, f32[27,11]{0,1:T(8,128)}, u32[]{:S(2)}) copy-start(f32[27,11]{0,1:T(8,128)} %constant.118.clone..sunk.2) | copy-start | bytes 3568
  67.9 2.1 copy-start.1
  78.2 2.1 copy-start.1
  88.5 2.1 copy-start.1
  98.8 2.1 copy-start.1
  109.0 2.1 copy-start.1
  119.3 2.1 copy-start.1
  129.6 2.1 copy-start.1
  139.9 2.1 copy-start.1
  149.5 2.3 copy-start.2
  155.0 7.7 %copy-start.3 = (bf16[8,256,128]{1,0,2:T(8,128)(2,1)S(1)}, bf16[8,256,128]{1,0,2:T(8,128)(2,1)}, u32[]{:S(2)}) copy-start(bf16[8,256,128]{1,0,2:T(8,128)(2,1)} %copy.37) | copy-start | bytes 1572868
  155.1 7.7 %copy-start.4 = (bf16[8,256,128]{1,0,2:T(8,128)(2,1)S(1)}, bf16[8,256,128]{1,0,2:T(8,128)(2,1)}, u32[]{:S(2)}) copy-start(bf16[8,256,128]{1,0,2:T(8,128)(2,1)} %copy.38) | copy-start | bytes 1572868
  156.1 19.0 %collective-permute-start.4 = (bf16[8,256,128]{2,0,1:T(8,128)(2,1)}, bf16[8,256,128]{2,0,1:T(8,128)(2,1)}, u32[]{:S(2)}, u32[]{:S(2)}) collective-permute-start(bf16[8,256,128]{2,0,1:T(8,128)(2,1)} %get-tuple-element.296), channel_id=1, source_target_pairs={{0,4},{4,8},{8,12},{1,5},{5,9},{9,13},{2,6},{6,10},{10,14},{3,7},{... | collective-permute-start | bytes 1572872 | tf_op jit(solution)/shard_map/ppermute | solution.py:32
  161.5 16.5 %collective-permute-start.5 = (bf16[8,256,128]{2,0,1:T(8,128)(2,1)}, bf16[8,256,128]{2,0,1:T(8,128)(2,1)}, u32[]{:S(2)}, u32[]{:S(2)}) collective-permute-start(bf16[8,256,128]{2,0,1:T(8,128)(2,1)} %get-tuple-element.297), channel_id=1, source_target_pairs={{4,0},{8,4},{12,8},{5,1},{9,5},{13,9},{6,2},{10,6},{14,10},{7,3},{... | collective-permute-start | bytes 1572872 | tf_op jit(solution)/shard_map/ppermute | solution.py:32
  162.8 4.7 %collective-permute-start.6 = (bf16[2,8,256,7]{2,1,3,0:T(8,128)(2,1)S(1)}, bf16[2,8,256,7]{2,1,3,0:T(8,128)(2,1)S(1)}, u32[]{:S(2)}, u32[]{:S(2)}) collective-permute-start(bf16[2,8,256,7]{2,1,3,0:T(8,128)(2,1)S(1)} %get-tuple-element.300), channel_id=1, source_target_pairs={{0,1},{2,3},{4,5},{6,7},{8,9},{10,11},{12,13},{14,15},{16,17},{18,... | collective-permute-start | bytes 172040 | tf_op jit(solution)/shard_map/ppermute | solution.py:23
  166.2 3.1 %collective-permute-start.7 = (bf16[2,8,256,7]{2,1,3,0:T(8,128)(2,1)S(1)}, bf16[2,8,256,7]{2,1,3,0:T(8,128)(2,1)S(1)}, u32[]{:S(2)}, u32[]{:S(2)}) collective-permute-start(bf16[2,8,256,7]{2,1,3,0:T(8,128)(2,1)S(1)} %get-tuple-element.301), channel_id=1, source_target_pairs={{1,0},{3,2},{5,4},{7,6},{9,8},{11,10},{13,12},{15,14},{17,16},{19,... | collective-permute-start | bytes 172040 | tf_op jit(solution)/shard_map/ppermute | solution.py:24
  (2 other events, 1.8 us)
Sparse Core Ops, SparseCore 0:
  180.7 20.5 reduce-scatter.1
where the time goes:
time: 273 us; the launch traced here: 270 us
  matrix products  100 us (37%)
  local copies, waits for them, and re-layouts  58.4 us (21%)
  other arithmetic  34.9 us (13%)
  between operations  21.7 us (8%)
  starting transfers between devices  19.9 us (7%)
  loops' own time  19.9 us (7%)
  blocking collectives  10.2 us (4%)
  waiting for transfers between devices  4.71 us (2%)
    dot_general x8, matrix products, matched(): jnp.dot(numer, pcol.astype(jnp.bfloat16), preferred_element_type=jnp.floa...  25.7 us
    dot_general x8, matrix products, convolve(): jnp.einsum('psc,pcd->sd', rows, mats, preferred_element_type=jnp.float32)  22.8 us
    dot_general x8, matrix products, matched(): jnp.dot(denom, (pcol * pcol).astype(jnp.bfloat16), preferred_element_type...  20.9 us
    another operation x1, loops' own time, on_device(): lax.map(matched, (widened[0], widened[1], psf_width.reshape(-1, 2), live))  19.9 us
    dot_general x8, matrix products, convolve(): jnp.einsum('kp,kcd->pcd', mixing, col_tab, precision=lax.Precision.HIGHEST)  16.7 us
    reshape x8, local copies, waits for them, and re-layouts, convolve(): rows = jnp.dot(gr_flat, template, preferred_element_type=jnp.float32).ast...  12.6 us
    dynamic_update_slice x8, other arithmetic, on_device(): lax.map(convolve, (padded, coefficients.reshape(-1, NB), exp_flat, var_fl...  12.5 us
    dot_general x8, matrix products, convolve(): jnp.dot(gr_flat, template, preferred_element_type=jnp.float32)  12.1 us
  transfers between devices with their start and end apart: 9, of which 2 were waited for; matrix products, arithmetic and copies ran while one was open for 33% of the time, Pallas kernels for 0%

commit v1 on v0

v1 whole, which is shorter than its diff:
```python
import functools

import jax
import jax.numpy as jnp
import numpy as np
from jax import lax
from jax.experimental import pallas as pl
from jax.experimental.pallas import tpu as pltpu
from jax.sharding import PartitionSpec as P

HW = 10
PW = 7

sigmas = (0.75, 1.5, 3.0)
degrees = (4, 2, 2)

VMEM = pltpu.VMEM
SMEM = pltpu.SMEM


def shifted(block, axis, distance):
    devices = range(lax.axis_size(axis))
    route = [(i - distance, i) for i in devices if i - distance in devices]
    return lax.ppermute(block, axis, route)


def fetched(block, axis, distance):
    devices = lax.axis_size(axis)
    return lax.ppermute(block, axis, [((i + distance) % devices, i) for i in range(devices)])


def sent(block, axis, distance):
    devices = lax.axis_size(axis)
    return lax.ppermute(block, axis, [(i, (i + distance) % devices) for i in range(devices)])


def basis_terms():
    terms = []
    offset = 0
    for group in range(3):
        for first in range(degrees[group] + 1):
            for second in range(degrees[group] + 1 - first):
                terms.append((group, first, second, offset + first))
        offset = offset + degrees[group] + 1
    return terms


def profile(offset, sigma, power, reach):
    grid = np.arange(-reach, reach + 1).astype(np.float32)
    base = np.exp(-grid * grid / np.float32(2.0 * sigma * sigma)) * (grid / reach) ** power
    scale = np.sqrt(np.sum(base * base))
    spot = offset.astype(np.float32)
    value = np.exp(-spot * spot / np.float32(2.0 * sigma * sigma)) * (spot / reach) ** power / scale
    return np.where(np.abs(offset) <= reach, value, 0.0).astype(np.float32)


def row_tables(count, reach):
    index = np.arange(count)
    offset = index[:, None] - index[None, :]
    tables = []
    for group in range(3):
        for first in range(degrees[group] + 1):
            tables.append(profile(offset, sigmas[group], first, reach))
    return np.stack(tables)


def ring_offset(width):
    lane = np.arange(width)
    return np.where(lane < width // 2, lane, lane - width)


def ring_profiles(width, reach):
    offset = ring_offset(width)
    return np.stack([profile(offset, sigmas[t[0]], t[2], reach) for t in basis_terms()])


def prepare_kernel(width_ref, live_ref, core_ref, coeff_ref, ring_ref, own_ref, other_ref,
                   norm_ref, inv_ref, prow_ref, pcol_ref, mats_ref, dist_ref, near_ref):
    tiles, size, cols = own_ref.shape
    wide = 2 * cols
    rows = lax.broadcasted_iota(jnp.int32, (size, size), 0)
    across = lax.broadcasted_iota(jnp.int32, (size, size), 1)
    gap = rows - across
    dist_ref[...] = (gap * gap).astype(jnp.float32)
    inner = lax.broadcasted_iota(jnp.int32, (wide, wide), 0)
    outer = lax.broadcasted_iota(jnp.int32, (wide, wide), 1)
    ring = jnp.abs(inner - outer)
    ring = jnp.minimum(ring, wide - ring)
    near_ref[...] = (ring * ring).astype(jnp.float32)
    lane = lax.broadcasted_iota(jnp.int32, (size, cols), 1)
    half = cols // 2
    keep = (lane >= half) == (core_ref[0] == 1)
    limit = float(PW * PW)
    spot = lax.broadcasted_iota(jnp.int32, (8, 128), 1)
    spot_low = spot.astype(jnp.float32) - PW

    terms = basis_terms()
    profiles = max(t[3] for t in terms) + 1

    def scale_of(width):
        rate = -0.5 / (width * width)
        base = jnp.where(spot <= 2 * PW, jnp.exp(spot_low * spot_low * rate), 0.0)
        return rate, 1.0 / jnp.sum(base[0:1], axis=1, keepdims=True)

    def one(t, carry):
        inv_own = 1.0 / own_ref[t]
        inv_other = jnp.where(keep, 1.0 / other_ref[t], 0.0)
        inv_ref[t, :, :cols] = inv_own
        inv_ref[t, :, cols:] = inv_other
        inv_low = jnp.concatenate([inv_own, inv_other], axis=1).astype(jnp.bfloat16)
        rate, scale = scale_of(jnp.full((8, 128), width_ref[t, 0], jnp.float32))
        rate = rate[0:1, 0:1]
        dist = dist_ref[...]
        prow = jnp.where(dist <= limit, jnp.exp(dist * rate) * scale, 0.0)
        prow_ref[t] = prow.astype(jnp.bfloat16)
        qrow = (prow * prow).astype(jnp.bfloat16)
        rate, scale = scale_of(jnp.full((8, 128), width_ref[t, 1], jnp.float32))
        rate = rate[0:1, 0:1]
        near = near_ref[:, :cols]
        pcol = jnp.where(near <= limit, jnp.exp(near * rate) * scale, 0.0)
        pcol_ref[t] = pcol.astype(jnp.bfloat16)
        qcol = (pcol * pcol).astype(jnp.bfloat16)
        denom = jnp.dot(qrow, inv_low, preferred_element_type=jnp.float32).astype(jnp.bfloat16)
        denom = jnp.dot(denom, qcol, preferred_element_type=jnp.float32)
        norm_ref[t] = live_ref[t] / jnp.sqrt(denom)
        for p in range(profiles):
            vec = jnp.zeros((1, wide), jnp.float32)
            for k, term in enumerate(terms):
                if term[3] == p:
                    vec = vec + coeff_ref[t, k] * ring_ref[k : k + 1, :]
            full = jnp.broadcast_to(vec, (wide, wide))
            full = pltpu.roll(full, 0, 1, stride=1, stride_axis=0)
            mats_ref[t, p * wide : (p + 1) * wide, :] = full.astype(jnp.bfloat16)
        return carry

    lax.fori_loop(0, tiles, one, 0)


def convolve_kernel(blocks, slots_ref, part_ref, live_ref, core_ref, *refs):
    own_blocks = refs[:blocks]
    other_blocks = refs[blocks : 2 * blocks]
    (gr_ref, exp_ref, expo_ref, inv_ref, mats_ref) = refs[2 * blocks : 2 * blocks + 5]
    low_ref = refs[2 * blocks + 5]
    out_refs = refs[2 * blocks + 6 : 3 * blocks + 6]
    tile_ref, rows_ref, acc_ref, sem = refs[3 * blocks + 6 :]
    tiles, size, wide = tile_ref.shape
    cols = wide // 2
    owned = own_blocks[0].shape[0]
    profiles = rows_ref.shape[1] // wide
    half = cols // 2

    def copies(t, b):
        slot = slots_ref[t]
        return (
            pltpu.make_async_copy(own_blocks[b].at[slot], tile_ref.at[t, :, pl.ds(0, cols)], sem.at[t, 0]),
            pltpu.make_async_copy(other_blocks[b].at[slot], tile_ref.at[t, :, pl.ds(cols, cols)], sem.at[t, 1]),
        )

    for t in range(tiles):
        for b in range(blocks):
            @pl.when(part_ref[t] == b)
            def _(t=t, b=b):
                for c in copies(t, b):
                    c.start()

    acc_ref[...] = jnp.zeros_like(acc_ref)
    lane = lax.broadcasted_iota(jnp.int32, (size, cols), 1)
    keep = (lane >= half) == (core_ref[0] == 1)

    def one(t, carry):
        for c in copies(t, 0):
            c.wait()
        other = tile_ref[t, :, cols:]
        other = jnp.where(keep, other.astype(jnp.float32), 0.0).astype(jnp.bfloat16)
        tile = jnp.concatenate([tile_ref[t, :, :cols], other], axis=1)
        for p in range(profiles):
            rows_ref[:, p * wide : (p + 1) * wide] = jnp.dot(
                gr_ref[p * size : (p + 1) * size, :], tile, preferred_element_type=jnp.float32
            ).astype(jnp.bfloat16)
        convolved = jnp.dot(rows_ref[...], mats_ref[t], preferred_element_type=jnp.float32)
        own = (exp_ref[t].astype(jnp.float32) - convolved[:, :cols]) * inv_ref[t, :, :cols]
        other = (expo_ref[t].astype(jnp.float32) - convolved[:, cols:]) * inv_ref[t, :, cols:]
        low_ref[t, :, :cols] = own.astype(jnp.bfloat16)
        low_ref[t, :, cols:] = other.astype(jnp.bfloat16)
        where = part_ref[t] * owned + slots_ref[t]
        acc_ref[where] += live_ref[t] * own
        return carry

    lax.fori_loop(0, tiles, one, 0)
    for b in range(blocks):
        out_refs[b][...] = acc_ref[b * owned : (b + 1) * owned].astype(out_refs[b].dtype)


def score_kernel(low_ref, prow_ref, pcol_ref, norm_ref, score_ref):
    tiles = low_ref.shape[0]

    def one(t, carry):
        numer = jnp.dot(prow_ref[t], low_ref[t], preferred_element_type=jnp.float32)
        numer = numer.astype(jnp.bfloat16)
        numer = jnp.dot(numer, pcol_ref[t], preferred_element_type=jnp.float32)
        score_ref[t] = numer * norm_ref[t]
        return carry

    lax.fori_loop(0, tiles, one, 0)


def shape(dims, dtype):
    return jax.ShapeDtypeStruct(dims, dtype)


def vmem(count):
    return [pl.BlockSpec(memory_space=VMEM)] * count


def smem(count):
    return [pl.BlockSpec(memory_space=SMEM)] * count


def anywhere(count):
    return [pl.BlockSpec(memory_space=pl.ANY)] * count


def on_device(templates, exposures, variance, coefficients, psf_width, patch_ids, live_count):
    size = templates.shape[2]
    cols = templates.shape[3]
    owned = templates.shape[1]
    slots = patch_ids.shape[2]
    wide = 2 * cols
    across = lax.axis_size("patch")
    patches_row = owned * across
    blocks = 3 * across
    me = lax.axis_index("patch")
    core = lax.axis_index("band").astype(jnp.int32).reshape(1)
    low = jnp.bfloat16

    own = templates.reshape(owned, size, cols)
    exp_flat = exposures.reshape(-1, size, cols)
    var_flat = variance.reshape(-1, size, cols)
    tiles = exp_flat.shape[0]
    swap = functools.partial(sent, axis="band", distance=1)

    below = shifted(own, "exp", 1)
    above = shifted(own, "exp", -1)
    row = [own] + [fetched(own, "patch", d) for d in range(1, across)]
    rows_below = [below] + [shifted(row[d], "exp", 1) for d in range(1, across)]
    rows_above = [above] + [shifted(row[d], "exp", -1) for d in range(1, across)]
    window = rows_below + row + rows_above
    window_other = [swap(b) for b in window]
    var_other = swap(var_flat)
    exp_other = swap(exp_flat)

    ids = patch_ids.reshape(-1)
    column = ids % patches_row
    shift = (column // owned - me + across) % across
    part = (ids // patches_row) * across + shift
    slot = column % owned
    live = (
        (jnp.arange(slots, dtype=jnp.int32)[None, None, :] < live_count[:, :, None])
        .astype(jnp.float32)
        .reshape(-1)
    )
    coeff = coefficients.reshape(tiles, -1)
    width = psf_width.reshape(tiles, 2)
    gr = jnp.asarray(row_tables(size, HW), dtype=low)
    profiles = gr.shape[0]
    gr = gr.reshape(-1, size)
    ring = jnp.asarray(ring_profiles(wide, HW))

    norm, inv, prow, pcol, mats = pl.pallas_call(
        prepare_kernel,
        name="prepare",
        out_shape=(
            shape((tiles, size, cols), jnp.float32),
            shape((tiles, size, wide), jnp.float32),
            shape((tiles, size, size), low),
            shape((tiles, wide, cols), low),
            shape((tiles, profiles * wide, wide), low),
        ),
        in_specs=smem(4) + vmem(3),
        out_specs=tuple(vmem(5)),
        scratch_shapes=[VMEM((size, size), jnp.float32), VMEM((wide, wide), jnp.float32)],
    )(width, live, core, coeff, ring, var_flat, var_other)

    outs = pl.pallas_call(
        functools.partial(convolve_kernel, blocks),
        name="convolve",
        out_shape=tuple(
            [shape((tiles, size, wide), low)]
            + [
                shape((owned, size, cols), jnp.float32 if b == across else low)
                for b in range(blocks)
            ]
        ),
        in_specs=smem(4) + anywhere(2 * blocks) + vmem(5),
        out_specs=tuple(vmem(1 + blocks)),
        scratch_shapes=[
            VMEM((tiles, size, wide), low),
            VMEM((size, profiles * wide), low),
            VMEM((blocks * owned, size, cols), jnp.float32),
            pltpu.SemaphoreType.DMA((tiles, 2)),
        ],
    )(slot, part, live, core, *window, *window_other, gr, exp_flat, exp_other, inv, mats)
    weighted_low = outs[0]
    parts = outs[1:]

    from_below = [shifted(parts[2 * across + d], "exp", 1) for d in range(across)]
    from_above = [shifted(parts[d], "exp", -1) for d in range(across)]
    total = parts[across] + from_below[0].astype(jnp.float32) + from_above[0].astype(jnp.float32)
    for d in range(1, across):
        merged = (
            parts[across + d].astype(jnp.float32)
            + from_below[d].astype(jnp.float32)
            + from_above[d].astype(jnp.float32)
        ).astype(low)
        total = total + sent(merged, "patch", d).astype(jnp.float32)

    score = pl.pallas_call(
        score_kernel,
        name="score",
        out_shape=shape((tiles, size, cols), jnp.float32),
        in_specs=vmem(4),
        out_specs=vmem(1)[0],
    )(weighted_low, prow, pcol, norm)
    return (total.reshape(1, owned, size, cols), score.reshape(exposures.shape))


def solution(mesh):
    assert mesh.shape["band"] == 2
    in_specs = (
        P(("groups", "exp"), "patch", None, "band"),
        P(("groups", "exp"), "patch", None, None, "band"),
        P(("groups", "exp"), "patch", None, None, "band"),
        P(("groups", "exp"), "patch", None, None),
        P(("groups", "exp"), "patch", None, None),
        P(("groups", "exp"), "patch", None),
        P(("groups", "exp"), "patch"),
    )
    out_specs = (
        P(("groups", "exp"), "patch", None, "band"),
        P(("groups", "exp"), "patch", None, None, "band"),
    )
    return jax.shard_map(
        on_device, mesh=mesh, in_specs=in_specs, out_specs=out_specs, check_vma=False
    )
```

time: 273 us -> 81.3 us (0.30)
  matrix products: 100 us -> 0 us
  local copies, waits for them, and re-layouts: 58.4 us -> 3.74 us
  Pallas kernels: 0 us -> 32.9 us
  other arithmetic: 34.9 us -> 3.64 us
  between operations: 21.7 us -> 0.88 us
  loops' own time: 19.9 us -> 0 us
  blocking collectives: 10.2 us -> 0 us
  starting transfers between devices: 19.9 us -> 29.1 us
  waiting for transfers between devices: 4.71 us -> 10.6 us
    dot_general x41 -> x0, matrix products: 100 us -> none  [the longest x8 25.7 us: matched(): jnp.dot(numer, pcol.astype(jnp.bfloat16), preferred_element_type=jnp.floa...]
    pallas_call x0 -> x3, Pallas kernels: none -> 32.9 us  [the longest x1 16.5 us: on_device(): pl.pallas_call(functools.partial(convolve_kernel, blocks), name='convolve...]
    another operation x2 -> x0, loops' own time: 19.9 us -> none  [the longest x1 19.9 us: on_device(): lax.map(matched, (widened[0], widened[1], psf_width.reshape(-1, 2), live))]
    ppermute x2 -> x8, starting transfers between devices: 6.64 us -> 23 us  [shifted(): return lax.ppermute(block, axis, route)]
    dynamic_update_slice x8 -> x0, other arithmetic: 12.5 us -> none  [on_device(): lax.map(convolve, (padded, coefficients.reshape(-1, NB), exp_flat, var_fl...]
    reduce_sum x19 -> x0, other arithmetic: 12.3 us -> none  [the longest x11 7.14 us: profile(): scale = jnp.sqrt(jnp.sum(base * base))]
    reshape x9 -> x1, local copies, waits for them, and re-layouts: 12.7 us -> 1.36 us  [on_device(): width = psf_width.reshape(tiles, 2)]
    another operation x3 -> x0, local copies, waits for them, and re-layouts: 11.3 us -> none  [the longest x1 10.2 us: column_tables(): jnp.stack([profile(offset, sigmas[term[0]], term[2], reach) for term in b...]
  transfers between devices with their start and end apart: 9 -> 18, of which waited for: 2 -> 4; matrix products, arithmetic and copies ran while one was open for 33% -> 7% of each run, Pallas kernels for 0% -> 20%
where the time goes in v1:
time: 81.3 us; the launch traced here: 80.8 us
  Pallas kernels  32.9 us (40%)
  starting transfers between devices  29.1 us (36%)
  waiting for transfers between devices  10.6 us (13%)
  local copies, waits for them, and re-layouts  3.74 us (5%)
  other arithmetic  3.64 us (4%)
  between operations  0.88 us (1%)
    ppermute x8, starting transfers between devices, shifted(): return lax.ppermute(block, axis, route)  23 us
    pallas_call x1, Pallas kernels, on_device(): pl.pallas_call(functools.partial(convolve_kernel, blocks), name='convolve...  16.5 us
    pallas_call x1, Pallas kernels, on_device(): pl.pallas_call(prepare_kernel, name='prepare', out_shape=(shape((tiles, s...  10.7 us
    ppermute x8, waiting for transfers between devices, shifted(): return lax.ppermute(block, axis, route)  10.6 us
    pallas_call x1, Pallas kernels, on_device(): pl.pallas_call(score_kernel, name='score', out_shape=shape((tiles, size,...  5.74 us
    ppermute x9, starting transfers between devices, sent(): lax.ppermute(block, axis, [(i, (i + distance) % devices) for i in range(d...  3.46 us
    ppermute x1, starting transfers between devices, fetched(): lax.ppermute(block, axis, [((i + distance) % devices, i) for i in range(d...  2.57 us
  transfers between devices with their start and end apart: 18, of which 4 were waited for; matrix products, arithmetic and copies ran while one was open for 7% of the time, Pallas kernels for 20%

profile of v1, /device:TPU:0, one launch (start us, length us, event | category | flops | bytes accessed | tf_op | source)
XLA Modules:
  0.0 80.8 jit_solution(4168127816153658977)
XLA Ops:
  1.2 1.3 %collective-permute-start.3 = (bf16[4,256,128]{2,1,0:T(8,128)(2,1)}, bf16[4,256,128]{2,1,0:T(8,128)(2,1)S(1)}, u32[]{:S(2)}, u32[]{:S(2)}) collective-permute-start(bf16[4,256,128]{2,1,0:T(8,128)(2,1)} %bitcast.17), channel_id=1, source_target_pairs={{4,0},{8,4},{12,8},{5,1},{9,5},{13,9},{6,2},{10,6},{14,10},{7,3},{... | collective-permute-start | bytes 786440 | tf_op jit(solution)/shard_map/ppermute | solution.py:24
  2.5 2.6 %collective-permute-start.1 = (bf16[4,256,128]{2,1,0:T(8,128)(2,1)}, bf16[4,256,128]{2,1,0:T(8,128)(2,1)S(1)}, u32[]{:S(2)}, u32[]{:S(2)}) collective-permute-start(bf16[4,256,128]{2,1,0:T(8,128)(2,1)} %bitcast.18), channel_id=1, source_target_pairs={{2,0},{0,2},{3,1},{1,3},{6,4},{4,6},{7,5},{5,7},{10,8},{8,10},{11,... | collective-permute-start | bytes 786440 | tf_op jit(solution)/shard_map/ppermute | solution.py:29
  5.2 4.4 %collective-permute-start = (bf16[4,256,128]{2,1,0:T(8,128)(2,1)}, bf16[4,256,128]{2,1,0:T(8,128)(2,1)S(1)}, u32[]{:S(2)}, u32[]{:S(2)}) collective-permute-start(bf16[4,256,128]{2,1,0:T(8,128)(2,1)} %bitcast.20), channel_id=1, source_target_pairs={{0,4},{4,8},{8,12},{1,5},{5,9},{9,13},{2,6},{6,10},{10,14},{3,7},{... | collective-permute-start | bytes 786440 | tf_op jit(solution)/shard_map/ppermute | solution.py:24
  9.6 3.2 %collective-permute-done.3.refs_4_ = bf16[4,256,128]{2,1,0:T(8,128)(2,1)S(1)} collective-permute-done((bf16[4,256,128]{2,1,0:T(8,128)(2,1)}, bf16[4,256,128]{2,1,0:T(8,128)(2,1)S(1)}, u32[]{:S(2)}, u32[]{:S(2)}) %collective-permute-start.3) | collective-permute-done | bytes 262176 | tf_op jit(solution)/shard_map/ppermute | solution.py:24
  12.8 1.3 %collective-permute-start.4 = (bf16[4,256,128]{2,1,0:T(8,128)(2,1)S(1)}, bf16[4,256,128]{2,1,0:T(8,128)(2,1)S(1)}, u32[]{:S(2)}, u32[]{:S(2)}) collective-permute-start(bf16[4,256,128]{2,1,0:T(8,128)(2,1)S(1)} %collective-permute-done.1.refs_3_), channel_id=1, source_target_pairs={{4,0},{8,4},{12,8},{5,1},{9,5},{13,9},{6,2},{10,6},{14,10},{7,3},{... | collective-permute-start | bytes 786440 | tf_op jit(solution)/shard_map/ppermute | solution.py:24
  14.2 4.6 %collective-permute-start.2 = (bf16[4,256,128]{2,1,0:T(8,128)(2,1)S(1)}, bf16[4,256,128]{2,1,0:T(8,128)(2,1)S(1)}, u32[]{:S(2)}, u32[]{:S(2)}) collective-permute-start(bf16[4,256,128]{2,1,0:T(8,128)(2,1)S(1)} %collective-permute-done.1.refs_3_), channel_id=1, source_target_pairs={{0,4},{4,8},{8,12},{1,5},{5,9},{9,13},{2,6},{6,10},{10,14},{3,7},{... | collective-permute-start | bytes 786440 | tf_op jit(solution)/shard_map/ppermute | solution.py:24
  18.7 0.8 reshape.51
  19.5 0.6 fusion
  20.6 2.8 %collective-permute-done.4.refs_5_ = bf16[4,256,128]{2,1,0:T(8,128)(2,1)S(1)} collective-permute-done((bf16[4,256,128]{2,1,0:T(8,128)(2,1)S(1)}, bf16[4,256,128]{2,1,0:T(8,128)(2,1)S(1)}, u32[]{:S(2)}, u32[]{:S(2)}) %collective-permute-start.4) | collective-permute-done | bytes 262176 | tf_op jit(solution)/shard_map/ppermute | solution.py:24
  23.4 1.2 %collective-permute-done.2.refs_1_ = bf16[4,256,128]{2,1,0:T(8,128)(2,1)S(1)} collective-permute-done((bf16[4,256,128]{2,1,0:T(8,128)(2,1)S(1)}, bf16[4,256,128]{2,1,0:T(8,128)(2,1)S(1)}, u32[]{:S(2)}, u32[]{:S(2)}) %collective-permute-start.2) | collective-permute-done | bytes 262176 | tf_op jit(solution)/shard_map/ppermute | solution.py:24
  25.7 0.7 lt.39
  26.6 1.4 %copy.13 = f32[1,2,4,2]{3,2,1,0:T(4,128)} copy(f32[1,2,4,2]{2,3,1,0:T(2,128)} %param.13) | data formatting | bytes 128 | tf_op jit(solution)/shard_map/reshape | solution.py:263
  28.5 10.7 %prepare.1 = (f32[8,256,128]{2,1,0:T(8,128)}, f32[8,256,256]{2,1,0:T(8,128)}, bf16[8,256,256]{2,1,0:T(8,128)(2,1)}, bf16[8,256,128]{2,1,0:T(8,128)(2,1)}, bf16[8,2816,256]{2,1,0:T(8,128)(2,1)}) custom-call(f32[8,2]{1,0:T(8,128)} %bitcast.22, f32[8]{0:T(128)} %compare_convert_fusion.live_ref, s32[1]{0:T(128)} %bitcast.1.core_ref, f32[8,27]{1,0:T(8,128)} %bitcast.23, ...), custom_call_target="tpu_custom_call" | custom-call | tf_op jit(solution)/shard_map/prepare/pallas_call | solution.py:269
  39.3 0.7 copy-done.1
  40.0 16.5 %convolve.1 = (bf16[8,256,256]{2,1,0:T(8,128)(2,1)}, bf16[4,256,128]{2,1,0:T(8,128)(2,1)}, bf16[4,256,128]{2,1,0:T(8,128)(2,1)}, f32[4,256,128]{2,1,0:T(8,128)},...) custom-call(s32[8]{0:T(128)} %and_select_fusion.3.slots_ref, ...), custom_call_target="tpu_custom_call" | custom-call | tf_op jit(solution)/shard_map/convolve/pallas_call | solution.py:284
  56.5 4.4 %collective-permute-start.15 = (bf16[4,256,128]{2,1,0:T(8,128)(2,1)}, bf16[4,256,128]{2,1,0:T(8,128)(2,1)S(1)}, u32[]{:S(2)}, u32[]{:S(2)}) collective-permute-start(bf16[4,256,128]{2,1,0:T(8,128)(2,1)} %get-tuple-element.20), channel_id=1, source_target_pairs={{0,4},{4,8},{8,12},{1,5},{5,9},{9,13},{2,6},{6,10},{10,14},{3,7},{... | collective-permute-start | bytes 786440 | tf_op jit(solution)/shard_map/ppermute | solution.py:24
  60.9 1.3 %collective-permute-start.16 = (bf16[4,256,128]{2,1,0:T(8,128)(2,1)}, bf16[4,256,128]{2,1,0:T(8,128)(2,1)S(1)}, u32[]{:S(2)}, u32[]{:S(2)}) collective-permute-start(bf16[4,256,128]{2,1,0:T(8,128)(2,1)} %get-tuple-element.21), channel_id=1, source_target_pairs={{4,0},{8,4},{12,8},{5,1},{9,5},{13,9},{6,2},{10,6},{14,10},{7,3},{... | collective-permute-start | bytes 786440 | tf_op jit(solution)/shard_map/ppermute | solution.py:24
  62.2 4.6 %collective-permute-start.13 = (bf16[4,256,128]{2,1,0:T(8,128)(2,1)}, bf16[4,256,128]{2,1,0:T(8,128)(2,1)S(1)}, u32[]{:S(2)}, u32[]{:S(2)}) collective-permute-start(bf16[4,256,128]{2,1,0:T(8,128)(2,1)} %get-tuple-element.17), channel_id=1, source_target_pairs={{0,4},{4,8},{8,12},{1,5},{5,9},{9,13},{2,6},{6,10},{10,14},{3,7},{... | collective-permute-start | bytes 786440 | tf_op jit(solution)/shard_map/ppermute | solution.py:24
  66.7 1.3 %collective-permute-start.14 = (bf16[4,256,128]{2,1,0:T(8,128)(2,1)}, bf16[4,256,128]{2,1,0:T(8,128)(2,1)S(1)}, u32[]{:S(2)}, u32[]{:S(2)}) collective-permute-start(bf16[4,256,128]{2,1,0:T(8,128)(2,1)} %get-tuple-element.18), channel_id=1, source_target_pairs={{4,0},{8,4},{12,8},{5,1},{9,5},{13,9},{6,2},{10,6},{14,10},{7,3},{... | collective-permute-start | bytes 786440 | tf_op jit(solution)/shard_map/ppermute | solution.py:24
  68.0 3.3 %collective-permute-done.16 = bf16[4,256,128]{2,1,0:T(8,128)(2,1)S(1)} collective-permute-done((bf16[4,256,128]{2,1,0:T(8,128)(2,1)}, bf16[4,256,128]{2,1,0:T(8,128)(2,1)S(1)}, u32[]{:S(2)}, u32[]{:S(2)}) %collective-permute-start.16) | collective-permute-done | bytes 262176 | tf_op jit(solution)/shard_map/ppermute | solution.py:24
  71.4 1.1 %add_convert_fusion = bf16[4,256,128]{2,1,0:T(8,128)(2,1)S(1)} fusion(bf16[4,256,128]{2,1,0:T(8,128)(2,1)S(1)} %collective-permute-done.16, bf16[4,256,128]{2,1,0:T(8,128)(2,1)S(1)} %collective-permute-done.15, bf16[4,256,128]{2,1,0:T(8,128)(2,1)} %get-tuple-element.19), kind=kLoop, calls=%fused_computation.1 | loop fusion | flops 786432 | bytes 1048576 | tf_op jit(solution)/shard_map/convert_element_type | solution.py:314
  72.4 1.7 %collective-permute-start.17 = (bf16[4,256,128]{2,1,0:T(8,128)(2,1)S(1)}, bf16[4,256,128]{2,1,0:T(8,128)(2,1)S(1)}, u32[]{:S(2)}, u32[]{:S(2)}) collective-permute-start(bf16[4,256,128]{2,1,0:T(8,128)(2,1)S(1)} %add_convert_fusion), channel_id=1, source_target_pairs={{0,2},{2,0},{1,3},{3,1},{4,6},{6,4},{5,7},{7,5},{8,10},{10,8},{9,1... | collective-permute-start | bytes 786440 | tf_op jit(solution)/shard_map/ppermute | solution.py:34
  74.1 5.7 %score.1 = f32[8,256,128]{2,1,0:T(8,128)} custom-call(bf16[8,256,256]{2,1,0:T(8,128)(2,1)} %get-tuple-element.22.low_ref, bf16[8,256,256]{2,1,0:T(8,128)(2,1)} %get-tuple-element.23.prow_ref, bf16[8,256,128]{2,1,0:T(8,128)(2,1)} %get-tuple-element.24.pcol_ref, f32[8,256,128]{2,1,0:T(8,128)} %get-tuple-element.25.norm_ref), custom_call_target="tpu_custom_call" | custom-call | tf_op jit(solution)/shard_map/score/pallas_call | solution.py:317
  79.9 0.9 %add_bitcast_fusion = f32[1,4,256,128]{3,2,1,0:T(8,128)} fusion(bf16[4,256,128]{2,1,0:T(8,128)(2,1)S(1)} %collective-permute-done.17, bf16[4,256,128]{2,1,0:T(8,128)(2,1)S(1)} %collective-permute-done.14, f32[4,256,128]{2,1,0:T(8,128)S(1)} %copy-done.2, bf16[4,256,128]{2,1,0:T(8,128)(2,1)S(1)} %collective-permute-done.13), kind=kLoop, calls=%fused_computation | loop fusion | flops 786432 | bytes 1835008 | tf_op jit(solution)/shard_map/reshape | solution.py:324
  (46 shorter events, 3.1 us)
Async XLA Ops:
  0.6 24.0 %collective-permute-start.12 = (f32[8,256,128]{2,1,0:T(8,128)}, f32[8,256,128]{2,1,0:T(8,128)S(1)}, u32[]{:S(2)}, u32[]{:S(2)}) collective-permute-start(f32[8,256,128]{2,1,0:T(8,128)} %bitcast.12), channel_id=1, source_target_pairs={{0,1},{1,0},{2,3},{3,2},{4,5},{5,4},{6,7},{7,6},{8,9},{9,8},{10,11... | collective-permute-start | bytes 3145736 | tf_op jit(solution)/shard_map/ppermute | solution.py:34
  1.2 11.6 %collective-permute-start.3 = (bf16[4,256,128]{2,1,0:T(8,128)(2,1)}, bf16[4,256,128]{2,1,0:T(8,128)(2,1)S(1)}, u32[]{:S(2)}, u32[]{:S(2)}) collective-permute-start(bf16[4,256,128]{2,1,0:T(8,128)(2,1)} %bitcast.17), channel_id=1, source_target_pairs={{4,0},{8,4},{12,8},{5,1},{9,5},{13,9},{6,2},{10,6},{14,10},{7,3},{... | collective-permute-start | bytes 786440 | tf_op jit(solution)/shard_map/ppermute | solution.py:24
  2.5 10.4 %collective-permute-start.1 = (bf16[4,256,128]{2,1,0:T(8,128)(2,1)}, bf16[4,256,128]{2,1,0:T(8,128)(2,1)S(1)}, u32[]{:S(2)}, u32[]{:S(2)}) collective-permute-start(bf16[4,256,128]{2,1,0:T(8,128)(2,1)} %bitcast.18), channel_id=1, source_target_pairs={{2,0},{0,2},{3,1},{1,3},{6,4},{4,6},{7,5},{5,7},{10,8},{8,10},{11,... | collective-permute-start | bytes 786440 | tf_op jit(solution)/shard_map/ppermute | solution.py:29
  5.0 9.1 %collective-permute-start.7 = (bf16[4,256,128]{2,1,0:T(8,128)(2,1)}, bf16[4,256,128]{2,1,0:T(8,128)(2,1)S(1)}, u32[]{:S(2)}, u32[]{:S(2)}) collective-permute-start(bf16[4,256,128]{2,1,0:T(8,128)(2,1)} %bitcast.19), channel_id=1, source_target_pairs={{0,1},{1,0},{2,3},{3,2},{4,5},{5,4},{6,7},{7,6},{8,9},{9,8},{10,11... | collective-permute-start | bytes 786440 | tf_op jit(solution)/shard_map/ppermute | solution.py:34
  5.2 14.3 %collective-permute-start = (bf16[4,256,128]{2,1,0:T(8,128)(2,1)}, bf16[4,256,128]{2,1,0:T(8,128)(2,1)S(1)}, u32[]{:S(2)}, u32[]{:S(2)}) collective-permute-start(bf16[4,256,128]{2,1,0:T(8,128)(2,1)} %bitcast.20), channel_id=1, source_target_pairs={{0,4},{4,8},{8,12},{1,5},{5,9},{9,13},{2,6},{6,10},{10,14},{3,7},{... | collective-permute-start | bytes 786440 | tf_op jit(solution)/shard_map/ppermute | solution.py:24
  12.8 26.4 %copy-start.3 = (bf16[4,256,128]{2,1,0:T(8,128)(2,1)}, bf16[4,256,128]{2,1,0:T(8,128)(2,1)S(1)}, u32[]{:S(2)}) copy-start(bf16[4,256,128]{2,1,0:T(8,128)(2,1)S(1)} %collective-permute-done.3.refs_4_) | copy-start | bytes 786436
  12.8 7.3 %collective-permute-start.9 = (bf16[4,256,128]{2,1,0:T(8,128)(2,1)S(1)}, bf16[4,256,128]{2,1,0:T(8,128)(2,1)S(1)}, u32[]{:S(2)}, u32[]{:S(2)}) collective-permute-start(bf16[4,256,128]{2,1,0:T(8,128)(2,1)S(1)} %collective-permute-done.3.refs_4_), channel_id=1, source_target_pairs={{0,1},{1,0},{2,3},{3,2},{4,5},{5,4},{6,7},{7,6},{8,9},{9,8},{10,11... | collective-permute-start | bytes 786440 | tf_op jit(solution)/shard_map/ppermute | solution.py:34
  12.8 26.4 %copy-start.4 = (bf16[4,256,128]{2,1,0:T(8,128)(2,1)}, bf16[4,256,128]{2,1,0:T(8,128)(2,1)S(1)}, u32[]{:S(2)}) copy-start(bf16[4,256,128]{2,1,0:T(8,128)(2,1)S(1)} %collective-permute-done.1.refs_3_) | copy-start | bytes 786436
  12.8 10.6 %collective-permute-start.4 = (bf16[4,256,128]{2,1,0:T(8,128)(2,1)S(1)}, bf16[4,256,128]{2,1,0:T(8,128)(2,1)S(1)}, u32[]{:S(2)}, u32[]{:S(2)}) collective-permute-start(bf16[4,256,128]{2,1,0:T(8,128)(2,1)S(1)} %collective-permute-done.1.refs_3_), channel_id=1, source_target_pairs={{4,0},{8,4},{12,8},{5,1},{9,5},{13,9},{6,2},{10,6},{14,10},{7,3},{... | collective-permute-start | bytes 786440 | tf_op jit(solution)/shard_map/ppermute | solution.py:24
  14.2 25.1 %copy-start.5 = (bf16[4,256,128]{2,1,0:T(8,128)(2,1)}, bf16[4,256,128]{2,1,0:T(8,128)(2,1)S(1)}, u32[]{:S(2)}) copy-start(bf16[4,256,128]{2,1,0:T(8,128)(2,1)S(1)} %collective-permute-done.7.refs_8_) | copy-start | bytes 786436
  14.2 10.5 %collective-permute-start.2 = (bf16[4,256,128]{2,1,0:T(8,128)(2,1)S(1)}, bf16[4,256,128]{2,1,0:T(8,128)(2,1)S(1)}, u32[]{:S(2)}, u32[]{:S(2)}) collective-permute-start(bf16[4,256,128]{2,1,0:T(8,128)(2,1)S(1)} %collective-permute-done.1.refs_3_), channel_id=1, source_target_pairs={{0,4},{4,8},{8,12},{1,5},{5,9},{9,13},{2,6},{6,10},{10,14},{3,7},{... | collective-permute-start | bytes 786440 | tf_op jit(solution)/shard_map/ppermute | solution.py:24
  19.5 19.7 %copy-start.6 = (bf16[4,256,128]{2,1,0:T(8,128)(2,1)}, bf16[4,256,128]{2,1,0:T(8,128)(2,1)S(1)}, u32[]{:S(2)}) copy-start(bf16[4,256,128]{2,1,0:T(8,128)(2,1)S(1)} %collective-permute-done.refs_0_) | copy-start | bytes 786436
  19.5 19.6 %collective-permute-start.11 = (bf16[8,256,128]{2,1,0:T(8,128)(2,1)}, bf16[8,256,128]{2,1,0:T(8,128)(2,1)S(1)}, u32[]{:S(2)}, u32[]{:S(2)}) collective-permute-start(bf16[8,256,128]{2,1,0:T(8,128)(2,1)} %bitcast.15), channel_id=1, source_target_pairs={{0,1},{1,0},{2,3},{3,2},{4,5},{5,4},{6,7},{7,6},{8,9},{9,8},{10,11... | collective-permute-start | bytes 1572872 | tf_op jit(solution)/shard_map/ppermute | solution.py:34
  20.2 19.1 %copy-start.7 = (bf16[4,256,128]{2,1,0:T(8,128)(2,1)}, bf16[4,256,128]{2,1,0:T(8,128)(2,1)S(1)}, u32[]{:S(2)}) copy-start(bf16[4,256,128]{2,1,0:T(8,128)(2,1)S(1)} %collective-permute-done.9.refs_10_) | copy-start | bytes 786436
  20.2 19.0 %collective-permute-start.8 = (bf16[4,256,128]{2,1,0:T(8,128)(2,1)S(1)}, bf16[4,256,128]{2,1,0:T(8,128)(2,1)}, u32[]{:S(2)}, u32[]{:S(2)}) collective-permute-start(bf16[4,256,128]{2,1,0:T(8,128)(2,1)S(1)} %collective-permute-done.1.refs_3_), channel_id=1, source_target_pairs={{0,1},{1,0},{2,3},{3,2},{4,5},{5,4},{6,7},{7,6},{8,9},{9,8},{10,11... | collective-permute-start | bytes 786440 | tf_op jit(solution)/shard_map/ppermute | solution.py:34
  23.4 15.8 %copy-start.8 = (bf16[4,256,128]{2,1,0:T(8,128)(2,1)}, bf16[4,256,128]{2,1,0:T(8,128)(2,1)S(1)}, u32[]{:S(2)}) copy-start(bf16[4,256,128]{2,1,0:T(8,128)(2,1)S(1)} %collective-permute-done.4.refs_5_) | copy-start | bytes 786436
  23.4 15.7 %collective-permute-start.5 = (bf16[4,256,128]{2,1,0:T(8,128)(2,1)S(1)}, bf16[4,256,128]{2,1,0:T(8,128)(2,1)}, u32[]{:S(2)}, u32[]{:S(2)}) collective-permute-start(bf16[4,256,128]{2,1,0:T(8,128)(2,1)S(1)} %collective-permute-done.refs_0_), channel_id=1, source_target_pairs={{0,1},{1,0},{2,3},{3,2},{4,5},{5,4},{6,7},{7,6},{8,9},{9,8},{10,11... | collective-permute-start | bytes 786440 | tf_op jit(solution)/shard_map/ppermute | solution.py:34
  24.6 14.5 %collective-permute-start.10 = (bf16[4,256,128]{2,1,0:T(8,128)(2,1)S(1)}, bf16[4,256,128]{2,1,0:T(8,128)(2,1)}, u32[]{:S(2)}, u32[]{:S(2)}) collective-permute-start(bf16[4,256,128]{2,1,0:T(8,128)(2,1)S(1)} %collective-permute-done.4.refs_5_), channel_id=1, source_target_pairs={{0,1},{1,0},{2,3},{3,2},{4,5},{5,4},{6,7},{7,6},{8,9},{9,8},{10,11... | collective-permute-start | bytes 786440 | tf_op jit(solution)/shard_map/ppermute | solution.py:34
  24.7 14.5 %collective-permute-start.6 = (bf16[4,256,128]{2,1,0:T(8,128)(2,1)S(1)}, bf16[4,256,128]{2,1,0:T(8,128)(2,1)}, u32[]{:S(2)}, u32[]{:S(2)}) collective-permute-start(bf16[4,256,128]{2,1,0:T(8,128)(2,1)S(1)} %collective-permute-done.2.refs_1_), channel_id=1, source_target_pairs={{0,1},{1,0},{2,3},{3,2},{4,5},{5,4},{6,7},{7,6},{8,9},{9,8},{10,11... | collective-permute-start | bytes 786440 | tf_op jit(solution)/shard_map/ppermute | solution.py:34
  56.5 11.6 %collective-permute-start.15 = (bf16[4,256,128]{2,1,0:T(8,128)(2,1)}, bf16[4,256,128]{2,1,0:T(8,128)(2,1)S(1)}, u32[]{:S(2)}, u32[]{:S(2)}) collective-permute-start(bf16[4,256,128]{2,1,0:T(8,128)(2,1)} %get-tuple-element.20), channel_id=1, source_target_pairs={{0,4},{4,8},{8,12},{1,5},{5,9},{9,13},{2,6},{6,10},{10,14},{3,7},{... | collective-permute-start | bytes 786440 | tf_op jit(solution)/shard_map/ppermute | solution.py:24
  60.9 10.5 %collective-permute-start.16 = (bf16[4,256,128]{2,1,0:T(8,128)(2,1)}, bf16[4,256,128]{2,1,0:T(8,128)(2,1)S(1)}, u32[]{:S(2)}, u32[]{:S(2)}) collective-permute-start(bf16[4,256,128]{2,1,0:T(8,128)(2,1)} %get-tuple-element.21), channel_id=1, source_target_pairs={{4,0},{8,4},{12,8},{5,1},{9,5},{13,9},{6,2},{10,6},{14,10},{7,3},{... | collective-permute-start | bytes 786440 | tf_op jit(solution)/shard_map/ppermute | solution.py:24
  62.2 17.7 %collective-permute-start.13 = (bf16[4,256,128]{2,1,0:T(8,128)(2,1)}, bf16[4,256,128]{2,1,0:T(8,128)(2,1)S(1)}, u32[]{:S(2)}, u32[]{:S(2)}) collective-permute-start(bf16[4,256,128]{2,1,0:T(8,128)(2,1)} %get-tuple-element.17), channel_id=1, source_target_pairs={{0,4},{4,8},{8,12},{1,5},{5,9},{9,13},{2,6},{6,10},{10,14},{3,7},{... | collective-permute-start | bytes 786440 | tf_op jit(solution)/shard_map/ppermute | solution.py:24
  66.7 13.2 %collective-permute-start.14 = (bf16[4,256,128]{2,1,0:T(8,128)(2,1)}, bf16[4,256,128]{2,1,0:T(8,128)(2,1)S(1)}, u32[]{:S(2)}, u32[]{:S(2)}) collective-permute-start(bf16[4,256,128]{2,1,0:T(8,128)(2,1)} %get-tuple-element.18), channel_id=1, source_target_pairs={{4,0},{8,4},{12,8},{5,1},{9,5},{13,9},{6,2},{10,6},{14,10},{7,3},{... | collective-permute-start | bytes 786440 | tf_op jit(solution)/shard_map/ppermute | solution.py:24
  72.4 7.5 %collective-permute-start.17 = (bf16[4,256,128]{2,1,0:T(8,128)(2,1)S(1)}, bf16[4,256,128]{2,1,0:T(8,128)(2,1)S(1)}, u32[]{:S(2)}, u32[]{:S(2)}) collective-permute-start(bf16[4,256,128]{2,1,0:T(8,128)(2,1)S(1)} %add_convert_fusion), channel_id=1, source_target_pairs={{0,2},{2,0},{1,3},{3,1},{4,6},{6,4},{5,7},{7,5},{8,10},{10,8},{9,1... | collective-permute-start | bytes 786440 | tf_op jit(solution)/shard_map/ppermute | solution.py:34
  (4 other events, 25.0 us)

commit v2 on v1

v2 whole, which is shorter than its diff:
```python
import functools

import jax
import jax.numpy as jnp
import numpy as np
from jax import lax
from jax.experimental import pallas as pl
from jax.experimental.pallas import tpu as pltpu
from jax.sharding import PartitionSpec as P

HW = 10
PW = 7

sigmas = (0.75, 1.5, 3.0)
degrees = (4, 2, 2)

VMEM = pltpu.VMEM
SMEM = pltpu.SMEM


def neighbours(groups, rows):
    if groups % 2 or rows < 2:
        line = [(g * rows + i, g * rows + i + 1) for g in range(groups) for i in range(rows - 1)]
        return line, [(j, i) for i, j in line], False
    ring = []
    for g in range(0, groups, 2):
        loop = [g * rows + i for i in range(rows)] + [(g + 1) * rows + i for i in reversed(range(rows))]
        ring += list(zip(loop, loop[1:] + loop[:1]))
    return ring, [(j, i) for i, j in ring], True


def fetched(block, axis, distance):
    devices = lax.axis_size(axis)
    return lax.ppermute(block, axis, [((i + distance) % devices, i) for i in range(devices)])


def sent(block, axis, distance):
    devices = lax.axis_size(axis)
    return lax.ppermute(block, axis, [(i, (i + distance) % devices) for i in range(devices)])


def basis_terms():
    terms = []
    offset = 0
    for group in range(3):
        for first in range(degrees[group] + 1):
            for second in range(degrees[group] + 1 - first):
                terms.append((group, first, second, offset + first))
        offset = offset + degrees[group] + 1
    return terms


def profile(offset, sigma, power, reach):
    grid = np.arange(-reach, reach + 1).astype(np.float32)
    base = np.exp(-grid * grid / np.float32(2.0 * sigma * sigma)) * (grid / reach) ** power
    scale = np.sqrt(np.sum(base * base))
    spot = offset.astype(np.float32)
    value = np.exp(-spot * spot / np.float32(2.0 * sigma * sigma)) * (spot / reach) ** power / scale
    return np.where(np.abs(offset) <= reach, value, 0.0).astype(np.float32)


def ring_profiles(width, reach):
    lane = np.arange(width)
    offset = np.where(lane < width // 2, lane, lane - width)
    return np.stack([profile(offset, sigmas[t[0]], t[2], reach) for t in basis_terms()])


def row_profiles(reach, rows, lanes):
    offset = np.arange(rows) - reach
    tables = []
    for group in range(3):
        for first in range(degrees[group] + 1):
            tables.append(profile(offset, sigmas[group], first, reach))
    table = np.stack(tables).astype(jnp.bfloat16).astype(np.float32)
    return np.broadcast_to(table[:, :, None], table.shape + (lanes,))


def taps_kernel(core_ref, coeff_ref, ring_ref, spread_ref, band_ref, taps_ref, edge_ref):
    tiles = coeff_ref.shape[0]
    cols = ring_ref.shape[1]
    group = cols // tiles
    reach = HW
    terms = basis_terms()
    profiles = spread_ref.shape[0]
    across = lax.broadcasted_iota(jnp.int32, (cols, cols), 1)
    down = lax.broadcasted_iota(jnp.int32, (cols, cols), 0)
    near = jnp.abs(across - down) <= reach
    same = (across // group) == (down // group)
    count = 2 * reach + 1
    turn = jnp.where(core_ref[0] == 0, group, cols - group)

    def one(t, carry):
        taps = jnp.zeros(taps_ref.shape[1:], jnp.float32)
        for p in range(profiles):
            vec = jnp.zeros((1, cols), jnp.float32)
            for k, term in enumerate(terms):
                if term[3] == p:
                    vec = vec + coeff_ref[t, k] * ring_ref[k : k + 1, :]
            vec = vec.astype(jnp.bfloat16).astype(jnp.float32)
            taps = taps + spread_ref[p] * vec
        taps_ref[t] = taps
        edge_ref[t] = pltpu.roll(taps, turn, 1)
        band_ref[t, 0:cols, :] = jnp.zeros((cols, cols), jnp.bfloat16)
        band_ref[t, (count + 1) * cols :, :] = jnp.zeros((cols, cols), jnp.bfloat16)
        for u in range(count):
            full = jnp.broadcast_to(taps_ref[t, u : u + 1, :], (cols, cols))
            full = pltpu.roll(full, 0, 1, stride=1, stride_axis=0)
            full = jnp.where(near, full, 0.0).astype(jnp.bfloat16)
            band_ref[t, (count - u) * cols : (count - u + 1) * cols, :] = full
        return carry

    lax.fori_loop(0, tiles, one, 0)
    band_ref[tiles, 0:cols, :] = jnp.zeros((cols, cols), jnp.bfloat16)
    band_ref[tiles, (count + 1) * cols :, :] = jnp.zeros((cols, cols), jnp.bfloat16)
    for u in range(count):
        full = jnp.concatenate(
            [jnp.broadcast_to(edge_ref[t, u : u + 1, :], (group, cols)) for t in range(tiles)], axis=0
        )
        full = pltpu.roll(full, 0, 1, stride=1, stride_axis=0)
        full = jnp.where(same, full, 0.0).astype(jnp.bfloat16)
        band_ref[tiles, (count - u) * cols : (count - u + 1) * cols, :] = full


def norms_kernel(width_ref, live_ref, core_ref, own_ref, other_ref,
                 norm_ref, inv_ref, prow_ref, pcol_ref, dist_ref, near_ref):
    tiles, size, cols = own_ref.shape
    wide = 2 * cols
    rows = lax.broadcasted_iota(jnp.int32, (size, size), 0)
    across = lax.broadcasted_iota(jnp.int32, (size, size), 1)
    gap = rows - across
    dist_ref[...] = (gap * gap).astype(jnp.float32)
    inner = lax.broadcasted_iota(jnp.int32, (wide, cols), 0)
    outer = lax.broadcasted_iota(jnp.int32, (wide, cols), 1)
    ring = jnp.abs(inner - outer)
    ring = jnp.minimum(ring, wide - ring)
    near_ref[...] = (ring * ring).astype(jnp.float32)
    lane = lax.broadcasted_iota(jnp.int32, (size, cols), 1)
    keep = (lane >= cols // 2) == (core_ref[0] == 1)
    limit = float(PW * PW)
    spot = lax.broadcasted_iota(jnp.int32, (8, 128), 1)
    spot_low = spot.astype(jnp.float32) - PW

    def table(width, square):
        rate = -0.5 / (width * width)
        base = jnp.where(spot <= 2 * PW, jnp.exp(spot_low * spot_low * rate), 0.0)
        scale = 1.0 / jnp.sum(base[0:1], axis=1, keepdims=True)
        return jnp.where(square <= limit, jnp.exp(square * rate[0:1, 0:1]) * scale, 0.0)

    def one(t, carry):
        inv_own = 1.0 / own_ref[t]
        inv_other = jnp.where(keep, 1.0 / other_ref[t], 0.0)
        inv_ref[t] = inv_own
        inv_low = jnp.concatenate([inv_own, inv_other], axis=1).astype(jnp.bfloat16)
        prow = table(jnp.full((8, 128), width_ref[t, 0], jnp.float32), dist_ref[...])
        prow_ref[t] = prow.astype(jnp.bfloat16)
        qrow = (prow * prow).astype(jnp.bfloat16)
        pcol = table(jnp.full((8, 128), width_ref[t, 1], jnp.float32), near_ref[...])
        pcol_ref[t] = pcol.astype(jnp.bfloat16)
        qcol = (pcol * pcol).astype(jnp.bfloat16)
        denom = jnp.dot(qrow, inv_low, preferred_element_type=jnp.float32).astype(jnp.bfloat16)
        denom = jnp.dot(denom, qcol, preferred_element_type=jnp.float32)
        norm_ref[t] = live_ref[t] / jnp.sqrt(denom)
        return carry

    lax.fori_loop(0, tiles, one, 0)


PAD = 16


def convolve_kernel(blocks, slots_ref, part_ref, live_ref, present_ref, core_ref, *refs):
    own_blocks = refs[:blocks]
    other_blocks = refs[blocks : 2 * blocks]
    (band_ref, exp_ref, inv_ref) = refs[2 * blocks : 2 * blocks + 3]
    low_ref = refs[2 * blocks + 3]
    out_refs = refs[2 * blocks + 4 : 3 * blocks + 4]
    tile_ref, padded_ref, lhs_ref, edge_ref, conv_ref, acc_ref, sem = refs[3 * blocks + 4 :]
    _, tiles, size, cols = tile_ref.shape
    owned = own_blocks[0].shape[0]
    group = cols // tiles
    count = 2 * HW + 2
    first = PAD - HW
    pairs = size // 2

    def copies(t, b):
        slot = slots_ref[t]
        return (
            pltpu.make_async_copy(own_blocks[b].at[slot], tile_ref.at[0, t], sem.at[t, 0]),
            pltpu.make_async_copy(other_blocks[b].at[slot], tile_ref.at[1, t], sem.at[t, 1]),
        )

    for t in range(tiles):
        for b in range(blocks):
            @pl.when(part_ref[t] == b)
            def _(t=t, b=b):
                for c in copies(t, b):
                    c.start()

    acc_ref[...] = jnp.zeros_like(acc_ref)
    padded_ref[0:PAD, :] = jnp.zeros((PAD, cols), jnp.float32)
    padded_ref[PAD + size :, :] = jnp.zeros((PAD, cols), jnp.float32)

    def spread(which):
        for r in range(count):
            lhs_ref[:, r * cols : (r + 1) * cols] = padded_ref[
                pl.ds(first + r, pairs, stride=2), :
            ].astype(jnp.bfloat16)
        weights = jnp.concatenate(
            [band_ref[which, cols:, :], band_ref[which, : count * cols, :]], axis=1
        )
        return jnp.dot(lhs_ref[...], weights, preferred_element_type=jnp.float32)

    lane = lax.broadcasted_iota(jnp.int32, (1, cols), 1)
    start = jnp.where(core_ref[0] == 0, 0, cols - group)
    target = cols - group - start
    strip = jnp.zeros((size, cols), jnp.float32)
    for t in range(tiles):
        copies(t, 0)[1].wait()
        moved = pltpu.roll(tile_ref[1, t].astype(jnp.float32), lax.rem(t * group - start + cols, cols), 1)
        strip = jnp.where(lane // group == t, moved, strip)
    padded_ref[PAD : PAD + size, :] = strip
    edge_ref[...] = spread(tiles)

    def one(t, carry):
        copies(t, 0)[0].wait()
        padded_ref[PAD : PAD + size, :] = tile_ref[0, t].astype(jnp.float32)
        both = spread(t)
        turn = lax.rem(target - t * group + cols, cols)
        for s in range(2):
            edge = pltpu.roll(edge_ref[:, s * cols : (s + 1) * cols], turn, 1)
            edge = jnp.where((lane >= target) & (lane < target + group), edge, 0.0)
            conv_ref[pl.ds(s, pairs, stride=2), :] = both[:, s * cols : (s + 1) * cols] + edge
        convolved = conv_ref[...] * present_ref[t]
        own = (exp_ref[t].astype(jnp.float32) - convolved) * inv_ref[t]
        low_ref[t] = own.astype(jnp.bfloat16)
        where = part_ref[t] * owned + slots_ref[t]
        acc_ref[where] += live_ref[t] * own
        return carry

    lax.fori_loop(0, tiles, one, 0)
    for b in range(blocks):
        out_refs[b][...] = acc_ref[b * owned : (b + 1) * owned].astype(out_refs[b].dtype)


def score_kernel(core_ref, low_ref, other_ref, prow_ref, pcol_ref, norm_ref, score_ref):
    tiles, size, cols = low_ref.shape
    lane = lax.broadcasted_iota(jnp.int32, (size, cols), 1)
    keep = (lane >= cols // 2) == (core_ref[0] == 1)

    def one(t, carry):
        other = jnp.where(keep, other_ref[t].astype(jnp.float32), 0.0).astype(jnp.bfloat16)
        full = jnp.concatenate([low_ref[t], other], axis=1)
        numer = jnp.dot(prow_ref[t], full, preferred_element_type=jnp.float32)
        numer = numer.astype(jnp.bfloat16)
        numer = jnp.dot(numer, pcol_ref[t], preferred_element_type=jnp.float32)
        score_ref[t] = numer * norm_ref[t]
        return carry

    lax.fori_loop(0, tiles, one, 0)


def shape(dims, dtype):
    return jax.ShapeDtypeStruct(dims, dtype)


def vmem(count):
    return [pl.BlockSpec(memory_space=VMEM)] * count


def smem(count):
    return [pl.BlockSpec(memory_space=SMEM)] * count


def anywhere(count):
    return [pl.BlockSpec(memory_space=pl.ANY)] * count


def params(mib):
    return pltpu.CompilerParams(vmem_limit_bytes=mib << 20)


def cost(micros):
    return pl.CostEstimate(flops=int(micros * 1e9), bytes_accessed=int(micros * 3e6), transcendentals=0)


def on_device(templates, exposures, variance, coefficients, psf_width, patch_ids, live_count):
    size = templates.shape[2]
    cols = templates.shape[3]
    owned = templates.shape[1]
    slots = patch_ids.shape[2]
    across = lax.axis_size("patch")
    patches_row = owned * across
    blocks = 3 * across
    me = lax.axis_index("patch")
    row_index = lax.axis_index("exp")
    rows = lax.axis_size("exp")
    core = lax.axis_index("band").astype(jnp.int32).reshape(1)
    low = jnp.bfloat16
    f32 = jnp.float32

    own = templates.reshape(owned, size, cols)
    exp_flat = exposures.reshape(-1, size, cols)
    var_flat = variance.reshape(-1, size, cols)
    tiles = exp_flat.shape[0]
    assert cols % tiles == 0 and cols // tiles >= HW and size % 32 == 0
    swap = functools.partial(sent, axis="band", distance=1)

    forth, back, closed = neighbours(lax.axis_size("groups"), rows)
    flip = lax.axis_index("groups") % 2 if closed else 0
    ahead = lambda block: lax.ppermute(block, ("groups", "exp"), forth)
    behind = lambda block: lax.ppermute(block, ("groups", "exp"), back)
    from_first = jnp.where(flip == 0, row_index > 0, row_index < rows - 1)
    from_last = jnp.where(flip == 0, row_index < rows - 1, row_index > 0)

    row = [own] + [fetched(own, "patch", d) for d in range(1, across)]
    firsts = [ahead(b) for b in row]
    lasts = [behind(b) for b in row]
    window = firsts + row + lasts
    window_other = [swap(b) for b in window]
    var_other = swap(var_flat)

    ids = patch_ids.reshape(-1)
    column = ids % patches_row
    shift = (column // owned - me + across) % across
    step = ids // patches_row
    present = ((row_index + step >= 1) & (row_index + step <= rows)).astype(f32)
    step = jnp.where(flip == 0, step, 2 - step)
    part = step * across + shift
    slot = column % owned
    live = (
        (jnp.arange(slots, dtype=jnp.int32)[None, None, :] < live_count[:, :, None])
        .astype(f32)
        .reshape(-1)
    )
    coeff = coefficients.reshape(tiles, -1)
    width = psf_width.reshape(tiles, 2)
    ring = jnp.asarray(ring_profiles(cols, HW))
    count = 2 * HW + 1
    held = -(-count // 8) * 8
    spread = jnp.asarray(row_profiles(HW, held, cols))

    band = pl.pallas_call(
        taps_kernel,
        name="taps",
        out_shape=shape((tiles + 1, (count + 2) * cols, cols), low),
        in_specs=smem(2) + vmem(2),
        out_specs=vmem(1)[0],
        scratch_shapes=[VMEM((tiles, held, cols), f32), VMEM((tiles, held, cols), f32)],
        compiler_params=params(12),
        cost_estimate=cost(3),
    )(core, coeff, ring, spread)

    norm, inv, prow, pcol = pl.pallas_call(
        norms_kernel,
        name="norms",
        out_shape=(
            shape((tiles, size, cols), f32),
            shape((tiles, size, cols), f32),
            shape((tiles, size, size), low),
            shape((tiles, 2 * cols, cols), low),
        ),
        in_specs=smem(3) + vmem(2),
        out_specs=tuple(vmem(4)),
        scratch_shapes=[VMEM((size, size), f32), VMEM((2 * cols, cols), f32)],
        compiler_params=params(12),
        cost_estimate=cost(5),
    )(width, live, core, var_flat, var_other)

    outs = pl.pallas_call(
        functools.partial(convolve_kernel, blocks),
        name="convolve",
        out_shape=tuple(
            [shape((tiles, size, cols), low)]
            + [shape((owned, size, cols), f32 if b == across else low) for b in range(blocks)]
        ),
        in_specs=smem(5) + anywhere(2 * blocks) + vmem(3),
        out_specs=tuple(vmem(1 + blocks)),
        scratch_shapes=[
            VMEM((2, tiles, size, cols), low),
            VMEM((size + 2 * PAD, cols), f32),
            VMEM((size // 2, (count + 1) * cols), low),
            VMEM((size // 2, 2 * cols), f32),
            VMEM((size, cols), f32),
            VMEM((blocks * owned, size, cols), f32),
            pltpu.SemaphoreType.DMA((tiles, 2)),
        ],
        compiler_params=params(24),
        cost_estimate=cost(5),
    )(slot, part, live, present, core, *window, *window_other, band, exp_flat, inv)
    weighted_low = outs[0]
    parts = outs[1:]

    from_ahead = [ahead(parts[2 * across + d]) for d in reversed(range(across))][::-1]
    from_behind = [behind(parts[d]) for d in reversed(range(across))][::-1]
    weighted_other = swap(weighted_low)

    def received(d):
        one = jnp.where(from_first, from_ahead[d].astype(f32), 0.0)
        return one + jnp.where(from_last, from_behind[d].astype(f32), 0.0)

    total = parts[across]
    for d in range(1, across):
        merged = (parts[across + d].astype(f32) + received(d)).astype(low)
        total = total + sent(merged, "patch", d).astype(f32)
    total = total + received(0)

    score = pl.pallas_call(
        score_kernel,
        name="score",
        out_shape=shape((tiles, size, cols), f32),
        in_specs=smem(1) + vmem(5),
        out_specs=vmem(1)[0],
        compiler_params=params(12),
        cost_estimate=cost(5),
    )(core, weighted_low, weighted_other, prow, pcol, norm)
    return (total.reshape(1, owned, size, cols), score.reshape(exposures.shape))


def solution(mesh):
    assert mesh.shape["band"] == 2
    in_specs = (
        P(("groups", "exp"), "patch", None, "band"),
        P(("groups", "exp"), "patch", None, None, "band"),
        P(("groups", "exp"), "patch", None, None, "band"),
        P(("groups", "exp"), "patch", None, None),
        P(("groups", "exp"), "patch", None, None),
        P(("groups", "exp"), "patch", None),
        P(("groups", "exp"), "patch"),
    )
    out_specs = (
        P(("groups", "exp"), "patch", None, "band"),
        P(("groups", "exp"), "patch", None, None, "band"),
    )
    return jax.shard_map(
        on_device, mesh=mesh, in_specs=in_specs, out_specs=out_specs, check_vma=False
    )
```

time: 81.3 us -> 58.2 us (0.72)
  starting transfers between devices: 29.1 us -> 14.6 us
  Pallas kernels: 32.9 us -> 18.8 us
  local copies, waits for them, and re-layouts: 3.74 us -> 12.7 us
  other arithmetic: 3.64 us -> 1.13 us
  waiting for transfers between devices: 10.6 us -> 9.63 us
    ppermute x8, starting transfers between devices: 23 us -> 9.52 us  [the longest x4 7.74 us: on_device(): behind = lambda block: lax.ppermute(block, ('groups', 'exp'), back)]
    unnamed x20 -> x30, local copies, waits for them, and re-layouts: 0.73 us -> 9.54 us
    pallas_call x1, Pallas kernels: 16.5 us -> 7.78 us  [on_device(): pl.pallas_call(functools.partial(convolve_kernel, blocks), name='convolve...]
    ppermute x8, waiting for transfers between devices: 10.6 us -> 5.87 us  [the longest x4 5.45 us: on_device(): ahead = lambda block: lax.ppermute(block, ('groups', 'exp'), forth)]
    ppermute x1, waiting for transfers between devices: 0.01 us -> 3.74 us  [fetched(): lax.ppermute(block, axis, [((i + distance) % devices, i) for i in range(d...]
    pallas_call x1 -> x2, Pallas kernels: 10.7 us -> 7.31 us  [the longest x1 4.1 us: on_device(): pl.pallas_call(norms_kernel, name='norms', out_shape=(shape((tiles, size,...]
    pallas_call x1, Pallas kernels: 5.74 us -> 3.67 us  [on_device(): pl.pallas_call(score_kernel, name='score', out_shape=shape((tiles, size,...]
    convert_element_type x2, other arithmetic: 1.54 us -> 0.16 us  [the longest x1 0.14 us: on_device(): merged = (parts[across + d].astype(f32) + received(d)).astype(low)]
  transfers between devices with their start and end apart: 18 -> 18, of which waited for: 4 -> 4; matrix products, arithmetic and copies ran while one was open for 7% -> 6% of each run, Pallas kernels for 20% -> 19%
where the time goes in v2:
time: 58.2 us; the launch traced here: 57.7 us
  Pallas kernels  18.8 us (32%)
  starting transfers between devices  14.6 us (25%)
  local copies, waits for them, and re-layouts  12.7 us (22%)
  waiting for transfers between devices  9.63 us (17%)
  other arithmetic  1.13 us (2%)
  between operations  0.81 us (1%)
    unnamed x30, local copies, waits for them, and re-layouts  9.54 us
    pallas_call x1, Pallas kernels, on_device(): pl.pallas_call(functools.partial(convolve_kernel, blocks), name='convolve...  7.78 us
    ppermute x4, starting transfers between devices, on_device(): behind = lambda block: lax.ppermute(block, ('groups', 'exp'), back)  7.74 us
    ppermute x4, waiting for transfers between devices, on_device(): ahead = lambda block: lax.ppermute(block, ('groups', 'exp'), forth)  5.45 us
    pallas_call x1, Pallas kernels, on_device(): pl.pallas_call(norms_kernel, name='norms', out_shape=(shape((tiles, size,...  4.1 us
    ppermute x1, waiting for transfers between devices, fetched(): lax.ppermute(block, axis, [((i + distance) % devices, i) for i in range(d...  3.74 us
    pallas_call x1, Pallas kernels, on_device(): pl.pallas_call(score_kernel, name='score', out_shape=shape((tiles, size,...  3.67 us
    ppermute x9, starting transfers between devices, sent(): lax.ppermute(block, axis, [(i, (i + distance) % devices) for i in range(d...  3.61 us
  transfers between devices with their start and end apart: 18, of which 4 were waited for; matrix products, arithmetic and copies ran while one was open for 6% of the time, Pallas kernels for 19%

profile of v2, /device:TPU:0, one launch (start us, length us, event | category | flops | bytes accessed | tf_op | source)
XLA Modules:
  0.0 57.7 jit_solution(16678057265953789049)
XLA Ops:
  1.3 2.9 %collective-permute-start.3 = (bf16[4,256,128]{2,1,0:T(8,128)(2,1)}, bf16[4,256,128]{2,1,0:T(8,128)(2,1)S(1)}, u32[]{:S(2)}, u32[]{:S(2)}) collective-permute-start(bf16[4,256,128]{2,1,0:T(8,128)(2,1)} %bitcast.17), channel_id=1, source_target_pairs={{4,0},{8,4},{12,8},{28,12},{24,28},{20,24},{16,20},{0,16},{5,1},{9... | collective-permute-start | bytes 786440 | tf_op jit(solution)/shard_map/ppermute | solution.py:311
  4.2 1.5 %collective-permute-start.1 = (bf16[4,256,128]{2,1,0:T(8,128)(2,1)}, bf16[4,256,128]{2,1,0:T(8,128)(2,1)S(1)}, u32[]{:S(2)}, u32[]{:S(2)}) collective-permute-start(bf16[4,256,128]{2,1,0:T(8,128)(2,1)} %bitcast.18), channel_id=1, source_target_pairs={{2,0},{0,2},{3,1},{1,3},{6,4},{4,6},{7,5},{5,7},{10,8},{8,10},{11,... | collective-permute-start | bytes 786440 | tf_op jit(solution)/shard_map/ppermute | solution.py:34
  6.2 0.8 %reshape.48 = s32[8]{0:T(128)S(1)} reshape(s32[1,2,4]{2,1,0:T(2,128)} %param.14) | data formatting | bytes 64 | tf_op jit(solution)/shard_map/reshape | solution.py:322
  7.9 0.8 %copy.13 = f32[1,2,4,2]{3,2,1,0:T(4,128)S(1)} copy(f32[1,2,4,2]{2,3,1,0:T(2,128)} %param.13) | data formatting | bytes 128 | tf_op jit(solution)/shard_map/reshape | solution.py:336
  8.7 3.7 %collective-permute-done.1.refs_3_ = bf16[4,256,128]{2,1,0:T(8,128)(2,1)S(1)} collective-permute-done((bf16[4,256,128]{2,1,0:T(8,128)(2,1)}, bf16[4,256,128]{2,1,0:T(8,128)(2,1)S(1)}, u32[]{:S(2)}, u32[]{:S(2)}) %collective-permute-start.1) | collective-permute-done | bytes 262176 | tf_op jit(solution)/shard_map/ppermute | solution.py:34
  12.4 1.6 %collective-permute-start.4 = (bf16[4,256,128]{2,1,0:T(8,128)(2,1)S(1)}, bf16[4,256,128]{2,1,0:T(8,128)(2,1)S(1)}, u32[]{:S(2)}, u32[]{:S(2)}) collective-permute-start(bf16[4,256,128]{2,1,0:T(8,128)(2,1)S(1)} %collective-permute-done.1.refs_3_), channel_id=1, source_target_pairs={{4,0},{8,4},{12,8},{28,12},{24,28},{20,24},{16,20},{0,16},{5,1},{9... | collective-permute-start | bytes 786440 | tf_op jit(solution)/shard_map/ppermute | solution.py:311
  14.5 0.8 %jit_solution_.3.spread_ref = f32[11,24,128]{2,1,0:T(8,128)S(1)} broadcast(f32[11,24]{1,0:T(8,128)} %constant.89.clone), dimensions={0,1} | broadcast | bytes 136224 | tf_op jit(solution)
  16.7 3.2 %taps.1.refs_12_ = bf16[9,2944,128]{2,1,0:T(8,128)(2,1)S(1)} custom-call(s32[1]{0:T(128)} %bitcast.1.core_ref, f32[8,27]{1,0:T(8,128)S(1)} %bitcast.21, f32[27,128]{1,0:T(8,128)S(1)} %copy-done.8, f32[11,24,128]{2,1,0:T(8,128)S(1)} %jit_solution_.3.spread_ref), custom_call_target="tpu_custom_call" | custom-call | flops 3000000000 | bytes 9000000 | tf_op jit(solution)/shard_map/taps/pallas_call | solution.py:342
  21.4 4.1 %norms.1 = (f32[8,256,128]{2,1,0:T(8,128)S(1)}, f32[8,256,128]{2,1,0:T(8,128)S(1)}, bf16[8,256,256]{2,1,0:T(8,128)(2,1)S(1)}, bf16[8,256,128]{2,1,0:T(8,128)(2,1)S(1)}) custom-call(f32[8,2]{1,0:T(8,128)S(1)} %bitcast.12, f32[8]{0:T(128)S(1)} %get-tuple-element.29.live_ref, s32[1]{0:T(128)} %bitcast.1.core_ref, f32[8,256,128]{2,1,0:T(8,128)S(1)} %bitcast.14, ...), custom_call_target="tpu_custom_call" | custom-call | flops 5000000000 | bytes 15000000 | tf_op jit(solution)/shard_map/norms/pallas_call | solution.py:353
  25.6 1.0 %copy-done.9 = f32[8,256,128]{2,1,0:T(8,128)} copy-done((f32[8,256,128]{2,1,0:T(8,128)}, f32[8,256,128]{2,1,0:T(8,128)S(1)}, u32[]{:S(2)}) %copy-start.9) | copy-done | bytes 1048600
  26.5 1.0 %copy-done.11 = bf16[8,256,256]{2,1,0:T(8,128)(2,1)} copy-done((bf16[8,256,256]{2,1,0:T(8,128)(2,1)}, bf16[8,256,256]{2,1,0:T(8,128)(2,1)S(1)}, u32[]{:S(2)}) %copy-start.11) | copy-done | bytes 1048600
  27.5 0.8 %copy-done.13 = bf16[8,256,128]{2,1,0:T(8,128)(2,1)} copy-done((bf16[8,256,128]{2,1,0:T(8,128)(2,1)}, bf16[8,256,128]{2,1,0:T(8,128)(2,1)S(1)}, u32[]{:S(2)}) %copy-start.13) | copy-done | bytes 524312
  28.3 0.9 %copy-done.4 = bf16[4,256,128]{2,1,0:T(8,128)(2,1)S(1)} copy-done((bf16[4,256,128]{2,1,0:T(8,128)(2,1)S(1)}, bf16[4,256,128]{2,1,0:T(8,128)(2,1)}, u32[]{:S(2)}) %copy-start.4) | copy-done | bytes 262168
  29.3 0.9 %copy-done.6 = bf16[4,256,128]{2,1,0:T(8,128)(2,1)S(1)} copy-done((bf16[4,256,128]{2,1,0:T(8,128)(2,1)S(1)}, bf16[4,256,128]{2,1,0:T(8,128)(2,1)}, u32[]{:S(2)}) %copy-start.6) | copy-done | bytes 262168
  30.2 7.8 %convolve.1 = (bf16[8,256,128]{2,1,0:T(8,128)(2,1)S(1)}, bf16[4,256,128]{2,1,0:T(8,128)(2,1)S(1)}, bf16[4,256,128]{2,1,0:T(8,128)(2,1)S(1)}, f32[4,256,128]{2,1,...) custom-call(s32[8]{0:T(128)S(1)} %and_select_fusion.3.slots_ref, ...), custom_call_target="tpu_custom_call" | custom-call | flops 5000000000 | bytes 15000000 | tf_op jit(solution)/shard_map/convolve/pallas_call | solution.py:369
  38.6 1.6 %collective-permute-start.13 = (bf16[4,256,128]{2,1,0:T(8,128)(2,1)S(1)}, bf16[4,256,128]{2,1,0:T(8,128)(2,1)S(1)}, u32[]{:S(2)}, u32[]{:S(2)}) collective-permute-start(bf16[4,256,128]{2,1,0:T(8,128)(2,1)S(1)} %get-tuple-element.17), channel_id=1, source_target_pairs={{4,0},{8,4},{12,8},{28,12},{24,28},{20,24},{16,20},{0,16},{5,1},{9... | collective-permute-start | bytes 786440 | tf_op jit(solution)/shard_map/ppermute | solution.py:311
  40.6 1.6 %collective-permute-start.16 = (bf16[4,256,128]{2,1,0:T(8,128)(2,1)S(1)}, bf16[4,256,128]{2,1,0:T(8,128)(2,1)S(1)}, u32[]{:S(2)}, u32[]{:S(2)}) collective-permute-start(bf16[4,256,128]{2,1,0:T(8,128)(2,1)S(1)} %get-tuple-element.19), channel_id=1, source_target_pairs={{4,0},{8,4},{12,8},{28,12},{24,28},{20,24},{16,20},{0,16},{5,1},{9... | collective-permute-start | bytes 786440 | tf_op jit(solution)/shard_map/ppermute | solution.py:311
  42.2 5.1 %collective-permute-done.12 = bf16[4,256,128]{2,1,0:T(8,128)(2,1)S(1)} collective-permute-done((bf16[4,256,128]{2,1,0:T(8,128)(2,1)S(1)}, bf16[4,256,128]{2,1,0:T(8,128)(2,1)S(1)}, u32[]{:S(2)}, u32[]{:S(2)}) %collective-permute-start.12) | collective-permute-done | bytes 262176 | tf_op jit(solution)/shard_map/ppermute | solution.py:310
  47.9 1.7 %collective-permute-start.14 = (bf16[4,256,128]{2,1,0:T(8,128)(2,1)S(1)}, bf16[4,256,128]{2,1,0:T(8,128)(2,1)S(1)}, u32[]{:S(2)}, u32[]{:S(2)}) collective-permute-start(bf16[4,256,128]{2,1,0:T(8,128)(2,1)S(1)} %add_convert_fusion), channel_id=1, source_target_pairs={{0,2},{2,0},{1,3},{3,1},{4,6},{6,4},{5,7},{7,5},{8,10},{10,8},{9,1... | collective-permute-start | bytes 786440 | tf_op jit(solution)/shard_map/ppermute | solution.py:39
  49.6 1.2 %copy-done.10 = f32[8,256,128]{2,1,0:T(8,128)S(1)} copy-done((f32[8,256,128]{2,1,0:T(8,128)S(1)}, f32[8,256,128]{2,1,0:T(8,128)}, u32[]{:S(2)}) %copy-start.10) | copy-done | bytes 1048600
  50.8 1.2 %copy-done.12 = bf16[8,256,256]{2,1,0:T(8,128)(2,1)S(1)} copy-done((bf16[8,256,256]{2,1,0:T(8,128)(2,1)S(1)}, bf16[8,256,256]{2,1,0:T(8,128)(2,1)}, u32[]{:S(2)}) %copy-start.12) | copy-done | bytes 1048600
  52.0 1.0 %copy-done.14 = bf16[8,256,128]{2,1,0:T(8,128)(2,1)S(1)} copy-done((bf16[8,256,128]{2,1,0:T(8,128)(2,1)S(1)}, bf16[8,256,128]{2,1,0:T(8,128)(2,1)}, u32[]{:S(2)}) %copy-start.14) | copy-done | bytes 524312
  53.1 3.7 %score.1 = f32[8,256,128]{2,1,0:T(8,128)} custom-call(s32[1]{0:T(128)} %bitcast.1.core_ref, bf16[8,256,128]{2,1,0:T(8,128)(2,1)S(1)} %get-tuple-element.20.low_ref, bf16[8,256,128]{2,1,0:T(8,128)(2,1)S(1)} %collective-permute-done.17.other_ref, bf16[8,256,256]{2,1,0:T(8,128)(2,1)S(1)} %copy-done.12, bf16[8,256,128]{2,1,0:T(8,128)(2,1)S(1)} %copy-done.14, ...), custom_call_target="tpu_custom_call" | custom-call | flops 5000000000 | bytes 15000000 | tf_op jit(solution)/shard_map/score/pallas_call | solution.py:407
  56.8 1.0 %add_bitcast_fusion = f32[1,4,256,128]{3,2,1,0:T(8,128)} fusion(bf16[4,256,128]{2,1,0:T(8,128)(2,1)S(1)} %collective-permute-done.16, bf16[4,256,128]{2,1,0:T(8,128)(2,1)S(1)} %collective-permute-done.15, f32[4,256,128]{2,1,0:T(8,128)S(1)} %get-tuple-element.14, bf16[4,256,128]{2,1,0:T(8,128)(2,1)S(1)} %collective-permute-done.14, pred[]{:T(512)S(6)} %select_n.77, ...), kind=kLoop, calls=%fused_computation | loop fusion | flops 1048576 | bytes 1835010 | tf_op jit(solution)/shard_map/reshape | solution.py:416
  (58 shorter events, 7.0 us)
Async XLA Ops:
  0.6 20.8 %copy-start = (f32[1,2,4,256,128]{4,3,2,1,0:T(8,128)S(1)}, f32[1,2,4,256,128]{4,3,2,1,0:T(8,128)}, u32[]{:S(2)}) copy-start(f32[1,2,4,256,128]{4,3,2,1,0:T(8,128)} %param.11) | copy-start | bytes 3145732
  0.6 20.4 %collective-permute-start.11 = (f32[8,256,128]{2,1,0:T(8,128)}, f32[8,256,128]{2,1,0:T(8,128)S(1)}, u32[]{:S(2)}, u32[]{:S(2)}) collective-permute-start(f32[8,256,128]{2,1,0:T(8,128)} %bitcast.13), channel_id=1, source_target_pairs={{0,1},{1,0},{2,3},{3,2},{4,5},{5,4},{6,7},{7,6},{8,9},{9,8},{10,11... | collective-permute-start | bytes 3145736 | tf_op jit(solution)/shard_map/ppermute | solution.py:39
  1.2 12.8 %collective-permute-start.7 = (bf16[4,256,128]{2,1,0:T(8,128)(2,1)}, bf16[4,256,128]{2,1,0:T(8,128)(2,1)S(1)}, u32[]{:S(2)}, u32[]{:S(2)}) collective-permute-start(bf16[4,256,128]{2,1,0:T(8,128)(2,1)} %bitcast.16), channel_id=1, source_target_pairs={{0,1},{1,0},{2,3},{3,2},{4,5},{5,4},{6,7},{7,6},{8,9},{9,8},{10,11... | collective-permute-start | bytes 786440 | tf_op jit(solution)/shard_map/ppermute | solution.py:39
  1.3 18.6 %collective-permute-start.3 = (bf16[4,256,128]{2,1,0:T(8,128)(2,1)}, bf16[4,256,128]{2,1,0:T(8,128)(2,1)S(1)}, u32[]{:S(2)}, u32[]{:S(2)}) collective-permute-start(bf16[4,256,128]{2,1,0:T(8,128)(2,1)} %bitcast.17), channel_id=1, source_target_pairs={{4,0},{8,4},{12,8},{28,12},{24,28},{20,24},{16,20},{0,16},{5,1},{9... | collective-permute-start | bytes 786440 | tf_op jit(solution)/shard_map/ppermute | solution.py:311
  4.2 8.2 %collective-permute-start.1 = (bf16[4,256,128]{2,1,0:T(8,128)(2,1)}, bf16[4,256,128]{2,1,0:T(8,128)(2,1)S(1)}, u32[]{:S(2)}, u32[]{:S(2)}) collective-permute-start(bf16[4,256,128]{2,1,0:T(8,128)(2,1)} %bitcast.18), channel_id=1, source_target_pairs={{2,0},{0,2},{3,1},{1,3},{6,4},{4,6},{7,5},{5,7},{10,8},{8,10},{11,... | collective-permute-start | bytes 786440 | tf_op jit(solution)/shard_map/ppermute | solution.py:34
  5.7 14.3 %collective-permute-start = (bf16[4,256,128]{2,1,0:T(8,128)(2,1)}, bf16[4,256,128]{2,1,0:T(8,128)(2,1)S(1)}, u32[]{:S(2)}, u32[]{:S(2)}) collective-permute-start(bf16[4,256,128]{2,1,0:T(8,128)(2,1)} %bitcast.19), channel_id=1, source_target_pairs={{0,4},{4,8},{8,12},{12,28},{28,24},{24,20},{20,16},{16,0},{1,5},{5... | collective-permute-start | bytes 786440 | tf_op jit(solution)/shard_map/ppermute | solution.py:310
  12.4 13.1 %copy-start.3 = (bf16[4,256,128]{2,1,0:T(8,128)(2,1)}, bf16[4,256,128]{2,1,0:T(8,128)(2,1)S(1)}, u32[]{:S(2)}) copy-start(bf16[4,256,128]{2,1,0:T(8,128)(2,1)S(1)} %collective-permute-done.1.refs_3_) | copy-start | bytes 786436
  12.4 8.0 %collective-permute-start.4 = (bf16[4,256,128]{2,1,0:T(8,128)(2,1)S(1)}, bf16[4,256,128]{2,1,0:T(8,128)(2,1)S(1)}, u32[]{:S(2)}, u32[]{:S(2)}) collective-permute-start(bf16[4,256,128]{2,1,0:T(8,128)(2,1)S(1)} %collective-permute-done.1.refs_3_), channel_id=1, source_target_pairs={{4,0},{8,4},{12,8},{28,12},{24,28},{20,24},{16,20},{0,16},{5,1},{9... | collective-permute-start | bytes 786440 | tf_op jit(solution)/shard_map/ppermute | solution.py:311
  14.0 6.9 %collective-permute-start.2 = (bf16[4,256,128]{2,1,0:T(8,128)(2,1)S(1)}, bf16[4,256,128]{2,1,0:T(8,128)(2,1)S(1)}, u32[]{:S(2)}, u32[]{:S(2)}) collective-permute-start(bf16[4,256,128]{2,1,0:T(8,128)(2,1)S(1)} %collective-permute-done.1.refs_3_), channel_id=1, source_target_pairs={{0,4},{4,8},{8,12},{12,28},{28,24},{24,20},{20,16},{16,0},{1,5},{5... | collective-permute-start | bytes 786440 | tf_op jit(solution)/shard_map/ppermute | solution.py:310
  19.9 8.4 %collective-permute-start.8 = (bf16[4,256,128]{2,1,0:T(8,128)(2,1)S(1)}, bf16[4,256,128]{2,1,0:T(8,128)(2,1)S(1)}, u32[]{:S(2)}, u32[]{:S(2)}) collective-permute-start(bf16[4,256,128]{2,1,0:T(8,128)(2,1)S(1)} %collective-permute-done.1.refs_3_), channel_id=1, source_target_pairs={{0,1},{1,0},{2,3},{3,2},{4,5},{5,4},{6,7},{7,6},{8,9},{9,8},{10,11... | collective-permute-start | bytes 786440 | tf_op jit(solution)/shard_map/ppermute | solution.py:39
  20.0 5.6 %copy-start.5 = (bf16[4,256,128]{2,1,0:T(8,128)(2,1)}, bf16[4,256,128]{2,1,0:T(8,128)(2,1)S(1)}, u32[]{:S(2)}) copy-start(bf16[4,256,128]{2,1,0:T(8,128)(2,1)S(1)} %collective-permute-done.refs_0_) | copy-start | bytes 786436
  20.0 8.3 %collective-permute-start.9 = (bf16[4,256,128]{2,1,0:T(8,128)(2,1)S(1)}, bf16[4,256,128]{2,1,0:T(8,128)(2,1)S(1)}, u32[]{:S(2)}, u32[]{:S(2)}) collective-permute-start(bf16[4,256,128]{2,1,0:T(8,128)(2,1)S(1)} %collective-permute-done.3.refs_4_), channel_id=1, source_target_pairs={{0,1},{1,0},{2,3},{3,2},{4,5},{5,4},{6,7},{7,6},{8,9},{9,8},{10,11... | collective-permute-start | bytes 786440 | tf_op jit(solution)/shard_map/ppermute | solution.py:39
  20.5 7.8 %collective-permute-start.5 = (bf16[4,256,128]{2,1,0:T(8,128)(2,1)S(1)}, bf16[4,256,128]{2,1,0:T(8,128)(2,1)S(1)}, u32[]{:S(2)}, u32[]{:S(2)}) collective-permute-start(bf16[4,256,128]{2,1,0:T(8,128)(2,1)S(1)} %collective-permute-done.refs_0_), channel_id=1, source_target_pairs={{0,1},{1,0},{2,3},{3,2},{4,5},{5,4},{6,7},{7,6},{8,9},{9,8},{10,11... | collective-permute-start | bytes 786440 | tf_op jit(solution)/shard_map/ppermute | solution.py:39
  20.9 7.4 %collective-permute-start.10 = (bf16[4,256,128]{2,1,0:T(8,128)(2,1)S(1)}, bf16[4,256,128]{2,1,0:T(8,128)(2,1)S(1)}, u32[]{:S(2)}, u32[]{:S(2)}) collective-permute-start(bf16[4,256,128]{2,1,0:T(8,128)(2,1)S(1)} %collective-permute-done.4.refs_5_), channel_id=1, source_target_pairs={{0,1},{1,0},{2,3},{3,2},{4,5},{5,4},{6,7},{7,6},{8,9},{9,8},{10,11... | collective-permute-start | bytes 786440 | tf_op jit(solution)/shard_map/ppermute | solution.py:39
  21.0 7.3 %collective-permute-start.6 = (bf16[4,256,128]{2,1,0:T(8,128)(2,1)S(1)}, bf16[4,256,128]{2,1,0:T(8,128)(2,1)S(1)}, u32[]{:S(2)}, u32[]{:S(2)}) collective-permute-start(bf16[4,256,128]{2,1,0:T(8,128)(2,1)S(1)} %collective-permute-done.2.refs_1_), channel_id=1, source_target_pairs={{0,1},{1,0},{2,3},{3,2},{4,5},{5,4},{6,7},{7,6},{8,9},{9,8},{10,11... | collective-permute-start | bytes 786440 | tf_op jit(solution)/shard_map/ppermute | solution.py:39
  21.4 6.9 %copy-start.1 = (bf16[1,2,4,256,128]{4,3,2,1,0:T(8,128)(2,1)S(1)}, bf16[1,2,4,256,128]{4,3,2,1,0:T(8,128)(2,1)}, u32[]{:S(2)}) copy-start(bf16[1,2,4,256,128]{4,3,2,1,0:T(8,128)(2,1)} %param.10) | copy-start | bytes 1572868
  21.4 6.9 %copy-start.2 = (bf16[1,4,256,128]{3,2,1,0:T(8,128)(2,1)S(1)}, bf16[1,4,256,128]{3,2,1,0:T(8,128)(2,1)}, u32[]{:S(2)}) copy-start(bf16[1,4,256,128]{3,2,1,0:T(8,128)(2,1)} %param.9) | copy-start | bytes 786436
  38.0 11.6 %collective-permute-start.17 = (bf16[8,256,128]{2,1,0:T(8,128)(2,1)S(1)}, bf16[8,256,128]{2,1,0:T(8,128)(2,1)S(1)}, u32[]{:S(2)}, u32[]{:S(2)}) collective-permute-start(bf16[8,256,128]{2,1,0:T(8,128)(2,1)S(1)} %get-tuple-element.20.low_ref), channel_id=1, source_target_pairs={{0,1},{1,0},{2,3},{3,2},{4,5},{5,4},{6,7},{7,6},{8,9},{9,8},{10,11... | collective-permute-start | bytes 1572872 | tf_op jit(solution)/shard_map/ppermute | solution.py:39
  38.2 9.2 %collective-permute-start.12 = (bf16[4,256,128]{2,1,0:T(8,128)(2,1)S(1)}, bf16[4,256,128]{2,1,0:T(8,128)(2,1)S(1)}, u32[]{:S(2)}, u32[]{:S(2)}) collective-permute-start(bf16[4,256,128]{2,1,0:T(8,128)(2,1)S(1)} %get-tuple-element.16), channel_id=1, source_target_pairs={{0,4},{4,8},{8,12},{12,28},{28,24},{24,20},{20,16},{16,0},{1,5},{5... | collective-permute-start | bytes 786440 | tf_op jit(solution)/shard_map/ppermute | solution.py:310
  38.6 9.2 %collective-permute-start.13 = (bf16[4,256,128]{2,1,0:T(8,128)(2,1)S(1)}, bf16[4,256,128]{2,1,0:T(8,128)(2,1)S(1)}, u32[]{:S(2)}, u32[]{:S(2)}) collective-permute-start(bf16[4,256,128]{2,1,0:T(8,128)(2,1)S(1)} %get-tuple-element.17), channel_id=1, source_target_pairs={{4,0},{8,4},{12,8},{28,12},{24,28},{20,24},{16,20},{0,16},{5,1},{9... | collective-permute-start | bytes 786440 | tf_op jit(solution)/shard_map/ppermute | solution.py:311
  40.2 16.5 %collective-permute-start.15 = (bf16[4,256,128]{2,1,0:T(8,128)(2,1)S(1)}, bf16[4,256,128]{2,1,0:T(8,128)(2,1)S(1)}, u32[]{:S(2)}, u32[]{:S(2)}) collective-permute-start(bf16[4,256,128]{2,1,0:T(8,128)(2,1)S(1)} %get-tuple-element.18), channel_id=1, source_target_pairs={{0,4},{4,8},{8,12},{12,28},{28,24},{24,20},{20,16},{16,0},{1,5},{5... | collective-permute-start | bytes 786440 | tf_op jit(solution)/shard_map/ppermute | solution.py:310
  40.6 16.1 %collective-permute-start.16 = (bf16[4,256,128]{2,1,0:T(8,128)(2,1)S(1)}, bf16[4,256,128]{2,1,0:T(8,128)(2,1)S(1)}, u32[]{:S(2)}, u32[]{:S(2)}) collective-permute-start(bf16[4,256,128]{2,1,0:T(8,128)(2,1)S(1)} %get-tuple-element.19), channel_id=1, source_target_pairs={{4,0},{8,4},{12,8},{28,12},{24,28},{20,24},{16,20},{0,16},{5,1},{9... | collective-permute-start | bytes 786440 | tf_op jit(solution)/shard_map/ppermute | solution.py:311
  47.9 8.8 %collective-permute-start.14 = (bf16[4,256,128]{2,1,0:T(8,128)(2,1)S(1)}, bf16[4,256,128]{2,1,0:T(8,128)(2,1)S(1)}, u32[]{:S(2)}, u32[]{:S(2)}) collective-permute-start(bf16[4,256,128]{2,1,0:T(8,128)(2,1)S(1)} %add_convert_fusion), channel_id=1, source_target_pairs={{0,2},{2,0},{1,3},{3,1},{4,6},{6,4},{5,7},{7,5},{8,10},{10,8},{9,1... | collective-permute-start | bytes 786440 | tf_op jit(solution)/shard_map/ppermute | solution.py:39
  49.6 1.2 %copy-start.10 = (f32[8,256,128]{2,1,0:T(8,128)S(1)}, f32[8,256,128]{2,1,0:T(8,128)}, u32[]{:S(2)}) copy-start(f32[8,256,128]{2,1,0:T(8,128)} %copy-done.9) | copy-start | bytes 3145732
  (9 other events, 8.3 us)

commit v3 on v2

--- a/solution.py
+++ b/solution.py
@@ -8,11 +8,13 @@
 from jax.experimental.pallas import tpu as pltpu
 from jax.sharding import PartitionSpec as P
 
+
 HW = 10
 PW = 7
 
 sigmas = (0.75, 1.5, 3.0)
 degrees = (4, 2, 2)
+
 
 VMEM = pltpu.VMEM
 SMEM = pltpu.SMEM
@@ -50,54 +52,53 @@
     return terms
 
 
-def profile(offset, sigma, power, reach):
-    grid = np.arange(-reach, reach + 1).astype(np.float32)
-    base = np.exp(-grid * grid / np.float32(2.0 * sigma * sigma)) * (grid / reach) ** power
-    scale = np.sqrt(np.sum(base * base))
-    spot = offset.astype(np.float32)
-    value = np.exp(-spot * spot / np.float32(2.0 * sigma * sigma)) * (spot / reach) ** power / scale
-    return np.where(np.abs(offset) <= reach, value, 0.0).astype(np.float32)
-
-
-def ring_profiles(width, reach):
-    lane = np.arange(width)
-    offset = np.where(lane < width // 2, lane, lane - width)
-    return np.stack([profile(offset, sigmas[t[0]], t[2], reach) for t in basis_terms()])
-
-
-def row_profiles(reach, rows, lanes):
-    offset = np.arange(rows) - reach
+def norm_of(sigma, power, reach):
+    grid = np.arange(-reach, reach + 1).astype(np.float64)
+    base = np.exp(-grid * grid / (2.0 * sigma * sigma)) * (grid / reach) ** power
+    return float(1.0 / np.sqrt(np.sum(base * base)))
+
+
+def profiles_of(offset, reach):
+    spot = offset.astype(jnp.float32)
+    inside = jnp.abs(offset) <= reach
     tables = []
     for group in range(3):
-        for first in range(degrees[group] + 1):
-            tables.append(profile(offset, sigmas[group], first, reach))
-    table = np.stack(tables).astype(jnp.bfloat16).astype(np.float32)
-    return np.broadcast_to(table[:, :, None], table.shape + (lanes,))
-
-
-def taps_kernel(core_ref, coeff_ref, ring_ref, spread_ref, band_ref, taps_ref, edge_ref):
-    tiles = coeff_ref.shape[0]
-    cols = ring_ref.shape[1]
+        base = jnp.where(inside, jnp.exp(spot * spot * (-0.5 / sigmas[group] ** 2)), 0.0)
+        for power in range(degrees[group] + 1):
+            tables.append(base * norm_of(sigmas[group], power, reach))
+            base = base * (spot / reach)
+    return tables
+
+
+def taps_kernel(coeff_ref, band_ref, taps_ref, edge_ref):
+    tiles, held, cols = taps_ref.shape
+    slots = coeff_ref.shape[2]
     group = cols // tiles
     reach = HW
     terms = basis_terms()
-    profiles = spread_ref.shape[0]
+    lane = lax.broadcasted_iota(jnp.int32, (1, cols), 1)
+    ring = profiles_of(jnp.where(lane < cols // 2, lane, lane - cols), reach)
+    spread = profiles_of(lax.broadcasted_iota(jnp.int32, (held, cols), 0) - reach, reach)
+    spread = [table.astype(jnp.bfloat16).astype(jnp.float32) for table in spread]
+    starts = [0]
+    for degree in degrees:
+        starts.append(starts[-1] + degree + 1)
     across = lax.broadcasted_iota(jnp.int32, (cols, cols), 1)
     down = lax.broadcasted_iota(jnp.int32, (cols, cols), 0)
     near = jnp.abs(across - down) <= reach
     same = (across // group) == (down // group)
     count = 2 * reach + 1
-    turn = jnp.where(core_ref[0] == 0, group, cols - group)
+    turn = jnp.where(lax.axis_index("band") == 0, group, cols - group)
 
     def one(t, carry):
         taps = jnp.zeros(taps_ref.shape[1:], jnp.float32)
-        for p in range(profiles):
+        for p in range(len(spread)):
             vec = jnp.zeros((1, cols), jnp.float32)
             for k, term in enumerate(terms):
                 if term[3] == p:
-                    vec = vec + coeff_ref[t, k] * ring_ref[k : k + 1, :]
+                    vec = vec + coeff_ref[0, t // slots, t % slots, k] * ring[starts[term[0]] + term[2]]
             vec = vec.astype(jnp.bfloat16).astype(jnp.float32)
-            taps = taps + spread_ref[p] * vec
+            taps = taps + spread[p] * vec
         taps_ref[t] = taps
         edge_ref[t] = pltpu.roll(taps, turn, 1)
         band_ref[t, 0:cols, :] = jnp.zeros((cols, cols), jnp.bfloat16)
@@ -121,7 +122,11 @@
         band_ref[tiles, (count - u) * cols : (count - u + 1) * cols, :] = full
 
 
-def norms_kernel(width_ref, live_ref, core_ref, own_ref, other_ref,
+def alive(live_ref, t, slots):
+    return jnp.where(t % slots < live_ref[0, t // slots], 1.0, 0.0)
+
+
+def norms_kernel(width_ref, live_ref, own_ref, other_ref,
                  norm_ref, inv_ref, prow_ref, pcol_ref, dist_ref, near_ref):
     tiles, size, cols = own_ref.shape
     wide = 2 * cols
@@ -135,7 +140,8 @@
     ring = jnp.minimum(ring, wide - ring)
     near_ref[...] = (ring * ring).astype(jnp.float32)
     lane = lax.broadcasted_iota(jnp.int32, (size, cols), 1)
-    keep = (lane >= cols // 2) == (core_ref[0] == 1)
+    keep = (lane >= cols // 2) == (lax.axis_index("band") == 1)
+    slots = width_ref.shape[3]
     limit = float(PW * PW)
     spot = lax.broadcasted_iota(jnp.int32, (8, 128), 1)
     spot_low = spot.astype(jnp.float32) - PW
@@ -151,15 +157,15 @@
         inv_other = jnp.where(keep, 1.0 / other_ref[t], 0.0)
         inv_ref[t] = inv_own
         inv_low = jnp.concatenate([inv_own, inv_other], axis=1).astype(jnp.bfloat16)
-        prow = table(jnp.full((8, 128), width_ref[t, 0], jnp.float32), dist_ref[...])
+        prow = table(jnp.full((8, 128), width_ref[0, t // slots, 0, t % slots], jnp.float32), dist_ref[...])
         prow_ref[t] = prow.astype(jnp.bfloat16)
         qrow = (prow * prow).astype(jnp.bfloat16)
-        pcol = table(jnp.full((8, 128), width_ref[t, 1], jnp.float32), near_ref[...])
+        pcol = table(jnp.full((8, 128), width_ref[0, t // slots, 1, t % slots], jnp.float32), near_ref[...])
         pcol_ref[t] = pcol.astype(jnp.bfloat16)
         qcol = (pcol * pcol).astype(jnp.bfloat16)
         denom = jnp.dot(qrow, inv_low, preferred_element_type=jnp.float32).astype(jnp.bfloat16)
         denom = jnp.dot(denom, qcol, preferred_element_type=jnp.float32)
-        norm_ref[t] = live_ref[t] / jnp.sqrt(denom)
+        norm_ref[t] = alive(live_ref, t, slots) / jnp.sqrt(denom)
         return carry
 
     lax.fori_loop(0, tiles, one, 0)
@@ -168,7 +174,7 @@
 PAD = 16
 
 
-def convolve_kernel(blocks, slots_ref, part_ref, live_ref, present_ref, core_ref, *refs):
+def convolve_kernel(blocks, closed, ids_ref, live_ref, *refs):
     own_blocks = refs[:blocks]
     other_blocks = refs[blocks : 2 * blocks]
     (band_ref, exp_ref, inv_ref) = refs[2 * blocks : 2 * blocks + 3]
@@ -182,18 +188,35 @@
     first = PAD - HW
     pairs = size // 2
 
-    def copies(t, b):
-        slot = slots_ref[t]
+    slots = ids_ref.shape[2]
+    core = lax.axis_index("band")
+    row = lax.axis_index("exp")
+    rows = lax.axis_size("exp")
+    columns = lax.axis_size("patch")
+    flip = lax.rem(lax.axis_index("groups"), 2) if closed else 0
+
+    def place(t):
+        name = ids_ref[0, t // slots, t % slots]
+        step = name // (owned * columns)
+        column = name - step * (owned * columns)
+        owner = column // owned
+        shift = lax.rem(owner - lax.axis_index("patch") + columns, columns)
+        inside = (row + step >= 1) & (row + step <= rows)
+        step = jnp.where(flip == 0, step, 2 - step)
+        return step * columns + shift, column - owner * owned, jnp.where(inside, 1.0, 0.0)
+
+    def copies(t, b, slot=0):
         return (
             pltpu.make_async_copy(own_blocks[b].at[slot], tile_ref.at[0, t], sem.at[t, 0]),
             pltpu.make_async_copy(other_blocks[b].at[slot], tile_ref.at[1, t], sem.at[t, 1]),
         )
 
     for t in range(tiles):
+        part, slot, _ = place(t)
         for b in range(blocks):
-            @pl.when(part_ref[t] == b)
-            def _(t=t, b=b):
-                for c in copies(t, b):
+            @pl.when(part == b)
+            def _(t=t, b=b, slot=slot):
+                for c in copies(t, b, slot):
                     c.start()
 
     acc_ref[...] = jnp.zeros_like(acc_ref)
@@ -211,7 +234,7 @@
         return jnp.dot(lhs_ref[...], weights, preferred_element_type=jnp.float32)
 
     lane = lax.broadcasted_iota(jnp.int32, (1, cols), 1)
-    start = jnp.where(core_ref[0] == 0, 0, cols - group)
+    start = jnp.where(core == 0, 0, cols - group)
     target = cols - group - start
     strip = jnp.zeros((size, cols), jnp.float32)
     for t in range(tiles):
@@ -230,11 +253,11 @@
             edge = pltpu.roll(edge_ref[:, s * cols : (s + 1) * cols], turn, 1)
             edge = jnp.where((lane >= target) & (lane < target + group), edge, 0.0)
             conv_ref[pl.ds(s, pairs, stride=2), :] = both[:, s * cols : (s + 1) * cols] + edge
-        convolved = conv_ref[...] * present_ref[t]
+        part, slot, present = place(t)
+        convolved = conv_ref[...] * present
         own = (exp_ref[t].astype(jnp.float32) - convolved) * inv_ref[t]
         low_ref[t] = own.astype(jnp.bfloat16)
-        where = part_ref[t] * owned + slots_ref[t]
-        acc_ref[where] += live_ref[t] * own
+        acc_ref[part * owned + slot] += alive(live_ref, t, slots) * own
         return carry
 
     lax.fori_loop(0, tiles, one, 0)
@@ -242,10 +265,10 @@
         out_refs[b][...] = acc_ref[b * owned : (b + 1) * owned].astype(out_refs[b].dtype)
 
 
-def score_kernel(core_ref, low_ref, other_ref, prow_ref, pcol_ref, norm_ref, score_ref):
+def score_kernel(low_ref, other_ref, prow_ref, pcol_ref, norm_ref, score_ref):
     tiles, size, cols = low_ref.shape
     lane = lax.broadcasted_iota(jnp.int32, (size, cols), 1)
-    keep = (lane >= cols // 2) == (core_ref[0] == 1)
+    keep = (lane >= cols // 2) == (lax.axis_index("band") == 1)
 
     def one(t, carry):
         other = jnp.where(keep, other_ref[t].astype(jnp.float32), 0.0).astype(jnp.bfloat16)
@@ -259,6 +282,29 @@
     lax.fori_loop(0, tiles, one, 0)
 
 
+def merge_kernel(closed, here_ref, first_ref, last_ref, *refs):
+    row = lax.axis_index("exp")
+    rows = lax.axis_size("exp")
+    flip = lax.rem(lax.axis_index("groups"), 2) if closed else 0
+    has_first = jnp.where(flip == 0, row > 0, row < rows - 1)
+    has_last = jnp.where(flip == 0, row < rows - 1, row > 0)
+    out_ref = refs[-1]
+    owned, size, _ = out_ref.shape
+    chunk = size // 4
+
+    def one(i, carry):
+        at = (i // 4, pl.ds(pl.multiple_of(i % 4 * chunk, chunk), chunk))
+        total = here_ref[at].astype(jnp.float32)
+        total = total + jnp.where(has_first, first_ref[at].astype(jnp.float32), 0.0)
+        total = total + jnp.where(has_last, last_ref[at].astype(jnp.float32), 0.0)
+        for ref in refs[:-1]:
+            total = total + ref[at].astype(jnp.float32)
+        out_ref[at] = total.astype(out_ref.dtype)
+        return carry
+
+    lax.fori_loop(0, owned * 4, one, 0)
+
+
 def shape(dims, dtype):
     return jax.ShapeDtypeStruct(dims, dtype)
 
@@ -287,14 +333,8 @@
     size = templates.shape[2]
     cols = templates.shape[3]
     owned = templates.shape[1]
-    slots = patch_ids.shape[2]
     across = lax.axis_size("patch")
-    patches_row = owned * across
     blocks = 3 * across
-    me = lax.axis_index("patch")
-    row_index = lax.axis_index("exp")
-    rows = lax.axis_size("exp")
-    core = lax.axis_index("band").astype(jnp.int32).reshape(1)
     low = jnp.bfloat16
     f32 = jnp.float32
 
@@ -305,50 +345,29 @@
     assert cols % tiles == 0 and cols // tiles >= HW and size % 32 == 0
     swap = functools.partial(sent, axis="band", distance=1)
 
-    forth, back, closed = neighbours(lax.axis_size("groups"), rows)
-    flip = lax.axis_index("groups") % 2 if closed else 0
+    forth, back, closed = neighbours(lax.axis_size("groups"), lax.axis_size("exp"))
     ahead = lambda block: lax.ppermute(block, ("groups", "exp"), forth)
     behind = lambda block: lax.ppermute(block, ("groups", "exp"), back)
-    from_first = jnp.where(flip == 0, row_index > 0, row_index < rows - 1)
-    from_last = jnp.where(flip == 0, row_index < rows - 1, row_index > 0)
-
     row = [own] + [fetched(own, "patch", d) for d in range(1, across)]
-    firsts = [ahead(b) for b in row]
-    lasts = [behind(b) for b in row]
-    window = firsts + row + lasts
-    window_other = [swap(b) for b in window]
+    firsts = [ahead(own)]
+    lasts = [behind(own)]
     var_other = swap(var_flat)
 
-    ids = patch_ids.reshape(-1)
-    column = ids % patches_row
-    shift = (column // owned - me + across) % across
-    step = ids // patches_row
-    present = ((row_index + step >= 1) & (row_index + step <= rows)).astype(f32)
-    step = jnp.where(flip == 0, step, 2 - step)
-    part = step * across + shift
-    slot = column % owned
-    live = (
-        (jnp.arange(slots, dtype=jnp.int32)[None, None, :] < live_count[:, :, None])
-        .astype(f32)
-        .reshape(-1)
-    )
-    coeff = coefficients.reshape(tiles, -1)
-    width = psf_width.reshape(tiles, 2)
-    ring = jnp.asarray(ring_profiles(cols, HW))
     count = 2 * HW + 1
     held = -(-count // 8) * 8
-    spread = jnp.asarray(row_profiles(HW, held, cols))
-
     band = pl.pallas_call(
         taps_kernel,
         name="taps",
         out_shape=shape((tiles + 1, (count + 2) * cols, cols), low),
-        in_specs=smem(2) + vmem(2),
+        in_specs=smem(1),
         out_specs=vmem(1)[0],
         scratch_shapes=[VMEM((tiles, held, cols), f32), VMEM((tiles, held, cols), f32)],
-        compiler_params=params(12),
+        compiler_params=params(4),
         cost_estimate=cost(3),
-    )(core, coeff, ring, spread)
+    )(coefficients)
+    band, row = lax.optimization_barrier((band, row))
+    firsts += [ahead(row[d]) for d in range(1, across)]
+    lasts += [behind(row[d]) for d in range(1, across)]
 
     norm, inv, prow, pcol = pl.pallas_call(
         norms_kernel,
@@ -359,21 +378,26 @@
             shape((tiles, size, size), low),
             shape((tiles, 2 * cols, cols), low),
         ),
-        in_specs=smem(3) + vmem(2),
+        in_specs=smem(2) + vmem(2),
         out_specs=tuple(vmem(4)),
         scratch_shapes=[VMEM((size, size), f32), VMEM((2 * cols, cols), f32)],
-        compiler_params=params(12),
+        compiler_params=params(6),
         cost_estimate=cost(5),
-    )(width, live, core, var_flat, var_other)
+    )(jnp.swapaxes(psf_width, 2, 3), live_count, var_flat, var_other)
+    early = [swap(b) for b in [firsts[0]] + row + [lasts[0]]]
+    inv, firsts[1:], lasts[1:] = lax.optimization_barrier((inv, firsts[1:], lasts[1:]))
+    window = firsts + row + lasts
+    window_other = early[:1] + [swap(b) for b in firsts[1:]] + early[1:-1]
+    window_other = window_other + early[-1:] + [swap(b) for b in lasts[1:]]
 
     outs = pl.pallas_call(
-        functools.partial(convolve_kernel, blocks),
+        functools.partial(convolve_kernel, blocks, closed),
         name="convolve",
         out_shape=tuple(
             [shape((tiles, size, cols), low)]
             + [shape((owned, size, cols), f32 if b == across else low) for b in range(blocks)]
         ),
-        in_specs=smem(5) + anywhere(2 * blocks) + vmem(3),
+        in_specs=smem(2) + anywhere(2 * blocks) + vmem(3),
         out_specs=tuple(vmem(1 + blocks)),
         scratch_shapes=[
             VMEM((2, tiles, size, cols), low),
@@ -384,35 +408,44 @@
             VMEM((blocks * owned, size, cols), f32),
             pltpu.SemaphoreType.DMA((tiles, 2)),
         ],
-        compiler_params=params(24),
+        compiler_params=params(12),
         cost_estimate=cost(5),
-    )(slot, part, live, present, core, *window, *window_other, band, exp_flat, inv)
+    )(patch_ids, live_count, *window, *window_other, band, exp_flat, inv)
     weighted_low = outs[0]
     parts = outs[1:]
 
-    from_ahead = [ahead(parts[2 * across + d]) for d in reversed(range(across))][::-1]
-    from_behind = [behind(parts[d]) for d in reversed(range(across))][::-1]
     weighted_other = swap(weighted_low)
-
-    def received(d):
-        one = jnp.where(from_first, from_ahead[d].astype(f32), 0.0)
-        return one + jnp.where(from_last, from_behind[d].astype(f32), 0.0)
-
-    total = parts[across]
-    for d in range(1, across):
-        merged = (parts[across + d].astype(f32) + received(d)).astype(low)
-        total = total + sent(merged, "patch", d).astype(f32)
-    total = total + received(0)
-
+    from_ahead = [ahead(parts[2 * across + d]) for d in range(across)]
+    from_behind = [behind(parts[d]) for d in range(across)]
     score = pl.pallas_call(
         score_kernel,
         name="score",
         out_shape=shape((tiles, size, cols), f32),
-        in_specs=smem(1) + vmem(5),
+        in_specs=vmem(5),
         out_specs=vmem(1)[0],
-        compiler_params=params(12),
+        compiler_params=params(4),
         cost_estimate=cost(5),
-    )(core, weighted_low, weighted_other, prow, pcol, norm)
+    )(weighted_low, weighted_other, prow, pcol, norm)
+    score, from_ahead[1:], from_behind[1:] = lax.optimization_barrier(
+        (score, from_ahead[1:], from_behind[1:])
+    )
+
+    def merge(dtype, *arrays):
+        return pl.pallas_call(
+            functools.partial(merge_kernel, closed),
+            name="merge",
+            out_shape=shape((owned, size, cols), dtype),
+            in_specs=vmem(len(arrays)),
+            out_specs=vmem(1)[0],
+            compiler_params=params(2),
+            cost_estimate=cost(0.5),
+        )(*arrays)
+
+    come = []
+    for d in range(1, across):
+        merged = merge(low, parts[across + d], from_ahead[d], from_behind[d])
+        come.append(sent(merged, "patch", d))
+    total = merge(f32, parts[across], from_ahead[0], from_behind[0], *come)
     return (total.reshape(1, owned, size, cols), score.reshape(exposures.shape))
 
 
@@ -431,6 +464,9 @@
         P(("groups", "exp"), "patch", None, "band"),
         P(("groups", "exp"), "patch", None, None, "band"),
     )
-    return jax.shard_map(
-        on_device, mesh=mesh, in_specs=in_specs, out_specs=out_specs, check_vma=False
-    )
+
+    def step(*args):
+        return on_device(*args)
+
+    step = jax.shard_map(step, mesh=mesh, in_specs=in_specs, out_specs=out_specs, check_vma=False)
+    return step

time: 58.2 us -> 55.9 us (0.960)
  local copies, waits for them, and re-layouts: 12.7 us -> 0.72 us
  waiting for transfers between devices: 9.63 us -> 19.9 us
  Pallas kernels: 18.8 us -> 20.3 us
  other arithmetic: 1.13 us -> 0 us
  starting transfers between devices: 14.6 us -> 14 us
    unnamed x30 -> x14, local copies, waits for them, and re-layouts: 9.54 us -> 0.72 us
    ppermute x9, waiting for transfers between devices: 0.02 us -> 7.45 us  [sent(): lax.ppermute(block, axis, [(i, (i + distance) % devices) for i in range(d...]
    ppermute x4, waiting for transfers between devices: 5.45 us -> 7.77 us  [on_device(): ahead = lambda block: lax.ppermute(block, ('groups', 'exp'), forth)]
    ppermute x4, waiting for transfers between devices: 0.42 us -> 2.1 us  [on_device(): behind = lambda block: lax.ppermute(block, ('groups', 'exp'), back)]
    reshape x2 -> x0, local copies, waits for them, and re-layouts: 1.53 us -> none  [the longest x1 0.78 us: on_device(): width = psf_width.reshape(tiles, 2)]
    pallas_call x1 -> x3, Pallas kernels: 7.78 us -> 9.2 us  [the longest x1 7.77 us: on_device(): pl.pallas_call(functools.partial(convolve_kernel, blocks, closed), name='...]
    ppermute x1, waiting for transfers between devices: 3.74 us -> 2.58 us  [fetched(): lax.ppermute(block, axis, [((i + distance) % devices, i) for i in range(d...]
    reshape x1 -> x0, other arithmetic: 0.95 us -> none  [on_device(): return (total.reshape(1, owned, size, cols), score.reshape(exposures.shape))]
  transfers between devices with their start and end apart: 18 -> 18, of which waited for: 4 -> 8; matrix products, arithmetic and copies ran while one was open for 6% -> 0% of each run, Pallas kernels for 19% -> 20%
where the time goes in v3:
time: 55.9 us; the launch traced here: 55.7 us
  Pallas kernels  20.3 us (36%)
  waiting for transfers between devices  19.9 us (36%)
  starting transfers between devices  14 us (25%)
  between operations  0.75 us (1%)
  local copies, waits for them, and re-layouts  0.72 us (1%)
    ppermute x4, waiting for transfers between devices, on_device(): ahead = lambda block: lax.ppermute(block, ('groups', 'exp'), forth)  7.77 us
    pallas_call x1, Pallas kernels, on_device(): pl.pallas_call(functools.partial(convolve_kernel, blocks, closed), name='...  7.77 us
    ppermute x9, waiting for transfers between devices, sent(): lax.ppermute(block, axis, [(i, (i + distance) % devices) for i in range(d...  7.45 us
    ppermute x4, starting transfers between devices, on_device(): behind = lambda block: lax.ppermute(block, ('groups', 'exp'), back)  7.3 us
    pallas_call x1, Pallas kernels, on_device(): pl.pallas_call(norms_kernel, name='norms', out_shape=(shape((tiles, size,...  4.12 us
    pallas_call x1, Pallas kernels, on_device(): pl.pallas_call(score_kernel, name='score', out_shape=shape((tiles, size,...  3.67 us
    ppermute x9, starting transfers between devices, sent(): lax.ppermute(block, axis, [(i, (i + distance) % devices) for i in range(d...  3.39 us
    pallas_call x1, Pallas kernels, on_device(): pl.pallas_call(taps_kernel, name='taps', out_shape=shape((tiles + 1, (cou...  3.31 us
  transfers between devices with their start and end apart: 18, of which 8 were waited for; matrix products, arithmetic and copies ran while one was open for 0% of the time, Pallas kernels for 20%

profile of v3, /device:TPU:0, one launch (start us, length us, event | category | flops | bytes accessed | tf_op | source)
XLA Modules:
  0.0 55.7 jit_solution(17675615010999258361)
XLA Ops:
  0.6 0.6 %collective-permute-start.1 = (f32[8,256,128]{2,1,0:T(8,128)}, f32[8,256,128]{2,1,0:T(8,128)S(1)}, u32[]{:S(2)}, u32[]{:S(2)}) collective-permute-start(f32[8,256,128]{2,1,0:T(8,128)} %bitcast.6), channel_id=1, source_target_pairs={{0,1},{1,0},{2,3},{3,2},{4,5},{5,4},{6,7},{7,6},{8,9},{9,8},{10,11... | collective-permute-start | bytes 3145736 | tf_op jit(solution)/shard_map/ppermute | solution.py:41
  1.2 2.6 %collective-permute-start.5 = (bf16[4,256,128]{2,1,0:T(8,128)(2,1)}, bf16[4,256,128]{2,1,0:T(8,128)(2,1)S(1)}, u32[]{:S(2)}, u32[]{:S(2)}) collective-permute-start(bf16[4,256,128]{2,1,0:T(8,128)(2,1)} %bitcast.9), channel_id=1, source_target_pairs={{4,0},{8,4},{12,8},{28,12},{24,28},{20,24},{16,20},{0,16},{5,1},{9... | collective-permute-start | bytes 786440 | tf_op jit(solution)/shard_map/ppermute | solution.py:350
  3.8 1.5 %collective-permute-start.2 = (bf16[4,256,128]{2,1,0:T(8,128)(2,1)}, bf16[4,256,128]{2,1,0:T(8,128)(2,1)S(1)}, u32[]{:S(2)}, u32[]{:S(2)}) collective-permute-start(bf16[4,256,128]{2,1,0:T(8,128)(2,1)} %bitcast.10), channel_id=1, source_target_pairs={{2,0},{0,2},{3,1},{1,3},{6,4},{4,6},{7,5},{5,7},{10,8},{8,10},{11,... | collective-permute-start | bytes 786440 | tf_op jit(solution)/shard_map/ppermute | solution.py:36
  5.3 0.5 collective-permute-start
  5.8 0.7 %copy-done.3 = f32[1,2,4,27]{3,2,1,0:T(4,128)S(1)} copy-done((f32[1,2,4,27]{3,2,1,0:T(4,128)S(1)}, f32[1,2,4,27]{3,2,1,0:T(4,128)}, u32[]{:S(2)}) %copy-start.3) | copy-done | bytes 888
  6.5 3.3 %taps.1.refs_12_ = bf16[9,2944,128]{2,1,0:T(8,128)(2,1)S(1)} custom-call(f32[1,2,4,27]{3,2,1,0:T(4,128)S(1)} %copy-done.3), custom_call_target="tpu_custom_call" | custom-call | flops 3000000000 | bytes 9000000 | tf_op jit(solution)/shard_map/taps/pallas_call | solution.py:358
  9.8 2.6 %collective-permute-done.2.refs_3_ = bf16[4,256,128]{2,1,0:T(8,128)(2,1)S(1)} collective-permute-done((bf16[4,256,128]{2,1,0:T(8,128)(2,1)}, bf16[4,256,128]{2,1,0:T(8,128)(2,1)S(1)}, u32[]{:S(2)}, u32[]{:S(2)}) %collective-permute-start.2) | collective-permute-done | bytes 262176 | tf_op jit(solution)/shard_map/ppermute | solution.py:36
  12.4 1.6 %collective-permute-start.4 = (bf16[4,256,128]{2,1,0:T(8,128)(2,1)S(1)}, bf16[4,256,128]{2,1,0:T(8,128)(2,1)S(1)}, u32[]{:S(2)}, u32[]{:S(2)}) collective-permute-start(bf16[4,256,128]{2,1,0:T(8,128)(2,1)S(1)} %collective-permute-done.2.refs_3_), channel_id=1, source_target_pairs={{4,0},{8,4},{12,8},{28,12},{24,28},{20,24},{16,20},{0,16},{5,1},{9... | collective-permute-start | bytes 786440 | tf_op jit(solution)/shard_map/ppermute | solution.py:350
  13.9 0.5 collective-permute-start.3
  14.5 4.1 %norms.1 = (f32[8,256,128]{2,1,0:T(8,128)S(1)}, f32[8,256,128]{2,1,0:T(8,128)S(1)}, bf16[8,256,256]{2,1,0:T(8,128)(2,1)S(1)}, bf16[8,256,128]{2,1,0:T(8,128)(2,1)S(1)}) custom-call(f32[1,2,2,4]{3,2,1,0:T(2,128)S(1)} %bitcast.14, s32[1,2]{1,0:T(1,128)S(1)} %copy-done.6, f32[8,256,128]{2,1,0:T(8,128)S(1)} %bitcast.7, ...), custom_call_target="tpu_custom_call" | custom-call | flops 5000000000 | bytes 15000000 | tf_op jit(solution)/shard_map/norms/pallas_call | solution.py:372
  18.6 0.6 collective-permute-start.8
  19.2 1.9 %collective-permute-done.4.refs_5_ = bf16[4,256,128]{2,1,0:T(8,128)(2,1)S(1)} collective-permute-done((bf16[4,256,128]{2,1,0:T(8,128)(2,1)S(1)}, bf16[4,256,128]{2,1,0:T(8,128)(2,1)S(1)}, u32[]{:S(2)}, u32[]{:S(2)}) %collective-permute-start.4) | collective-permute-done | bytes 262176 | tf_op jit(solution)/shard_map/ppermute | solution.py:350
  21.1 1.3 %collective-permute-done.3.refs_1_ = bf16[4,256,128]{2,1,0:T(8,128)(2,1)S(1)} collective-permute-done((bf16[4,256,128]{2,1,0:T(8,128)(2,1)S(1)}, bf16[4,256,128]{2,1,0:T(8,128)(2,1)S(1)}, u32[]{:S(2)}, u32[]{:S(2)}) %collective-permute-start.3) | collective-permute-done | bytes 262176 | tf_op jit(solution)/shard_map/ppermute | solution.py:349
  22.4 0.5 collective-permute-start.11
  22.9 1.0 %collective-permute-done.7.refs_7_ = bf16[4,256,128]{2,1,0:T(8,128)(2,1)S(1)} collective-permute-done((bf16[4,256,128]{2,1,0:T(8,128)(2,1)S(1)}, bf16[4,256,128]{2,1,0:T(8,128)(2,1)S(1)}, u32[]{:S(2)}, u32[]{:S(2)}) %collective-permute-start.7) | collective-permute-done | bytes 262176 | tf_op jit(solution)/shard_map/ppermute | solution.py:41
  24.3 7.8 %convolve.1 = (bf16[8,256,128]{2,1,0:T(8,128)(2,1)S(1)}, bf16[4,256,128]{2,1,0:T(8,128)(2,1)S(1)}, bf16[4,256,128]{2,1,0:T(8,128)(2,1)S(1)}, f32[4,256,128]{2,1,...) custom-call(s32[1,2,4]{2,1,0:T(2,128)S(1)} %copy-done.5, ...), custom_call_target="tpu_custom_call" | custom-call | flops 5000000000 | bytes 15000000 | tf_op jit(solution)/shard_map/convolve/pallas_call | solution.py:393
  32.7 1.6 %collective-permute-start.13 = (bf16[4,256,128]{2,1,0:T(8,128)(2,1)S(1)}, bf16[4,256,128]{2,1,0:T(8,128)(2,1)S(1)}, u32[]{:S(2)}, u32[]{:S(2)}) collective-permute-start(bf16[4,256,128]{2,1,0:T(8,128)(2,1)S(1)} %get-tuple-element.31), channel_id=1, source_target_pairs={{4,0},{8,4},{12,8},{28,12},{24,28},{20,24},{16,20},{0,16},{5,1},{9... | collective-permute-start | bytes 786440 | tf_op jit(solution)/shard_map/ppermute | solution.py:350
  34.3 0.4 collective-permute-start.15
  34.7 1.6 %collective-permute-start.16 = (bf16[4,256,128]{2,1,0:T(8,128)(2,1)S(1)}, bf16[4,256,128]{2,1,0:T(8,128)(2,1)S(1)}, u32[]{:S(2)}, u32[]{:S(2)}) collective-permute-start(bf16[4,256,128]{2,1,0:T(8,128)(2,1)S(1)} %get-tuple-element.38), channel_id=1, source_target_pairs={{4,0},{8,4},{12,8},{28,12},{24,28},{20,24},{16,20},{0,16},{5,1},{9... | collective-permute-start | bytes 786440 | tf_op jit(solution)/shard_map/ppermute | solution.py:350
  36.3 3.7 %score.1 = f32[8,256,128]{2,1,0:T(8,128)} custom-call(bf16[8,256,128]{2,1,0:T(8,128)(2,1)S(1)} %get-tuple-element.33.low_ref, bf16[8,256,128]{2,1,0:T(8,128)(2,1)S(1)} %collective-permute-done.14.other_ref, bf16[8,256,256]{2,1,0:T(8,128)(2,1)S(1)} %get-tuple-element.34.prow_ref, bf16[8,256,128]{2,1,0:T(8,128)(2,1)S(1)} %get-tuple-element.35.pcol_ref, ...), custom_call_target="tpu_custom_call" | custom-call | flops 5000000000 | bytes 15000000 | tf_op jit(solution)/shard_map/score/pallas_call | solution.py:420
  40.0 6.5 %collective-permute-done.15.first_ref = bf16[4,256,128]{2,1,0:T(8,128)(2,1)S(1)} collective-permute-done((bf16[4,256,128]{2,1,0:T(8,128)(2,1)S(1)}, bf16[4,256,128]{2,1,0:T(8,128)(2,1)S(1)}, u32[]{:S(2)}, u32[]{:S(2)}) %collective-permute-start.15) | collective-permute-done | bytes 262176 | tf_op jit(solution)/shard_map/ppermute | solution.py:349
  47.0 1.6 %collective-permute-start.17 = (bf16[4,256,128]{2,1,0:T(8,128)(2,1)S(1)}, bf16[4,256,128]{2,1,0:T(8,128)(2,1)S(1)}, u32[]{:S(2)}, u32[]{:S(2)}) collective-permute-start(bf16[4,256,128]{2,1,0:T(8,128)(2,1)S(1)} %merge.2), channel_id=1, source_target_pairs={{0,2},{2,0},{1,3},{3,1},{4,6},{6,4},{5,7},{7,5},{8,10},{10,8},{9,1... | collective-permute-start | bytes 786440 | tf_op jit(solution)/shard_map/ppermute | solution.py:41
  48.5 6.1 %collective-permute-done.17.refs_0_ = bf16[4,256,128]{2,1,0:T(8,128)(2,1)S(1)} collective-permute-done((bf16[4,256,128]{2,1,0:T(8,128)(2,1)S(1)}, bf16[4,256,128]{2,1,0:T(8,128)(2,1)S(1)}, u32[]{:S(2)}, u32[]{:S(2)}) %collective-permute-start.17) | collective-permute-done | bytes 262176 | tf_op jit(solution)/shard_map/ppermute | solution.py:41
  54.6 1.1 %merge.3 = f32[4,256,128]{2,1,0:T(8,128)} custom-call(f32[4,256,128]{2,1,0:T(8,128)S(1)} %get-tuple-element.29.here_ref, bf16[4,256,128]{2,1,0:T(8,128)(2,1)S(1)} %collective-permute-done.12.first_ref, bf16[4,256,128]{2,1,0:T(8,128)(2,1)S(1)} %collective-permute-done.13.last_ref, bf16[4,256,128]{2,1,0:T(8,128)(2,1)S(1)} %collective-permute-done.17.refs_0_), custom_call_target="tpu_custom_call" | custom-call | flops 500000000 | bytes 1500000 | tf_op jit(solution)/shard_map/merge/pallas_call | solution.py:434
  (32 shorter events, 1.6 us)
Async XLA Ops:
  0.6 13.8 %copy-start = (f32[1,2,4,256,128]{4,3,2,1,0:T(8,128)S(1)}, f32[1,2,4,256,128]{4,3,2,1,0:T(8,128)}, u32[]{:S(2)}) copy-start(f32[1,2,4,256,128]{4,3,2,1,0:T(8,128)} %param.9) | copy-start | bytes 3145732
  0.6 13.8 %collective-permute-start.1 = (f32[8,256,128]{2,1,0:T(8,128)}, f32[8,256,128]{2,1,0:T(8,128)S(1)}, u32[]{:S(2)}, u32[]{:S(2)}) collective-permute-start(f32[8,256,128]{2,1,0:T(8,128)} %bitcast.6), channel_id=1, source_target_pairs={{0,1},{1,0},{2,3},{3,2},{4,5},{5,4},{6,7},{7,6},{8,9},{9,8},{10,11... | collective-permute-start | bytes 3145736 | tf_op jit(solution)/shard_map/ppermute | solution.py:41
  1.2 12.7 %collective-permute-start.5 = (bf16[4,256,128]{2,1,0:T(8,128)(2,1)}, bf16[4,256,128]{2,1,0:T(8,128)(2,1)S(1)}, u32[]{:S(2)}, u32[]{:S(2)}) collective-permute-start(bf16[4,256,128]{2,1,0:T(8,128)(2,1)} %bitcast.9), channel_id=1, source_target_pairs={{4,0},{8,4},{12,8},{28,12},{24,28},{20,24},{16,20},{0,16},{5,1},{9... | collective-permute-start | bytes 786440 | tf_op jit(solution)/shard_map/ppermute | solution.py:350
  3.8 8.6 %collective-permute-start.2 = (bf16[4,256,128]{2,1,0:T(8,128)(2,1)}, bf16[4,256,128]{2,1,0:T(8,128)(2,1)S(1)}, u32[]{:S(2)}, u32[]{:S(2)}) collective-permute-start(bf16[4,256,128]{2,1,0:T(8,128)(2,1)} %bitcast.10), channel_id=1, source_target_pairs={{2,0},{0,2},{3,1},{1,3},{6,4},{4,6},{7,5},{5,7},{10,8},{8,10},{11,... | collective-permute-start | bytes 786440 | tf_op jit(solution)/shard_map/ppermute | solution.py:36
  5.3 13.3 %collective-permute-start = (bf16[4,256,128]{2,1,0:T(8,128)(2,1)}, bf16[4,256,128]{2,1,0:T(8,128)(2,1)S(1)}, u32[]{:S(2)}, u32[]{:S(2)}) collective-permute-start(bf16[4,256,128]{2,1,0:T(8,128)(2,1)} %bitcast.11), channel_id=1, source_target_pairs={{0,4},{4,8},{8,12},{12,28},{28,24},{24,20},{20,16},{16,0},{1,5},{5... | collective-permute-start | bytes 786440 | tf_op jit(solution)/shard_map/ppermute | solution.py:349
  6.5 8.0 %copy-start.4 = (f32[1,2,4,2]{2,3,1,0:T(2,128)S(1)}, f32[1,2,4,2]{2,3,1,0:T(2,128)}, u32[]{:S(2)}) copy-start(f32[1,2,4,2]{2,3,1,0:T(2,128)} %param.11) | copy-start | bytes 196
  6.5 8.0 %copy-start.6 = (s32[1,2]{1,0:T(1,128)S(1)}, s32[1,2]{1,0:T(1,128)}, u32[]{:S(2)}) copy-start(s32[1,2]{1,0:T(1,128)} %live_ref.3) | copy-start | bytes 28
  12.4 10.5 %collective-permute-start.9 = (bf16[4,256,128]{2,1,0:T(8,128)(2,1)S(1)}, bf16[4,256,128]{2,1,0:T(8,128)(2,1)S(1)}, u32[]{:S(2)}, u32[]{:S(2)}) collective-permute-start(bf16[4,256,128]{2,1,0:T(8,128)(2,1)S(1)} %collective-permute-done.2.refs_3_), channel_id=1, source_target_pairs={{0,1},{1,0},{2,3},{3,2},{4,5},{5,4},{6,7},{7,6},{8,9},{9,8},{10,11... | collective-permute-start | bytes 786440 | tf_op jit(solution)/shard_map/ppermute | solution.py:41
  12.4 8.7 %collective-permute-start.4 = (bf16[4,256,128]{2,1,0:T(8,128)(2,1)S(1)}, bf16[4,256,128]{2,1,0:T(8,128)(2,1)S(1)}, u32[]{:S(2)}, u32[]{:S(2)}) collective-permute-start(bf16[4,256,128]{2,1,0:T(8,128)(2,1)S(1)} %collective-permute-done.2.refs_3_), channel_id=1, source_target_pairs={{4,0},{8,4},{12,8},{28,12},{24,28},{20,24},{16,20},{0,16},{5,1},{9... | collective-permute-start | bytes 786440 | tf_op jit(solution)/shard_map/ppermute | solution.py:350
  13.9 8.4 %collective-permute-start.3 = (bf16[4,256,128]{2,1,0:T(8,128)(2,1)S(1)}, bf16[4,256,128]{2,1,0:T(8,128)(2,1)S(1)}, u32[]{:S(2)}, u32[]{:S(2)}) collective-permute-start(bf16[4,256,128]{2,1,0:T(8,128)(2,1)S(1)} %collective-permute-done.2.refs_3_), channel_id=1, source_target_pairs={{0,4},{4,8},{8,12},{12,28},{28,24},{24,20},{20,16},{16,0},{1,5},{5... | collective-permute-start | bytes 786440 | tf_op jit(solution)/shard_map/ppermute | solution.py:349
  14.4 8.0 %collective-permute-start.10 = (bf16[4,256,128]{2,1,0:T(8,128)(2,1)S(1)}, bf16[4,256,128]{2,1,0:T(8,128)(2,1)S(1)}, u32[]{:S(2)}, u32[]{:S(2)}) collective-permute-start(bf16[4,256,128]{2,1,0:T(8,128)(2,1)S(1)} %collective-permute-done.5.refs_4_), channel_id=1, source_target_pairs={{0,1},{1,0},{2,3},{3,2},{4,5},{5,4},{6,7},{7,6},{8,9},{9,8},{10,11... | collective-permute-start | bytes 786440 | tf_op jit(solution)/shard_map/ppermute | solution.py:41
  14.4 4.2 %copy-start.2 = (bf16[1,4,256,128]{3,2,1,0:T(8,128)(2,1)S(1)}, bf16[1,4,256,128]{3,2,1,0:T(8,128)(2,1)}, u32[]{:S(2)}) copy-start(bf16[1,4,256,128]{3,2,1,0:T(8,128)(2,1)} %param.7) | copy-start | bytes 786436
  14.4 9.9 %copy-start.1 = (bf16[1,2,4,256,128]{4,3,2,1,0:T(8,128)(2,1)S(1)}, bf16[1,2,4,256,128]{4,3,2,1,0:T(8,128)(2,1)}, u32[]{:S(2)}) copy-start(bf16[1,2,4,256,128]{4,3,2,1,0:T(8,128)(2,1)} %param.8) | copy-start | bytes 1572868
  14.4 9.8 %copy-start.5 = (s32[1,2,4]{2,1,0:T(2,128)S(1)}, s32[1,2,4]{2,1,0:T(2,128)}, u32[]{:S(2)}) copy-start(s32[1,2,4]{2,1,0:T(2,128)} %ids_ref.1) | copy-start | bytes 100
  18.6 4.3 %collective-permute-start.8 = (bf16[4,256,128]{2,1,0:T(8,128)(2,1)S(1)}, bf16[4,256,128]{2,1,0:T(8,128)(2,1)S(1)}, u32[]{:S(2)}, u32[]{:S(2)}) collective-permute-start(bf16[4,256,128]{2,1,0:T(8,128)(2,1)S(1)} %bitcast.12), channel_id=1, source_target_pairs={{0,1},{1,0},{2,3},{3,2},{4,5},{5,4},{6,7},{7,6},{8,9},{9,8},{10,11... | collective-permute-start | bytes 786440 | tf_op jit(solution)/shard_map/ppermute | solution.py:41
  21.1 1.8 %collective-permute-start.6 = (bf16[4,256,128]{2,1,0:T(8,128)(2,1)S(1)}, bf16[4,256,128]{2,1,0:T(8,128)(2,1)S(1)}, u32[]{:S(2)}, u32[]{:S(2)}) collective-permute-start(bf16[4,256,128]{2,1,0:T(8,128)(2,1)S(1)} %collective-permute-done.refs_0_), channel_id=1, source_target_pairs={{0,1},{1,0},{2,3},{3,2},{4,5},{5,4},{6,7},{7,6},{8,9},{9,8},{10,11... | collective-permute-start | bytes 786440 | tf_op jit(solution)/shard_map/ppermute | solution.py:41
  22.4 1.5 %collective-permute-start.7 = (bf16[4,256,128]{2,1,0:T(8,128)(2,1)S(1)}, bf16[4,256,128]{2,1,0:T(8,128)(2,1)S(1)}, u32[]{:S(2)}, u32[]{:S(2)}) collective-permute-start(bf16[4,256,128]{2,1,0:T(8,128)(2,1)S(1)} %collective-permute-done.3.refs_1_), channel_id=1, source_target_pairs={{0,1},{1,0},{2,3},{3,2},{4,5},{5,4},{6,7},{7,6},{8,9},{9,8},{10,11... | collective-permute-start | bytes 786440 | tf_op jit(solution)/shard_map/ppermute | solution.py:41
  22.4 1.9 %collective-permute-start.11 = (bf16[4,256,128]{2,1,0:T(8,128)(2,1)S(1)}, bf16[4,256,128]{2,1,0:T(8,128)(2,1)S(1)}, u32[]{:S(2)}, u32[]{:S(2)}) collective-permute-start(bf16[4,256,128]{2,1,0:T(8,128)(2,1)S(1)} %collective-permute-done.4.refs_5_), channel_id=1, source_target_pairs={{0,1},{1,0},{2,3},{3,2},{4,5},{5,4},{6,7},{7,6},{8,9},{9,8},{10,11... | collective-permute-start | bytes 786440 | tf_op jit(solution)/shard_map/ppermute | solution.py:41
  32.1 4.3 %collective-permute-start.14 = (bf16[8,256,128]{2,1,0:T(8,128)(2,1)S(1)}, bf16[8,256,128]{2,1,0:T(8,128)(2,1)S(1)}, u32[]{:S(2)}, u32[]{:S(2)}) collective-permute-start(bf16[8,256,128]{2,1,0:T(8,128)(2,1)S(1)} %get-tuple-element.33.low_ref), channel_id=1, source_target_pairs={{0,1},{1,0},{2,3},{3,2},{4,5},{5,4},{6,7},{7,6},{8,9},{9,8},{10,11... | collective-permute-start | bytes 1572872 | tf_op jit(solution)/shard_map/ppermute | solution.py:41
  32.3 16.3 %collective-permute-start.12 = (bf16[4,256,128]{2,1,0:T(8,128)(2,1)S(1)}, bf16[4,256,128]{2,1,0:T(8,128)(2,1)S(1)}, u32[]{:S(2)}, u32[]{:S(2)}) collective-permute-start(bf16[4,256,128]{2,1,0:T(8,128)(2,1)S(1)} %get-tuple-element.30), channel_id=1, source_target_pairs={{0,4},{4,8},{8,12},{12,28},{28,24},{24,20},{20,16},{16,0},{1,5},{5... | collective-permute-start | bytes 786440 | tf_op jit(solution)/shard_map/ppermute | solution.py:349
  32.7 15.8 %collective-permute-start.13 = (bf16[4,256,128]{2,1,0:T(8,128)(2,1)S(1)}, bf16[4,256,128]{2,1,0:T(8,128)(2,1)S(1)}, u32[]{:S(2)}, u32[]{:S(2)}) collective-permute-start(bf16[4,256,128]{2,1,0:T(8,128)(2,1)S(1)} %get-tuple-element.31), channel_id=1, source_target_pairs={{4,0},{8,4},{12,8},{28,12},{24,28},{20,24},{16,20},{0,16},{5,1},{9... | collective-permute-start | bytes 786440 | tf_op jit(solution)/shard_map/ppermute | solution.py:350
  34.3 12.2 %collective-permute-start.15 = (bf16[4,256,128]{2,1,0:T(8,128)(2,1)S(1)}, bf16[4,256,128]{2,1,0:T(8,128)(2,1)S(1)}, u32[]{:S(2)}, u32[]{:S(2)}) collective-permute-start(bf16[4,256,128]{2,1,0:T(8,128)(2,1)S(1)} %get-tuple-element.37), channel_id=1, source_target_pairs={{0,4},{4,8},{8,12},{12,28},{28,24},{24,20},{20,16},{16,0},{1,5},{5... | collective-permute-start | bytes 786440 | tf_op jit(solution)/shard_map/ppermute | solution.py:349
  34.7 11.9 %collective-permute-start.16 = (bf16[4,256,128]{2,1,0:T(8,128)(2,1)S(1)}, bf16[4,256,128]{2,1,0:T(8,128)(2,1)S(1)}, u32[]{:S(2)}, u32[]{:S(2)}) collective-permute-start(bf16[4,256,128]{2,1,0:T(8,128)(2,1)S(1)} %get-tuple-element.38), channel_id=1, source_target_pairs={{4,0},{8,4},{12,8},{28,12},{24,28},{20,24},{16,20},{0,16},{5,1},{9... | collective-permute-start | bytes 786440 | tf_op jit(solution)/shard_map/ppermute | solution.py:350
  47.0 7.6 %collective-permute-start.17 = (bf16[4,256,128]{2,1,0:T(8,128)(2,1)S(1)}, bf16[4,256,128]{2,1,0:T(8,128)(2,1)S(1)}, u32[]{:S(2)}, u32[]{:S(2)}) collective-permute-start(bf16[4,256,128]{2,1,0:T(8,128)(2,1)S(1)} %merge.2), channel_id=1, source_target_pairs={{0,2},{2,0},{1,3},{3,1},{4,6},{6,4},{5,7},{7,5},{8,10},{10,8},{9,1... | collective-permute-start | bytes 786440 | tf_op jit(solution)/shard_map/ppermute | solution.py:41
  (1 other events, 0.7 us)

commit v4 on v3

--- a/solution.py
+++ b/solution.py
@@ -110,7 +110,7 @@
             band_ref[t, (count - u) * cols : (count - u + 1) * cols, :] = full
         return carry
 
-    lax.fori_loop(0, tiles, one, 0)
+    lax.fori_loop(0, tiles, one, 0, unroll=tiles)
     band_ref[tiles, 0:cols, :] = jnp.zeros((cols, cols), jnp.bfloat16)
     band_ref[tiles, (count + 1) * cols :, :] = jnp.zeros((cols, cols), jnp.bfloat16)
     for u in range(count):
@@ -127,7 +127,7 @@
 
 
 def norms_kernel(width_ref, live_ref, own_ref, other_ref,
-                 norm_ref, inv_ref, prow_ref, pcol_ref, dist_ref, near_ref):
+                 norm_ref, prow_ref, pcol_ref, dist_ref, near_ref):
     tiles, size, cols = own_ref.shape
     wide = 2 * cols
     rows = lax.broadcasted_iota(jnp.int32, (size, size), 0)
@@ -155,7 +155,6 @@
     def one(t, carry):
         inv_own = 1.0 / own_ref[t]
         inv_other = jnp.where(keep, 1.0 / other_ref[t], 0.0)
-        inv_ref[t] = inv_own
         inv_low = jnp.concatenate([inv_own, inv_other], axis=1).astype(jnp.bfloat16)
         prow = table(jnp.full((8, 128), width_ref[0, t // slots, 0, t % slots], jnp.float32), dist_ref[...])
         prow_ref[t] = prow.astype(jnp.bfloat16)
@@ -168,25 +167,26 @@
         norm_ref[t] = alive(live_ref, t, slots) / jnp.sqrt(denom)
         return carry
 
-    lax.fori_loop(0, tiles, one, 0)
+    lax.fori_loop(0, tiles, one, 0, unroll=tiles)
 
 
 PAD = 16
 
 
-def convolve_kernel(blocks, closed, ids_ref, live_ref, *refs):
+def convolve_kernel(blocks, closed, pieces, ids_ref, live_ref, *refs):
     own_blocks = refs[:blocks]
     other_blocks = refs[blocks : 2 * blocks]
-    (band_ref, exp_ref, inv_ref) = refs[2 * blocks : 2 * blocks + 3]
+    (band_ref, exp_ref, var_ref) = refs[2 * blocks : 2 * blocks + 3]
     low_ref = refs[2 * blocks + 3]
-    out_refs = refs[2 * blocks + 4 : 3 * blocks + 4]
-    tile_ref, padded_ref, lhs_ref, edge_ref, conv_ref, acc_ref, sem = refs[3 * blocks + 4 :]
+    out_refs = refs[2 * blocks + 4 : 2 * blocks + 4 + len(pieces)]
+    tile_ref, padded_ref, lhs_ref, edge_ref, conv_ref, acc_ref = refs[2 * blocks + 4 + len(pieces) :]
     _, tiles, size, cols = tile_ref.shape
     owned = own_blocks[0].shape[0]
     group = cols // tiles
     count = 2 * HW + 2
     first = PAD - HW
     pairs = size // 2
+    side = padded_ref.shape[0]
 
     slots = ids_ref.shape[2]
     core = lax.axis_index("band")
@@ -205,64 +205,64 @@
         step = jnp.where(flip == 0, step, 2 - step)
         return step * columns + shift, column - owner * owned, jnp.where(inside, 1.0, 0.0)
 
-    def copies(t, b, slot=0):
-        return (
-            pltpu.make_async_copy(own_blocks[b].at[slot], tile_ref.at[0, t], sem.at[t, 0]),
-            pltpu.make_async_copy(other_blocks[b].at[slot], tile_ref.at[1, t], sem.at[t, 1]),
-        )
-
     for t in range(tiles):
         part, slot, _ = place(t)
         for b in range(blocks):
             @pl.when(part == b)
             def _(t=t, b=b, slot=slot):
-                for c in copies(t, b, slot):
-                    c.start()
+                tile_ref[0, t] = own_blocks[b][slot]
+                tile_ref[1, t] = other_blocks[b][slot]
 
     acc_ref[...] = jnp.zeros_like(acc_ref)
-    padded_ref[0:PAD, :] = jnp.zeros((PAD, cols), jnp.float32)
-    padded_ref[PAD + size :, :] = jnp.zeros((PAD, cols), jnp.float32)
-
-    def spread(which):
+    for n in range(side):
+        padded_ref[n, 0:PAD, :] = jnp.zeros((PAD, cols), jnp.float32)
+        padded_ref[n, PAD + size :, :] = jnp.zeros((PAD, cols), jnp.float32)
+
+    def build(n):
         for r in range(count):
-            lhs_ref[:, r * cols : (r + 1) * cols] = padded_ref[
-                pl.ds(first + r, pairs, stride=2), :
+            lhs_ref[n, :, r * cols : (r + 1) * cols] = padded_ref[
+                n, pl.ds(first + r, pairs, stride=2), :
             ].astype(jnp.bfloat16)
+
+    def spread(n, which):
         weights = jnp.concatenate(
             [band_ref[which, cols:, :], band_ref[which, : count * cols, :]], axis=1
         )
-        return jnp.dot(lhs_ref[...], weights, preferred_element_type=jnp.float32)
+        return jnp.dot(lhs_ref[n], weights, preferred_element_type=jnp.float32)
 
     lane = lax.broadcasted_iota(jnp.int32, (1, cols), 1)
     start = jnp.where(core == 0, 0, cols - group)
     target = cols - group - start
     strip = jnp.zeros((size, cols), jnp.float32)
     for t in range(tiles):
-        copies(t, 0)[1].wait()
         moved = pltpu.roll(tile_ref[1, t].astype(jnp.float32), lax.rem(t * group - start + cols, cols), 1)
         strip = jnp.where(lane // group == t, moved, strip)
-    padded_ref[PAD : PAD + size, :] = strip
-    edge_ref[...] = spread(tiles)
-
-    def one(t, carry):
-        copies(t, 0)[0].wait()
-        padded_ref[PAD : PAD + size, :] = tile_ref[0, t].astype(jnp.float32)
-        both = spread(t)
-        turn = lax.rem(target - t * group + cols, cols)
-        for s in range(2):
-            edge = pltpu.roll(edge_ref[:, s * cols : (s + 1) * cols], turn, 1)
-            edge = jnp.where((lane >= target) & (lane < target + group), edge, 0.0)
-            conv_ref[pl.ds(s, pairs, stride=2), :] = both[:, s * cols : (s + 1) * cols] + edge
-        part, slot, present = place(t)
-        convolved = conv_ref[...] * present
-        own = (exp_ref[t].astype(jnp.float32) - convolved) * inv_ref[t]
-        low_ref[t] = own.astype(jnp.bfloat16)
-        acc_ref[part * owned + slot] += alive(live_ref, t, slots) * own
+    padded_ref[0, PAD : PAD + size, :] = strip
+    build(0)
+    edge_ref[...] = spread(0, tiles)
+
+    def some(i, carry):
+        for n in range(side):
+            padded_ref[n, PAD : PAD + size, :] = tile_ref[0, i * side + n].astype(jnp.float32)
+            build(n)
+        both = [spread(n, i * side + n) for n in range(side)]
+        for n in range(side):
+            t = i * side + n
+            turn = lax.rem(target - t * group + cols, cols)
+            for s in range(2):
+                edge = pltpu.roll(edge_ref[:, s * cols : (s + 1) * cols], turn, 1)
+                edge = jnp.where((lane >= target) & (lane < target + group), edge, 0.0)
+                conv_ref[n, pl.ds(s, pairs, stride=2), :] = both[n][:, s * cols : (s + 1) * cols] + edge
+            part, slot, present = place(t)
+            convolved = conv_ref[n] * present
+            own = (exp_ref[t].astype(jnp.float32) - convolved) * (1.0 / var_ref[t])
+            low_ref[t] = own.astype(jnp.bfloat16)
+            acc_ref[part * owned + slot] += alive(live_ref, t, slots) * own
         return carry
 
-    lax.fori_loop(0, tiles, one, 0)
-    for b in range(blocks):
-        out_refs[b][...] = acc_ref[b * owned : (b + 1) * owned].astype(out_refs[b].dtype)
+    lax.fori_loop(0, tiles // side, some, 0)
+    for ref, (b, begin, end) in zip(out_refs, pieces):
+        ref[...] = acc_ref[b * owned + begin : b * owned + end].astype(ref.dtype)
 
 
 def score_kernel(low_ref, other_ref, prow_ref, pcol_ref, norm_ref, score_ref):
@@ -279,7 +279,7 @@
         score_ref[t] = numer * norm_ref[t]
         return carry
 
-    lax.fori_loop(0, tiles, one, 0)
+    lax.fori_loop(0, tiles, one, 0, unroll=tiles)
 
 
 def merge_kernel(closed, here_ref, first_ref, last_ref, *refs):
@@ -288,21 +288,31 @@
     flip = lax.rem(lax.axis_index("groups"), 2) if closed else 0
     has_first = jnp.where(flip == 0, row > 0, row < rows - 1)
     has_last = jnp.where(flip == 0, row < rows - 1, row > 0)
-    out_ref = refs[-1]
-    owned, size, _ = out_ref.shape
-    chunk = size // 4
-
-    def one(i, carry):
-        at = (i // 4, pl.ds(pl.multiple_of(i % 4 * chunk, chunk), chunk))
-        total = here_ref[at].astype(jnp.float32)
-        total = total + jnp.where(has_first, first_ref[at].astype(jnp.float32), 0.0)
-        total = total + jnp.where(has_last, last_ref[at].astype(jnp.float32), 0.0)
-        for ref in refs[:-1]:
-            total = total + ref[at].astype(jnp.float32)
-        out_ref[at] = total.astype(out_ref.dtype)
-        return carry
-
-    lax.fori_loop(0, owned * 4, one, 0)
+    out_ref, made_ref, sem = refs[-3:]
+    come = refs[:-3]
+    owned = here_ref.shape[0]
+    cuts = halves(owned)
+    moves = []
+    for patch in range(owned):
+        total = here_ref[patch].astype(jnp.float32)
+        total = total + jnp.where(has_first, first_ref[patch].astype(jnp.float32), 0.0)
+        total = total + jnp.where(has_last, last_ref[patch].astype(jnp.float32), 0.0)
+        for n, ref in enumerate(come):
+            begin, end = cuts[n % len(cuts)]
+            if begin <= patch < end:
+                total = total + ref[patch - begin].astype(jnp.float32)
+        if not come:
+            out_ref[patch] = total.astype(out_ref.dtype)
+        else:
+            made_ref[patch] = total
+            moves.append(pltpu.make_async_copy(made_ref.at[patch], out_ref.at[patch], sem.at[patch]))
+            moves[-1].start()
+    for move in moves:
+        move.wait()
+
+
+def halves(count):
+    return [(0, count // 2), (count // 2, count)] if count % 2 == 0 else [(0, count)]
 
 
 def shape(dims, dtype):
@@ -315,10 +325,6 @@
 
 def smem(count):
     return [pl.BlockSpec(memory_space=SMEM)] * count
-
-
-def anywhere(count):
-    return [pl.BlockSpec(memory_space=pl.ANY)] * count
 
 
 def params(mib):
@@ -369,54 +375,80 @@
     firsts += [ahead(row[d]) for d in range(1, across)]
     lasts += [behind(row[d]) for d in range(1, across)]
 
-    norm, inv, prow, pcol = pl.pallas_call(
+    norm, prow, pcol = pl.pallas_call(
         norms_kernel,
         name="norms",
         out_shape=(
-            shape((tiles, size, cols), f32),
             shape((tiles, size, cols), f32),
             shape((tiles, size, size), low),
             shape((tiles, 2 * cols, cols), low),
         ),
         in_specs=smem(2) + vmem(2),
-        out_specs=tuple(vmem(4)),
+        out_specs=tuple(vmem(3)),
         scratch_shapes=[VMEM((size, size), f32), VMEM((2 * cols, cols), f32)],
         compiler_params=params(6),
         cost_estimate=cost(5),
     )(jnp.swapaxes(psf_width, 2, 3), live_count, var_flat, var_other)
+    norm, firsts[1:], lasts[1:] = lax.optimization_barrier((norm, firsts[1:], lasts[1:]))
     early = [swap(b) for b in [firsts[0]] + row + [lasts[0]]]
-    inv, firsts[1:], lasts[1:] = lax.optimization_barrier((inv, firsts[1:], lasts[1:]))
     window = firsts + row + lasts
     window_other = early[:1] + [swap(b) for b in firsts[1:]] + early[1:-1]
     window_other = window_other + early[-1:] + [swap(b) for b in lasts[1:]]
 
+    side = 2 if tiles % 2 == 0 else 1
+    cuts = halves(owned)
+    pieces = [(b, 0, owned) for b in (0, across, 2 * across)]
+    pieces += [(n * across + d, *cut) for d in range(1, across) for cut in cuts for n in range(3)]
     outs = pl.pallas_call(
-        functools.partial(convolve_kernel, blocks, closed),
+        functools.partial(convolve_kernel, blocks, closed, pieces),
         name="convolve",
         out_shape=tuple(
             [shape((tiles, size, cols), low)]
-            + [shape((owned, size, cols), f32 if b == across else low) for b in range(blocks)]
+            + [shape((e - a, size, cols), f32 if b == across else low) for b, a, e in pieces]
         ),
-        in_specs=smem(2) + anywhere(2 * blocks) + vmem(3),
-        out_specs=tuple(vmem(1 + blocks)),
+        in_specs=smem(2) + vmem(2 * blocks + 3),
+        out_specs=tuple(vmem(1 + len(pieces))),
         scratch_shapes=[
             VMEM((2, tiles, size, cols), low),
-            VMEM((size + 2 * PAD, cols), f32),
-            VMEM((size // 2, (count + 1) * cols), low),
+            VMEM((side, size + 2 * PAD, cols), f32),
+            VMEM((side, size // 2, (count + 1) * cols), low),
             VMEM((size // 2, 2 * cols), f32),
-            VMEM((size, cols), f32),
+            VMEM((side, size, cols), f32),
             VMEM((blocks * owned, size, cols), f32),
-            pltpu.SemaphoreType.DMA((tiles, 2)),
         ],
         compiler_params=params(12),
         cost_estimate=cost(5),
-    )(patch_ids, live_count, *window, *window_other, band, exp_flat, inv)
+    )(patch_ids, live_count, *window, *window_other, band, exp_flat, var_flat)
     weighted_low = outs[0]
-    parts = outs[1:]
-
+    parts = dict(zip(pieces, outs[1:]))
+    whole = (0, owned)
     weighted_other = swap(weighted_low)
-    from_ahead = [ahead(parts[2 * across + d]) for d in range(across)]
-    from_behind = [behind(parts[d]) for d in range(across)]
+    from_ahead = ahead(parts[(2 * across, *whole)])
+    from_behind = behind(parts[(0, *whole)])
+
+    def merge(dtype, here, *arrays):
+        final = len(arrays) > 2
+        return pl.pallas_call(
+            functools.partial(merge_kernel, closed),
+            name="merge",
+            out_shape=shape(here.shape, dtype),
+            in_specs=vmem(1 + len(arrays)),
+            out_specs=pl.BlockSpec(memory_space=pl.ANY if final else VMEM),
+            scratch_shapes=[
+                VMEM(here.shape if final else (1, 8, 128), f32),
+                pltpu.SemaphoreType.DMA((here.shape[0],)),
+            ],
+            compiler_params=params(4),
+            cost_estimate=cost(0.5),
+        )(here, *arrays)
+
+    come = []
+    for d in range(1, across):
+        for cut in cuts:
+            merged = merge(
+                low, parts[(across + d, *cut)], ahead(parts[(2 * across + d, *cut)]), behind(parts[(d, *cut)])
+            )
+            come.append(sent(merged, "patch", d))
     score = pl.pallas_call(
         score_kernel,
         name="score",
@@ -426,26 +458,9 @@
         compiler_params=params(4),
         cost_estimate=cost(5),
     )(weighted_low, weighted_other, prow, pcol, norm)
-    score, from_ahead[1:], from_behind[1:] = lax.optimization_barrier(
-        (score, from_ahead[1:], from_behind[1:])
-    )
-
-    def merge(dtype, *arrays):
-        return pl.pallas_call(
-            functools.partial(merge_kernel, closed),
-            name="merge",
-            out_shape=shape((owned, size, cols), dtype),
-            in_specs=vmem(len(arrays)),
-            out_specs=vmem(1)[0],
-            compiler_params=params(2),
-            cost_estimate=cost(0.5),
-        )(*arrays)
-
-    come = []
-    for d in range(1, across):
-        merged = merge(low, parts[across + d], from_ahead[d], from_behind[d])
-        come.append(sent(merged, "patch", d))
-    total = merge(f32, parts[across], from_ahead[0], from_behind[0], *come)
+
+    score, come = lax.optimization_barrier((score, come))
+    total = merge(f32, parts[(across, *whole)], from_ahead, from_behind, *come)
     return (total.reshape(1, owned, size, cols), score.reshape(exposures.shape))
 
 

time: 55.9 us -> 46.9 us (0.84)
  Pallas kernels: 20.3 us -> 12.7 us
  waiting for transfers between devices: 19.9 us -> 15.9 us
  starting transfers between devices: 14 us -> 16.6 us
    ppermute x4 -> x5, waiting for transfers between devices: 7.77 us -> 4.28 us  [on_device(): ahead = lambda block: lax.ppermute(block, ('groups', 'exp'), forth)]
    ppermute x9 -> x10, waiting for transfers between devices: 7.45 us -> 4.39 us  [sent(): lax.ppermute(block, axis, [(i, (i + distance) % devices) for i in range(d...]
    pallas_call x1, Pallas kernels: 7.77 us -> 5 us  [on_device(): pl.pallas_call(functools.partial(convolve_kernel, blocks, closed, pieces)...]
    pallas_call x1, Pallas kernels: 4.12 us -> 2.19 us  [on_device(): pl.pallas_call(norms_kernel, name='norms', out_shape=(shape((tiles, size,...]
    ppermute x4 -> x5, waiting for transfers between devices: 2.1 us -> 3.86 us  [on_device(): behind = lambda block: lax.ppermute(block, ('groups', 'exp'), back)]
    pallas_call x1, Pallas kernels: 3.67 us -> 1.92 us  [on_device(): pl.pallas_call(score_kernel, name='score', out_shape=shape((tiles, size,...]
    ppermute x4 -> x5, starting transfers between devices: 7.3 us -> 8.86 us  [on_device(): behind = lambda block: lax.ppermute(block, ('groups', 'exp'), back)]
    ppermute x1, waiting for transfers between devices: 2.58 us -> 3.41 us  [fetched(): lax.ppermute(block, axis, [((i + distance) % devices, i) for i in range(d...]
  transfers between devices with their start and end apart: 18 -> 21, of which waited for: 8 -> 9; matrix products, arithmetic and copies ran while one was open for 0% -> 0% of each run, Pallas kernels for 20% -> 15%
where the time goes in v4:
time: 46.9 us; the launch traced here: 46.7 us
  starting transfers between devices  16.6 us (35%)
  waiting for transfers between devices  15.9 us (34%)
  Pallas kernels  12.7 us (27%)
  between operations  0.76 us (2%)
  local copies, waits for them, and re-layouts  0.72 us (2%)
    ppermute x5, starting transfers between devices, on_device(): behind = lambda block: lax.ppermute(block, ('groups', 'exp'), back)  8.86 us
    pallas_call x1, Pallas kernels, on_device(): pl.pallas_call(functools.partial(convolve_kernel, blocks, closed, pieces)...  5 us
    ppermute x10, waiting for transfers between devices, sent(): lax.ppermute(block, axis, [(i, (i + distance) % devices) for i in range(d...  4.39 us
    ppermute x5, waiting for transfers between devices, on_device(): ahead = lambda block: lax.ppermute(block, ('groups', 'exp'), forth)  4.28 us
    ppermute x10, starting transfers between devices, sent(): lax.ppermute(block, axis, [(i, (i + distance) % devices) for i in range(d...  3.92 us
    ppermute x5, waiting for transfers between devices, on_device(): behind = lambda block: lax.ppermute(block, ('groups', 'exp'), back)  3.86 us
    ppermute x1, waiting for transfers between devices, fetched(): lax.ppermute(block, axis, [((i + distance) % devices, i) for i in range(d...  3.41 us
    pallas_call x1, Pallas kernels, on_device(): pl.pallas_call(taps_kernel, name='taps', out_shape=shape((tiles + 1, (cou...  2.48 us
  transfers between devices with their start and end apart: 21, of which 9 were waited for; matrix products, arithmetic and copies ran while one was open for 0% of the time, Pallas kernels for 15%

profile of v4, /device:TPU:0, one launch (start us, length us, event | category | flops | bytes accessed | tf_op | source)
XLA Modules:
  0.0 46.7 jit_solution(2632225363197982699)
XLA Ops:
  0.6 0.6 %collective-permute-start.1 = (f32[8,256,128]{2,1,0:T(8,128)}, f32[8,256,128]{2,1,0:T(8,128)S(1)}, u32[]{:S(2)}, u32[]{:S(2)}) collective-permute-start(f32[8,256,128]{2,1,0:T(8,128)} %bitcast.6), channel_id=1, source_target_pairs={{0,1},{1,0},{2,3},{3,2},{4,5},{5,4},{6,7},{7,6},{8,9},{9,8},{10,11... | collective-permute-start | bytes 3145736 | tf_op jit(solution)/shard_map/ppermute | solution.py:41
  1.2 2.6 %collective-permute-start.5 = (bf16[4,256,128]{2,1,0:T(8,128)(2,1)}, bf16[4,256,128]{2,1,0:T(8,128)(2,1)S(1)}, u32[]{:S(2)}, u32[]{:S(2)}) collective-permute-start(bf16[4,256,128]{2,1,0:T(8,128)(2,1)} %bitcast.10), channel_id=1, source_target_pairs={{4,0},{8,4},{12,8},{28,12},{24,28},{20,24},{16,20},{0,16},{5,1},{9... | collective-permute-start | bytes 786440 | tf_op jit(solution)/shard_map/ppermute | solution.py:356
  3.8 1.5 %collective-permute-start.2 = (bf16[4,256,128]{2,1,0:T(8,128)(2,1)}, bf16[4,256,128]{2,1,0:T(8,128)(2,1)S(1)}, u32[]{:S(2)}, u32[]{:S(2)}) collective-permute-start(bf16[4,256,128]{2,1,0:T(8,128)(2,1)} %bitcast.11), channel_id=1, source_target_pairs={{2,0},{0,2},{3,1},{1,3},{6,4},{4,6},{7,5},{5,7},{10,8},{8,10},{11,... | collective-permute-start | bytes 786440 | tf_op jit(solution)/shard_map/ppermute | solution.py:36
  5.8 0.7 %copy-done.3 = f32[1,2,4,27]{3,2,1,0:T(4,128)S(1)} copy-done((f32[1,2,4,27]{3,2,1,0:T(4,128)S(1)}, f32[1,2,4,27]{3,2,1,0:T(4,128)}, u32[]{:S(2)}) %copy-start.3) | copy-done | bytes 888
  6.5 2.5 %taps.1.refs_12_ = bf16[9,2944,128]{2,1,0:T(8,128)(2,1)S(1)} custom-call(f32[1,2,4,27]{3,2,1,0:T(4,128)S(1)} %copy-done.3), custom_call_target="tpu_custom_call" | custom-call | flops 3000000000 | bytes 9000000 | tf_op jit(solution)/shard_map/taps/pallas_call | solution.py:364
  8.9 3.4 %collective-permute-done.2.refs_3_ = bf16[4,256,128]{2,1,0:T(8,128)(2,1)S(1)} collective-permute-done((bf16[4,256,128]{2,1,0:T(8,128)(2,1)}, bf16[4,256,128]{2,1,0:T(8,128)(2,1)S(1)}, u32[]{:S(2)}, u32[]{:S(2)}) %collective-permute-start.2) | collective-permute-done | bytes 262176 | tf_op jit(solution)/shard_map/ppermute | solution.py:36
  12.4 1.6 %collective-permute-start.4 = (bf16[4,256,128]{2,1,0:T(8,128)(2,1)S(1)}, bf16[4,256,128]{2,1,0:T(8,128)(2,1)S(1)}, u32[]{:S(2)}, u32[]{:S(2)}) collective-permute-start(bf16[4,256,128]{2,1,0:T(8,128)(2,1)S(1)} %collective-permute-done.2.refs_3_), channel_id=1, source_target_pairs={{4,0},{8,4},{12,8},{28,12},{24,28},{20,24},{16,20},{0,16},{5,1},{9... | collective-permute-start | bytes 786440 | tf_op jit(solution)/shard_map/ppermute | solution.py:356
  14.5 2.2 %norms.1 = (f32[8,256,128]{2,1,0:T(8,128)S(1)}, bf16[8,256,256]{2,1,0:T(8,128)(2,1)S(1)}, bf16[8,256,128]{2,1,0:T(8,128)(2,1)S(1)}) custom-call(f32[1,2,2,4]{3,2,1,0:T(2,128)S(1)} %bitcast.15, s32[1,2]{1,0:T(1,128)S(1)} %copy-done.6, f32[8,256,128]{2,1,0:T(8,128)S(1)} %bitcast.7, f32[8,256,128]{2,1,0:T(8,128)S(1)} %collective-permute-done.1.other_ref), custom_call_target="tpu_custom_call" | custom-call | flops 5000000000 | bytes 15000000 | tf_op jit(solution)/shard_map/norms/pallas_call | solution.py:378
  16.7 0.6 %collective-permute-start.8 = (bf16[4,256,128]{2,1,0:T(8,128)(2,1)S(1)}, bf16[4,256,128]{2,1,0:T(8,128)(2,1)S(1)}, u32[]{:S(2)}, u32[]{:S(2)}) collective-permute-start(bf16[4,256,128]{2,1,0:T(8,128)(2,1)S(1)} %bitcast.13), channel_id=1, source_target_pairs={{0,1},{1,0},{2,3},{3,2},{4,5},{5,4},{6,7},{7,6},{8,9},{9,8},{10,11... | collective-permute-start | bytes 786440 | tf_op jit(solution)/shard_map/ppermute | solution.py:41
  17.2 3.8 %collective-permute-done.4.refs_5_ = bf16[4,256,128]{2,1,0:T(8,128)(2,1)S(1)} collective-permute-done((bf16[4,256,128]{2,1,0:T(8,128)(2,1)S(1)}, bf16[4,256,128]{2,1,0:T(8,128)(2,1)S(1)}, u32[]{:S(2)}, u32[]{:S(2)}) %collective-permute-start.4) | collective-permute-done | bytes 262176 | tf_op jit(solution)/shard_map/ppermute | solution.py:356
  21.1 1.3 %collective-permute-done.3.refs_1_ = bf16[4,256,128]{2,1,0:T(8,128)(2,1)S(1)} collective-permute-done((bf16[4,256,128]{2,1,0:T(8,128)(2,1)S(1)}, bf16[4,256,128]{2,1,0:T(8,128)(2,1)S(1)}, u32[]{:S(2)}, u32[]{:S(2)}) %collective-permute-start.3) | collective-permute-done | bytes 262176 | tf_op jit(solution)/shard_map/ppermute | solution.py:355
  22.9 1.0 %collective-permute-done.7.refs_7_ = bf16[4,256,128]{2,1,0:T(8,128)(2,1)S(1)} collective-permute-done((bf16[4,256,128]{2,1,0:T(8,128)(2,1)S(1)}, bf16[4,256,128]{2,1,0:T(8,128)(2,1)S(1)}, u32[]{:S(2)}, u32[]{:S(2)}) %collective-permute-start.7) | collective-permute-done | bytes 262176 | tf_op jit(solution)/shard_map/ppermute | solution.py:41
  24.3 5.0 %convolve.1 = (bf16[8,256,128]{2,1,0:T(8,128)(2,1)S(1)}, bf16[4,256,128]{2,1,0:T(8,128)(2,1)S(1)}, f32[4,256,128]{2,1,0:T(8,128)S(1)}, bf16[4,256,128]{2,1,0:T(8...) custom-call(s32[1,2,4]{2,1,0:T(2,128)S(1)} %copy-done.5, ...), custom_call_target="tpu_custom_call" | custom-call | flops 5000000000 | bytes 15000000 | tf_op jit(solution)/shard_map/convolve/pallas_call | solution.py:402
  30.0 1.6 %collective-permute-start.16 = (bf16[2,256,128]{2,1,0:T(8,128)(2,1)S(1)}, bf16[2,256,128]{2,1,0:T(8,128)(2,1)S(1)}, u32[]{:S(2)}, u32[]{:S(2)}) collective-permute-start(bf16[2,256,128]{2,1,0:T(8,128)(2,1)S(1)} %get-tuple-element.39), channel_id=1, source_target_pairs={{4,0},{8,4},{12,8},{28,12},{24,28},{20,24},{16,20},{0,16},{5,1},{9... | collective-permute-start | bytes 393224 | tf_op jit(solution)/shard_map/ppermute | solution.py:356
  32.0 1.6 %collective-permute-start.19 = (bf16[2,256,128]{2,1,0:T(8,128)(2,1)S(1)}, bf16[2,256,128]{2,1,0:T(8,128)(2,1)S(1)}, u32[]{:S(2)}, u32[]{:S(2)}) collective-permute-start(bf16[2,256,128]{2,1,0:T(8,128)(2,1)S(1)} %get-tuple-element.42), channel_id=1, source_target_pairs={{4,0},{8,4},{12,8},{28,12},{24,28},{20,24},{16,20},{0,16},{5,1},{9... | collective-permute-start | bytes 393224 | tf_op jit(solution)/shard_map/ppermute | solution.py:356
  33.6 2.3 %collective-permute-done.15.first_ref = bf16[2,256,128]{2,1,0:T(8,128)(2,1)S(1)} collective-permute-done((bf16[2,256,128]{2,1,0:T(8,128)(2,1)S(1)}, bf16[2,256,128]{2,1,0:T(8,128)(2,1)S(1)}, u32[]{:S(2)}, u32[]{:S(2)}) %collective-permute-start.15) | collective-permute-done | bytes 131104 | tf_op jit(solution)/shard_map/ppermute | solution.py:355
  36.3 1.6 %collective-permute-start.13 = (bf16[4,256,128]{2,1,0:T(8,128)(2,1)S(1)}, bf16[4,256,128]{2,1,0:T(8,128)(2,1)S(1)}, u32[]{:S(2)}, u32[]{:S(2)}) collective-permute-start(bf16[4,256,128]{2,1,0:T(8,128)(2,1)S(1)} %get-tuple-element.32), channel_id=1, source_target_pairs={{4,0},{8,4},{12,8},{28,12},{24,28},{20,24},{16,20},{0,16},{5,1},{9... | collective-permute-start | bytes 786440 | tf_op jit(solution)/shard_map/ppermute | solution.py:356
  38.0 0.7 %collective-permute-done.18.first_ref = bf16[2,256,128]{2,1,0:T(8,128)(2,1)S(1)} collective-permute-done((bf16[2,256,128]{2,1,0:T(8,128)(2,1)S(1)}, bf16[2,256,128]{2,1,0:T(8,128)(2,1)S(1)}, u32[]{:S(2)}, u32[]{:S(2)}) %collective-permute-start.18) | collective-permute-done | bytes 131104 | tf_op jit(solution)/shard_map/ppermute | solution.py:355
  38.7 1.5 %collective-permute-start.17 = (bf16[2,256,128]{2,1,0:T(8,128)(2,1)S(1)}, bf16[2,256,128]{2,1,0:T(8,128)(2,1)S(1)}, u32[]{:S(2)}, u32[]{:S(2)}) collective-permute-start(bf16[2,256,128]{2,1,0:T(8,128)(2,1)S(1)} %merge.3), channel_id=1, source_target_pairs={{0,2},{2,0},{1,3},{3,1},{4,6},{6,4},{5,7},{7,5},{8,10},{10,8},{9,1... | collective-permute-start | bytes 393224 | tf_op jit(solution)/shard_map/ppermute | solution.py:41
  40.3 0.6 %collective-permute-start.20 = (bf16[2,256,128]{2,1,0:T(8,128)(2,1)S(1)}, bf16[2,256,128]{2,1,0:T(8,128)(2,1)S(1)}, u32[]{:S(2)}, u32[]{:S(2)}) collective-permute-start(bf16[2,256,128]{2,1,0:T(8,128)(2,1)S(1)} %merge.4), channel_id=1, source_target_pairs={{0,2},{2,0},{1,3},{3,1},{4,6},{6,4},{5,7},{7,5},{8,10},{10,8},{9,1... | collective-permute-start | bytes 393224 | tf_op jit(solution)/shard_map/ppermute | solution.py:41
  40.9 1.9 %score.1 = f32[8,256,128]{2,1,0:T(8,128)} custom-call(bf16[8,256,128]{2,1,0:T(8,128)(2,1)S(1)} %get-tuple-element.33.low_ref, bf16[8,256,128]{2,1,0:T(8,128)(2,1)S(1)} %collective-permute-done.14.other_ref, bf16[8,256,256]{2,1,0:T(8,128)(2,1)S(1)} %get-tuple-element.34.prow_ref, bf16[8,256,128]{2,1,0:T(8,128)(2,1)S(1)} %get-tuple-element.35.pcol_ref, ...), custom_call_target="tpu_custom_call" | custom-call | flops 5000000000 | bytes 15000000 | tf_op jit(solution)/shard_map/score/pallas_call | solution.py:452
  42.8 1.6 %collective-permute-done.17.refs_0_ = bf16[2,256,128]{2,1,0:T(8,128)(2,1)S(1)} collective-permute-done((bf16[2,256,128]{2,1,0:T(8,128)(2,1)S(1)}, bf16[2,256,128]{2,1,0:T(8,128)(2,1)S(1)}, u32[]{:S(2)}, u32[]{:S(2)}) %collective-permute-start.17) | collective-permute-done | bytes 131104 | tf_op jit(solution)/shard_map/ppermute | solution.py:41
  44.4 1.4 %collective-permute-done.20.refs_1_ = bf16[2,256,128]{2,1,0:T(8,128)(2,1)S(1)} collective-permute-done((bf16[2,256,128]{2,1,0:T(8,128)(2,1)S(1)}, bf16[2,256,128]{2,1,0:T(8,128)(2,1)S(1)}, u32[]{:S(2)}, u32[]{:S(2)}) %collective-permute-start.20) | collective-permute-done | bytes 131104 | tf_op jit(solution)/shard_map/ppermute | solution.py:41
  45.8 0.9 %merge.5 = f32[4,256,128]{2,1,0:T(8,128)} custom-call(f32[4,256,128]{2,1,0:T(8,128)S(1)} %get-tuple-element.30.here_ref, bf16[4,256,128]{2,1,0:T(8,128)(2,1)S(1)} %collective-permute-done.12.first_ref, bf16[4,256,128]{2,1,0:T(8,128)(2,1)S(1)} %collective-permute-done.13.last_ref, bf16[2,256,128]{2,1,0:T(8,128)(2,1)S(1)} %collective-permute-done.17.refs_0_, ...), custom_call_target="tpu_custom_call" | custom-call | flops 500000000 | bytes 1500000 | tf_op jit(solution)/shard_map/merge/pallas_call | solution.py:431
  (39 shorter events, 3.7 us)
Async XLA Ops:
  0.6 13.8 %copy-start = (f32[1,2,4,256,128]{4,3,2,1,0:T(8,128)S(1)}, f32[1,2,4,256,128]{4,3,2,1,0:T(8,128)}, u32[]{:S(2)}) copy-start(f32[1,2,4,256,128]{4,3,2,1,0:T(8,128)} %param.9) | copy-start | bytes 3145732
  0.6 13.8 %collective-permute-start.1 = (f32[8,256,128]{2,1,0:T(8,128)}, f32[8,256,128]{2,1,0:T(8,128)S(1)}, u32[]{:S(2)}, u32[]{:S(2)}) collective-permute-start(f32[8,256,128]{2,1,0:T(8,128)} %bitcast.6), channel_id=1, source_target_pairs={{0,1},{1,0},{2,3},{3,2},{4,5},{5,4},{6,7},{7,6},{8,9},{9,8},{10,11... | collective-permute-start | bytes 3145736 | tf_op jit(solution)/shard_map/ppermute | solution.py:41
  1.2 12.7 %collective-permute-start.5 = (bf16[4,256,128]{2,1,0:T(8,128)(2,1)}, bf16[4,256,128]{2,1,0:T(8,128)(2,1)S(1)}, u32[]{:S(2)}, u32[]{:S(2)}) collective-permute-start(bf16[4,256,128]{2,1,0:T(8,128)(2,1)} %bitcast.10), channel_id=1, source_target_pairs={{4,0},{8,4},{12,8},{28,12},{24,28},{20,24},{16,20},{0,16},{5,1},{9... | collective-permute-start | bytes 786440 | tf_op jit(solution)/shard_map/ppermute | solution.py:356
  3.8 8.6 %collective-permute-start.2 = (bf16[4,256,128]{2,1,0:T(8,128)(2,1)}, bf16[4,256,128]{2,1,0:T(8,128)(2,1)S(1)}, u32[]{:S(2)}, u32[]{:S(2)}) collective-permute-start(bf16[4,256,128]{2,1,0:T(8,128)(2,1)} %bitcast.11), channel_id=1, source_target_pairs={{2,0},{0,2},{3,1},{1,3},{6,4},{4,6},{7,5},{5,7},{10,8},{8,10},{11,... | collective-permute-start | bytes 786440 | tf_op jit(solution)/shard_map/ppermute | solution.py:36
  5.3 11.4 %collective-permute-start = (bf16[4,256,128]{2,1,0:T(8,128)(2,1)}, bf16[4,256,128]{2,1,0:T(8,128)(2,1)S(1)}, u32[]{:S(2)}, u32[]{:S(2)}) collective-permute-start(bf16[4,256,128]{2,1,0:T(8,128)(2,1)} %bitcast.12), channel_id=1, source_target_pairs={{0,4},{4,8},{8,12},{12,28},{28,24},{24,20},{20,16},{16,0},{1,5},{5... | collective-permute-start | bytes 786440 | tf_op jit(solution)/shard_map/ppermute | solution.py:355
  12.4 10.5 %collective-permute-start.9 = (bf16[4,256,128]{2,1,0:T(8,128)(2,1)S(1)}, bf16[4,256,128]{2,1,0:T(8,128)(2,1)S(1)}, u32[]{:S(2)}, u32[]{:S(2)}) collective-permute-start(bf16[4,256,128]{2,1,0:T(8,128)(2,1)S(1)} %collective-permute-done.2.refs_3_), channel_id=1, source_target_pairs={{0,1},{1,0},{2,3},{3,2},{4,5},{5,4},{6,7},{7,6},{8,9},{9,8},{10,11... | collective-permute-start | bytes 786440 | tf_op jit(solution)/shard_map/ppermute | solution.py:41
  12.4 8.7 %collective-permute-start.4 = (bf16[4,256,128]{2,1,0:T(8,128)(2,1)S(1)}, bf16[4,256,128]{2,1,0:T(8,128)(2,1)S(1)}, u32[]{:S(2)}, u32[]{:S(2)}) collective-permute-start(bf16[4,256,128]{2,1,0:T(8,128)(2,1)S(1)} %collective-permute-done.2.refs_3_), channel_id=1, source_target_pairs={{4,0},{8,4},{12,8},{28,12},{24,28},{20,24},{16,20},{0,16},{5,1},{9... | collective-permute-start | bytes 786440 | tf_op jit(solution)/shard_map/ppermute | solution.py:356
  13.9 8.4 %collective-permute-start.3 = (bf16[4,256,128]{2,1,0:T(8,128)(2,1)S(1)}, bf16[4,256,128]{2,1,0:T(8,128)(2,1)S(1)}, u32[]{:S(2)}, u32[]{:S(2)}) collective-permute-start(bf16[4,256,128]{2,1,0:T(8,128)(2,1)S(1)} %collective-permute-done.2.refs_3_), channel_id=1, source_target_pairs={{0,4},{4,8},{8,12},{12,28},{28,24},{24,20},{20,16},{16,0},{1,5},{5... | collective-permute-start | bytes 786440 | tf_op jit(solution)/shard_map/ppermute | solution.py:355
  14.4 8.0 %collective-permute-start.10 = (bf16[4,256,128]{2,1,0:T(8,128)(2,1)S(1)}, bf16[4,256,128]{2,1,0:T(8,128)(2,1)S(1)}, u32[]{:S(2)}, u32[]{:S(2)}) collective-permute-start(bf16[4,256,128]{2,1,0:T(8,128)(2,1)S(1)} %collective-permute-done.5.refs_4_), channel_id=1, source_target_pairs={{0,1},{1,0},{2,3},{3,2},{4,5},{5,4},{6,7},{7,6},{8,9},{9,8},{10,11... | collective-permute-start | bytes 786440 | tf_op jit(solution)/shard_map/ppermute | solution.py:41
  14.4 9.9 %copy-start.1 = (bf16[1,2,4,256,128]{4,3,2,1,0:T(8,128)(2,1)S(1)}, bf16[1,2,4,256,128]{4,3,2,1,0:T(8,128)(2,1)}, u32[]{:S(2)}) copy-start(bf16[1,2,4,256,128]{4,3,2,1,0:T(8,128)(2,1)} %param.8) | copy-start | bytes 1572868
  14.4 9.8 %copy-start.5 = (s32[1,2,4]{2,1,0:T(2,128)S(1)}, s32[1,2,4]{2,1,0:T(2,128)}, u32[]{:S(2)}) copy-start(s32[1,2,4]{2,1,0:T(2,128)} %ids_ref.1) | copy-start | bytes 100
  16.7 6.2 %collective-permute-start.8 = (bf16[4,256,128]{2,1,0:T(8,128)(2,1)S(1)}, bf16[4,256,128]{2,1,0:T(8,128)(2,1)S(1)}, u32[]{:S(2)}, u32[]{:S(2)}) collective-permute-start(bf16[4,256,128]{2,1,0:T(8,128)(2,1)S(1)} %bitcast.13), channel_id=1, source_target_pairs={{0,1},{1,0},{2,3},{3,2},{4,5},{5,4},{6,7},{7,6},{8,9},{9,8},{10,11... | collective-permute-start | bytes 786440 | tf_op jit(solution)/shard_map/ppermute | solution.py:41
  21.1 1.8 %collective-permute-start.6 = (bf16[4,256,128]{2,1,0:T(8,128)(2,1)S(1)}, bf16[4,256,128]{2,1,0:T(8,128)(2,1)S(1)}, u32[]{:S(2)}, u32[]{:S(2)}) collective-permute-start(bf16[4,256,128]{2,1,0:T(8,128)(2,1)S(1)} %collective-permute-done.refs_0_), channel_id=1, source_target_pairs={{0,1},{1,0},{2,3},{3,2},{4,5},{5,4},{6,7},{7,6},{8,9},{9,8},{10,11... | collective-permute-start | bytes 786440 | tf_op jit(solution)/shard_map/ppermute | solution.py:41
  22.4 1.5 %collective-permute-start.7 = (bf16[4,256,128]{2,1,0:T(8,128)(2,1)S(1)}, bf16[4,256,128]{2,1,0:T(8,128)(2,1)S(1)}, u32[]{:S(2)}, u32[]{:S(2)}) collective-permute-start(bf16[4,256,128]{2,1,0:T(8,128)(2,1)S(1)} %collective-permute-done.3.refs_1_), channel_id=1, source_target_pairs={{0,1},{1,0},{2,3},{3,2},{4,5},{5,4},{6,7},{7,6},{8,9},{9,8},{10,11... | collective-permute-start | bytes 786440 | tf_op jit(solution)/shard_map/ppermute | solution.py:41
  22.4 1.9 %collective-permute-start.11 = (bf16[4,256,128]{2,1,0:T(8,128)(2,1)S(1)}, bf16[4,256,128]{2,1,0:T(8,128)(2,1)S(1)}, u32[]{:S(2)}, u32[]{:S(2)}) collective-permute-start(bf16[4,256,128]{2,1,0:T(8,128)(2,1)S(1)} %collective-permute-done.4.refs_5_), channel_id=1, source_target_pairs={{0,1},{1,0},{2,3},{3,2},{4,5},{5,4},{6,7},{7,6},{8,9},{9,8},{10,11... | collective-permute-start | bytes 786440 | tf_op jit(solution)/shard_map/ppermute | solution.py:41
  29.3 11.6 %collective-permute-start.14 = (bf16[8,256,128]{2,1,0:T(8,128)(2,1)S(1)}, bf16[8,256,128]{2,1,0:T(8,128)(2,1)S(1)}, u32[]{:S(2)}, u32[]{:S(2)}) collective-permute-start(bf16[8,256,128]{2,1,0:T(8,128)(2,1)S(1)} %get-tuple-element.33.low_ref), channel_id=1, source_target_pairs={{0,1},{1,0},{2,3},{3,2},{4,5},{5,4},{6,7},{7,6},{8,9},{9,8},{10,11... | collective-permute-start | bytes 1572872 | tf_op jit(solution)/shard_map/ppermute | solution.py:41
  29.5 6.4 %collective-permute-start.15 = (bf16[2,256,128]{2,1,0:T(8,128)(2,1)S(1)}, bf16[2,256,128]{2,1,0:T(8,128)(2,1)S(1)}, u32[]{:S(2)}, u32[]{:S(2)}) collective-permute-start(bf16[2,256,128]{2,1,0:T(8,128)(2,1)S(1)} %get-tuple-element.38), channel_id=1, source_target_pairs={{0,4},{4,8},{8,12},{12,28},{28,24},{24,20},{20,16},{16,0},{1,5},{5... | collective-permute-start | bytes 393224 | tf_op jit(solution)/shard_map/ppermute | solution.py:355
  30.0 6.4 %collective-permute-start.16 = (bf16[2,256,128]{2,1,0:T(8,128)(2,1)S(1)}, bf16[2,256,128]{2,1,0:T(8,128)(2,1)S(1)}, u32[]{:S(2)}, u32[]{:S(2)}) collective-permute-start(bf16[2,256,128]{2,1,0:T(8,128)(2,1)S(1)} %get-tuple-element.39), channel_id=1, source_target_pairs={{4,0},{8,4},{12,8},{28,12},{24,28},{20,24},{16,20},{0,16},{5,1},{9... | collective-permute-start | bytes 393224 | tf_op jit(solution)/shard_map/ppermute | solution.py:356
  31.5 7.2 %collective-permute-start.18 = (bf16[2,256,128]{2,1,0:T(8,128)(2,1)S(1)}, bf16[2,256,128]{2,1,0:T(8,128)(2,1)S(1)}, u32[]{:S(2)}, u32[]{:S(2)}) collective-permute-start(bf16[2,256,128]{2,1,0:T(8,128)(2,1)S(1)} %get-tuple-element.41), channel_id=1, source_target_pairs={{0,4},{4,8},{8,12},{12,28},{28,24},{24,20},{20,16},{16,0},{1,5},{5... | collective-permute-start | bytes 393224 | tf_op jit(solution)/shard_map/ppermute | solution.py:355
  32.0 8.2 %collective-permute-start.19 = (bf16[2,256,128]{2,1,0:T(8,128)(2,1)S(1)}, bf16[2,256,128]{2,1,0:T(8,128)(2,1)S(1)}, u32[]{:S(2)}, u32[]{:S(2)}) collective-permute-start(bf16[2,256,128]{2,1,0:T(8,128)(2,1)S(1)} %get-tuple-element.42), channel_id=1, source_target_pairs={{4,0},{8,4},{12,8},{28,12},{24,28},{20,24},{16,20},{0,16},{5,1},{9... | collective-permute-start | bytes 393224 | tf_op jit(solution)/shard_map/ppermute | solution.py:356
  35.9 9.9 %collective-permute-start.12 = (bf16[4,256,128]{2,1,0:T(8,128)(2,1)S(1)}, bf16[4,256,128]{2,1,0:T(8,128)(2,1)S(1)}, u32[]{:S(2)}, u32[]{:S(2)}) collective-permute-start(bf16[4,256,128]{2,1,0:T(8,128)(2,1)S(1)} %get-tuple-element.31), channel_id=1, source_target_pairs={{0,4},{4,8},{8,12},{12,28},{28,24},{24,20},{20,16},{16,0},{1,5},{5... | collective-permute-start | bytes 786440 | tf_op jit(solution)/shard_map/ppermute | solution.py:355
  36.3 9.5 %collective-permute-start.13 = (bf16[4,256,128]{2,1,0:T(8,128)(2,1)S(1)}, bf16[4,256,128]{2,1,0:T(8,128)(2,1)S(1)}, u32[]{:S(2)}, u32[]{:S(2)}) collective-permute-start(bf16[4,256,128]{2,1,0:T(8,128)(2,1)S(1)} %get-tuple-element.32), channel_id=1, source_target_pairs={{4,0},{8,4},{12,8},{28,12},{24,28},{20,24},{16,20},{0,16},{5,1},{9... | collective-permute-start | bytes 786440 | tf_op jit(solution)/shard_map/ppermute | solution.py:356
  38.7 5.7 %collective-permute-start.17 = (bf16[2,256,128]{2,1,0:T(8,128)(2,1)S(1)}, bf16[2,256,128]{2,1,0:T(8,128)(2,1)S(1)}, u32[]{:S(2)}, u32[]{:S(2)}) collective-permute-start(bf16[2,256,128]{2,1,0:T(8,128)(2,1)S(1)} %merge.3), channel_id=1, source_target_pairs={{0,2},{2,0},{1,3},{3,1},{4,6},{6,4},{5,7},{7,5},{8,10},{10,8},{9,1... | collective-permute-start | bytes 393224 | tf_op jit(solution)/shard_map/ppermute | solution.py:41
  40.3 5.5 %collective-permute-start.20 = (bf16[2,256,128]{2,1,0:T(8,128)(2,1)S(1)}, bf16[2,256,128]{2,1,0:T(8,128)(2,1)S(1)}, u32[]{:S(2)}, u32[]{:S(2)}) collective-permute-start(bf16[2,256,128]{2,1,0:T(8,128)(2,1)S(1)} %merge.4), channel_id=1, source_target_pairs={{0,2},{2,0},{1,3},{3,1},{4,6},{6,4},{5,7},{7,5},{8,10},{10,8},{9,1... | collective-permute-start | bytes 393224 | tf_op jit(solution)/shard_map/ppermute | solution.py:41
  (4 other events, 18.8 us)

commit v5 on v4

--- a/solution.py
+++ b/solution.py
@@ -173,94 +173,131 @@
 PAD = 16
 
 
-def convolve_kernel(blocks, closed, pieces, ids_ref, live_ref, *refs):
-    own_blocks = refs[:blocks]
-    other_blocks = refs[blocks : 2 * blocks]
-    (band_ref, exp_ref, var_ref) = refs[2 * blocks : 2 * blocks + 3]
-    low_ref = refs[2 * blocks + 3]
-    out_refs = refs[2 * blocks + 4 : 2 * blocks + 4 + len(pieces)]
-    tile_ref, padded_ref, lhs_ref, edge_ref, conv_ref, acc_ref = refs[2 * blocks + 4 + len(pieces) :]
-    _, tiles, size, cols = tile_ref.shape
-    owned = own_blocks[0].shape[0]
-    group = cols // tiles
-    count = 2 * HW + 2
-    first = PAD - HW
-    pairs = size // 2
-    side = padded_ref.shape[0]
-
+def place(ids_ref, t, owned, closed):
     slots = ids_ref.shape[2]
-    core = lax.axis_index("band")
     row = lax.axis_index("exp")
     rows = lax.axis_size("exp")
     columns = lax.axis_size("patch")
     flip = lax.rem(lax.axis_index("groups"), 2) if closed else 0
-
-    def place(t):
-        name = ids_ref[0, t // slots, t % slots]
-        step = name // (owned * columns)
-        column = name - step * (owned * columns)
-        owner = column // owned
-        shift = lax.rem(owner - lax.axis_index("patch") + columns, columns)
-        inside = (row + step >= 1) & (row + step <= rows)
-        step = jnp.where(flip == 0, step, 2 - step)
-        return step * columns + shift, column - owner * owned, jnp.where(inside, 1.0, 0.0)
-
+    name = ids_ref[0, t // slots, t % slots]
+    step = name // (owned * columns)
+    column = name - step * (owned * columns)
+    owner = column // owned
+    shift = lax.rem(owner - lax.axis_index("patch") + columns, columns)
+    inside = (row + step >= 1) & (row + step <= rows)
+    step = jnp.where(flip == 0, step, 2 - step)
+    return step * columns + shift, column - owner * owned, jnp.where(inside, 1.0, 0.0)
+
+
+def clear_ends(padded_ref):
+    cols = padded_ref.shape[2]
+    for n in range(padded_ref.shape[0]):
+        padded_ref[n, 0:PAD, :] = jnp.zeros((PAD, cols), jnp.float32)
+        padded_ref[n, -PAD:, :] = jnp.zeros((PAD, cols), jnp.float32)
+
+
+def build(padded_ref, lhs_ref, n):
+    pairs = lhs_ref.shape[1]
+    cols = padded_ref.shape[2]
+    for r in range(2 * HW + 2):
+        lhs_ref[n, :, r * cols : (r + 1) * cols] = padded_ref[
+            n, pl.ds(PAD - HW + r, pairs, stride=2), :
+        ].astype(jnp.bfloat16)
+
+
+def spread(lhs_ref, band_ref, n, which):
+    cols = band_ref.shape[2]
+    count = 2 * HW + 2
+    weights = jnp.concatenate(
+        [band_ref[which, cols:, :], band_ref[which, : count * cols, :]], axis=1
+    )
+    return jnp.dot(lhs_ref[n], weights, preferred_element_type=jnp.float32)
+
+
+def multiply_kernel(members, closed, carried, ids_ref, *refs):
+    blocks = refs[: len(members)]
+    band_ref = refs[len(members)]
+    conv_ref, padded_ref, lhs_ref, list_ref = refs[len(members) + 1 + carried :]
+    tiles, size, cols = conv_ref.shape
+    owned = blocks[0].shape[0]
+    side, pairs, _ = lhs_ref.shape
+    clear_ends(padded_ref)
+
+    count = 0
     for t in range(tiles):
-        part, slot, _ = place(t)
+        part, _, _ = place(ids_ref, t, owned, closed)
+        here = functools.reduce(lambda a, b: a | b, [part == b for b in members])
+
+        @pl.when(here)
+        def _(t=t, count=count):
+            list_ref[count] = t
+
+        count = count + jnp.where(here, 1, 0)
+
+    def some(i, carry):
+        names = [list_ref[jnp.minimum(i * side + n, count - 1)] for n in range(side)]
+        for n, t in enumerate(names):
+            part, slot, _ = place(ids_ref, t, owned, closed)
+            for b, ref in zip(members, blocks):
+                @pl.when(part == b)
+                def _(n=n, ref=ref, slot=slot):
+                    padded_ref[n, PAD : PAD + size, :] = ref[slot].astype(jnp.float32)
+        for n in range(side):
+            build(padded_ref, lhs_ref, n)
+        both = [spread(lhs_ref, band_ref, n, t) for n, t in enumerate(names)]
+        for n, t in enumerate(names):
+            for s in range(2):
+                conv_ref[t, pl.ds(s, pairs, stride=2), :] = both[n][:, s * cols : (s + 1) * cols]
+        return carry
+
+    lax.fori_loop(0, (count + side - 1) // side, some, 0)
+
+
+def convolve_kernel(blocks, closed, pieces, ids_ref, live_ref, *refs):
+    other_blocks = refs[:blocks]
+    (conv_ref, band_ref, exp_ref, var_ref, low_ref) = refs[blocks : blocks + 5]
+    out_refs = refs[blocks + 5 : blocks + 5 + len(pieces)]
+    tile_ref, padded_ref, lhs_ref, edge_ref, acc_ref = refs[blocks + 5 + len(pieces) :]
+    tiles, size, cols = tile_ref.shape
+    owned = other_blocks[0].shape[0]
+    slots = ids_ref.shape[2]
+    group = cols // tiles
+    pairs = size // 2
+    core = lax.axis_index("band")
+
+    for t in range(tiles):
+        part, slot, _ = place(ids_ref, t, owned, closed)
         for b in range(blocks):
             @pl.when(part == b)
             def _(t=t, b=b, slot=slot):
-                tile_ref[0, t] = own_blocks[b][slot]
-                tile_ref[1, t] = other_blocks[b][slot]
+                tile_ref[t] = other_blocks[b][slot]
 
     acc_ref[...] = jnp.zeros_like(acc_ref)
-    for n in range(side):
-        padded_ref[n, 0:PAD, :] = jnp.zeros((PAD, cols), jnp.float32)
-        padded_ref[n, PAD + size :, :] = jnp.zeros((PAD, cols), jnp.float32)
-
-    def build(n):
-        for r in range(count):
-            lhs_ref[n, :, r * cols : (r + 1) * cols] = padded_ref[
-                n, pl.ds(first + r, pairs, stride=2), :
-            ].astype(jnp.bfloat16)
-
-    def spread(n, which):
-        weights = jnp.concatenate(
-            [band_ref[which, cols:, :], band_ref[which, : count * cols, :]], axis=1
-        )
-        return jnp.dot(lhs_ref[n], weights, preferred_element_type=jnp.float32)
-
+    clear_ends(padded_ref)
     lane = lax.broadcasted_iota(jnp.int32, (1, cols), 1)
     start = jnp.where(core == 0, 0, cols - group)
     target = cols - group - start
     strip = jnp.zeros((size, cols), jnp.float32)
     for t in range(tiles):
-        moved = pltpu.roll(tile_ref[1, t].astype(jnp.float32), lax.rem(t * group - start + cols, cols), 1)
+        moved = pltpu.roll(tile_ref[t].astype(jnp.float32), lax.rem(t * group - start + cols, cols), 1)
         strip = jnp.where(lane // group == t, moved, strip)
     padded_ref[0, PAD : PAD + size, :] = strip
-    build(0)
-    edge_ref[...] = spread(0, tiles)
-
-    def some(i, carry):
-        for n in range(side):
-            padded_ref[n, PAD : PAD + size, :] = tile_ref[0, i * side + n].astype(jnp.float32)
-            build(n)
-        both = [spread(n, i * side + n) for n in range(side)]
-        for n in range(side):
-            t = i * side + n
-            turn = lax.rem(target - t * group + cols, cols)
-            for s in range(2):
-                edge = pltpu.roll(edge_ref[:, s * cols : (s + 1) * cols], turn, 1)
-                edge = jnp.where((lane >= target) & (lane < target + group), edge, 0.0)
-                conv_ref[n, pl.ds(s, pairs, stride=2), :] = both[n][:, s * cols : (s + 1) * cols] + edge
-            part, slot, present = place(t)
-            convolved = conv_ref[n] * present
-            own = (exp_ref[t].astype(jnp.float32) - convolved) * (1.0 / var_ref[t])
-            low_ref[t] = own.astype(jnp.bfloat16)
-            acc_ref[part * owned + slot] += alive(live_ref, t, slots) * own
+    build(padded_ref, lhs_ref, 0)
+    both = spread(lhs_ref, band_ref, 0, tiles)
+    for s in range(2):
+        edge_ref[pl.ds(s, pairs, stride=2), :] = both[:, s * cols : (s + 1) * cols]
+
+    def one(t, carry):
+        edge = pltpu.roll(edge_ref[...], lax.rem(target - t * group + cols, cols), 1)
+        edge = jnp.where((lane >= target) & (lane < target + group), edge, 0.0)
+        part, slot, present = place(ids_ref, t, owned, closed)
+        convolved = (conv_ref[t] + edge) * present
+        own = (exp_ref[t].astype(jnp.float32) - convolved) * (1.0 / var_ref[t])
+        low_ref[t] = own.astype(jnp.bfloat16)
+        acc_ref[part * owned + slot] += alive(live_ref, t, slots) * own
         return carry
 
-    lax.fori_loop(0, tiles // side, some, 0)
+    lax.fori_loop(0, tiles, one, 0, unroll=2)
     for ref, (b, begin, end) in zip(out_refs, pieces):
         ref[...] = acc_ref[b * owned + begin : b * owned + end].astype(ref.dtype)
 
@@ -389,13 +426,37 @@
         compiler_params=params(6),
         cost_estimate=cost(5),
     )(jnp.swapaxes(psf_width, 2, 3), live_count, var_flat, var_other)
-    norm, firsts[1:], lasts[1:] = lax.optimization_barrier((norm, firsts[1:], lasts[1:]))
+    side = 2 if tiles % 2 == 0 else 1
+
+    def multiply(members, sources, *carried):
+        return pl.pallas_call(
+            functools.partial(multiply_kernel, members, closed, len(carried)),
+            name="multiply",
+            out_shape=shape((tiles, size, cols), f32),
+            in_specs=smem(1) + vmem(len(sources) + 1 + len(carried)),
+            out_specs=vmem(1)[0],
+            input_output_aliases={len(sources) + 2: 0} if carried else {},
+            scratch_shapes=[
+                VMEM((side, size + 2 * PAD, cols), f32),
+                VMEM((side, size // 2, (count + 1) * cols), low),
+                SMEM((tiles,), jnp.int32),
+            ],
+            compiler_params=params(8),
+            cost_estimate=cost(3),
+        )(patch_ids, *sources, band, *carried)
+
+    soon = [0] + list(range(across, 2 * across)) + [2 * across]
+    conv = multiply(soon, [firsts[0]] + row + [lasts[0]])
+    norm, conv, firsts[1:], lasts[1:] = lax.optimization_barrier(
+        (norm, conv, firsts[1:], lasts[1:])
+    )
     early = [swap(b) for b in [firsts[0]] + row + [lasts[0]]]
-    window = firsts + row + lasts
+    later = [b for b in range(blocks) if b not in soon]
+    if later:
+        conv = multiply(later, firsts[1:] + lasts[1:], conv)
     window_other = early[:1] + [swap(b) for b in firsts[1:]] + early[1:-1]
     window_other = window_other + early[-1:] + [swap(b) for b in lasts[1:]]
 
-    side = 2 if tiles % 2 == 0 else 1
     cuts = halves(owned)
     pieces = [(b, 0, owned) for b in (0, across, 2 * across)]
     pieces += [(n * across + d, *cut) for d in range(1, across) for cut in cuts for n in range(3)]
@@ -406,19 +467,18 @@
             [shape((tiles, size, cols), low)]
             + [shape((e - a, size, cols), f32 if b == across else low) for b, a, e in pieces]
         ),
-        in_specs=smem(2) + vmem(2 * blocks + 3),
+        in_specs=smem(2) + vmem(blocks + 4),
         out_specs=tuple(vmem(1 + len(pieces))),
         scratch_shapes=[
-            VMEM((2, tiles, size, cols), low),
-            VMEM((side, size + 2 * PAD, cols), f32),
-            VMEM((side, size // 2, (count + 1) * cols), low),
-            VMEM((size // 2, 2 * cols), f32),
-            VMEM((side, size, cols), f32),
+            VMEM((tiles, size, cols), low),
+            VMEM((1, size + 2 * PAD, cols), f32),
+            VMEM((1, size // 2, (count + 1) * cols), low),
+            VMEM((size, cols), f32),
             VMEM((blocks * owned, size, cols), f32),
         ],
         compiler_params=params(12),
         cost_estimate=cost(5),
-    )(patch_ids, live_count, *window, *window_other, band, exp_flat, var_flat)
+    )(patch_ids, live_count, *window_other, conv, band, exp_flat, var_flat)
     weighted_low = outs[0]
     parts = dict(zip(pieces, outs[1:]))
     whole = (0, owned)
@@ -446,7 +506,10 @@
     for d in range(1, across):
         for cut in cuts:
             merged = merge(
-                low, parts[(across + d, *cut)], ahead(parts[(2 * across + d, *cut)]), behind(parts[(d, *cut)])
+                low,
+                parts[(across + d, *cut)],
+                ahead(parts[(2 * across + d, *cut)]),
+                behind(parts[(d, *cut)]),
             )
             come.append(sent(merged, "patch", d))
     score = pl.pallas_call(

time: 46.9 us -> 45.6 us (0.972)
  waiting for transfers between devices: 15.9 us -> 11.9 us
  Pallas kernels: 12.7 us -> 15 us
    pallas_call x0 -> x2, Pallas kernels: none -> 4.77 us  [multiply(): pl.pallas_call(functools.partial(multiply_kernel, members, closed, len(ca...]
    ppermute x5, waiting for transfers between devices: 3.86 us -> 0.61 us  [on_device(): behind = lambda block: lax.ppermute(block, ('groups', 'exp'), back)]
    pallas_call x1, Pallas kernels: 5 us -> 2.54 us  [on_device(): pl.pallas_call(functools.partial(convolve_kernel, blocks, closed, pieces)...]
    ppermute x5, starting transfers between devices: 8.86 us -> 10.2 us  [on_device(): behind = lambda block: lax.ppermute(block, ('groups', 'exp'), back)]
    ppermute x5, starting transfers between devices: 2.32 us -> 1.5 us  [on_device(): ahead = lambda block: lax.ppermute(block, ('groups', 'exp'), forth)]
    ppermute x10, waiting for transfers between devices: 4.39 us -> 3.7 us  [sent(): lax.ppermute(block, axis, [(i, (i + distance) % devices) for i in range(d...]
  transfers between devices with their start and end apart: 21 -> 21, of which waited for: 9 -> 7; matrix products, arithmetic and copies ran while one was open for 0% -> 0% of each run, Pallas kernels for 15% -> 26%
where the time goes in v5:
time: 45.6 us; the launch traced here: 45.4 us
  starting transfers between devices  17 us (37%)
  Pallas kernels  15 us (33%)
  waiting for transfers between devices  11.9 us (26%)
  between operations  0.82 us (2%)
  local copies, waits for them, and re-layouts  0.72 us (2%)
    ppermute x5, starting transfers between devices, on_device(): behind = lambda block: lax.ppermute(block, ('groups', 'exp'), back)  10.2 us
    pallas_call x2, Pallas kernels, multiply(): pl.pallas_call(functools.partial(multiply_kernel, members, closed, len(ca...  4.77 us
    ppermute x5, waiting for transfers between devices, on_device(): ahead = lambda block: lax.ppermute(block, ('groups', 'exp'), forth)  4.17 us
    ppermute x10, starting transfers between devices, sent(): lax.ppermute(block, axis, [(i, (i + distance) % devices) for i in range(d...  3.8 us
    ppermute x10, waiting for transfers between devices, sent(): lax.ppermute(block, axis, [(i, (i + distance) % devices) for i in range(d...  3.7 us
    ppermute x1, waiting for transfers between devices, fetched(): lax.ppermute(block, axis, [((i + distance) % devices, i) for i in range(d...  3.37 us
    pallas_call x1, Pallas kernels, on_device(): pl.pallas_call(functools.partial(convolve_kernel, blocks, closed, pieces)...  2.54 us
    pallas_call x1, Pallas kernels, on_device(): pl.pallas_call(taps_kernel, name='taps', out_shape=shape((tiles + 1, (cou...  2.48 us
  transfers between devices with their start and end apart: 21, of which 7 were waited for; matrix products, arithmetic and copies ran while one was open for 0% of the time, Pallas kernels for 26%

profile of v5, /device:TPU:0, one launch (start us, length us, event | category | flops | bytes accessed | tf_op | source)
XLA Modules:
  0.0 45.4 jit_solution(6825778369544645391)
XLA Ops:
  1.2 2.6 %collective-permute-start.4 = (bf16[4,256,128]{2,1,0:T(8,128)(2,1)}, bf16[4,256,128]{2,1,0:T(8,128)(2,1)S(1)}, u32[]{:S(2)}, u32[]{:S(2)}) collective-permute-start(bf16[4,256,128]{2,1,0:T(8,128)(2,1)} %bitcast.10), channel_id=1, source_target_pairs={{4,0},{8,4},{12,8},{28,12},{24,28},{20,24},{16,20},{0,16},{5,1},{9... | collective-permute-start | bytes 786440 | tf_op jit(solution)/shard_map/ppermute | solution.py:393
  3.8 1.5 %collective-permute-start.3 = (bf16[4,256,128]{2,1,0:T(8,128)(2,1)}, bf16[4,256,128]{2,1,0:T(8,128)(2,1)S(1)}, u32[]{:S(2)}, u32[]{:S(2)}) collective-permute-start(bf16[4,256,128]{2,1,0:T(8,128)(2,1)} %bitcast.11), channel_id=1, source_target_pairs={{2,0},{0,2},{3,1},{1,3},{6,4},{4,6},{7,5},{5,7},{10,8},{8,10},{11,... | collective-permute-start | bytes 786440 | tf_op jit(solution)/shard_map/ppermute | solution.py:36
  5.8 0.7 %copy-done.3 = f32[1,2,4,27]{3,2,1,0:T(4,128)S(1)} copy-done((f32[1,2,4,27]{3,2,1,0:T(4,128)S(1)}, f32[1,2,4,27]{3,2,1,0:T(4,128)}, u32[]{:S(2)}) %copy-start.3) | copy-done | bytes 888
  6.5 2.5 %taps.1.refs_4_.refs_2_.refs_7_ = bf16[9,2944,128]{2,1,0:T(8,128)(2,1)S(1)} custom-call(f32[1,2,4,27]{3,2,1,0:T(4,128)S(1)} %copy-done.3), custom_call_target="tpu_custom_call" | custom-call | flops 3000000000 | bytes 9000000 | tf_op jit(solution)/shard_map/taps/pallas_call | solution.py:401
  9.0 3.4 %collective-permute-done.3.refs_2_ = bf16[4,256,128]{2,1,0:T(8,128)(2,1)S(1)} collective-permute-done((bf16[4,256,128]{2,1,0:T(8,128)(2,1)}, bf16[4,256,128]{2,1,0:T(8,128)(2,1)S(1)}, u32[]{:S(2)}, u32[]{:S(2)}) %collective-permute-start.3) | collective-permute-done | bytes 262176 | tf_op jit(solution)/shard_map/ppermute | solution.py:36
  12.4 1.6 %collective-permute-start.6 = (bf16[4,256,128]{2,1,0:T(8,128)(2,1)S(1)}, bf16[4,256,128]{2,1,0:T(8,128)(2,1)S(1)}, u32[]{:S(2)}, u32[]{:S(2)}) collective-permute-start(bf16[4,256,128]{2,1,0:T(8,128)(2,1)S(1)} %collective-permute-done.3.refs_2_), channel_id=1, source_target_pairs={{4,0},{8,4},{12,8},{28,12},{24,28},{20,24},{16,20},{0,16},{5,1},{9... | collective-permute-start | bytes 786440 | tf_op jit(solution)/shard_map/ppermute | solution.py:393
  14.4 3.3 %multiply.2.refs_3_ = f32[8,256,128]{2,1,0:T(8,128)S(1)} custom-call(s32[1,2,4]{2,1,0:T(2,128)S(1)} %copy-done.5, bf16[4,256,128]{2,1,0:T(8,128)(2,1)S(1)} %collective-permute-done.refs_0_, bf16[4,256,128]{2,1,0:T(8,128)(2,1)S(1)} %bitcast.14, bf16[4,256,128]{2,1,0:T(8,128)(2,1)S(1)} %collective-permute-done.3.refs_2_, ...), custom_call_target="tpu_custom_call" | custom-call | flops 3000000000 | bytes 9000000 | tf_op jit(solution)/shard_map/multiply/pallas_call | solution.py:432
  17.7 0.6 %collective-permute-start.10 = (bf16[4,256,128]{2,1,0:T(8,128)(2,1)S(1)}, bf16[4,256,128]{2,1,0:T(8,128)(2,1)S(1)}, u32[]{:S(2)}, u32[]{:S(2)}) collective-permute-start(bf16[4,256,128]{2,1,0:T(8,128)(2,1)S(1)} %collective-permute-done.4.refs_3_), channel_id=1, source_target_pairs={{0,1},{1,0},{2,3},{3,2},{4,5},{5,4},{6,7},{7,6},{8,9},{9,8},{10,11... | collective-permute-start | bytes 786440 | tf_op jit(solution)/shard_map/ppermute | solution.py:41
  18.2 2.2 %norms.1 = (f32[8,256,128]{2,1,0:T(8,128)S(1)}, bf16[8,256,256]{2,1,0:T(8,128)(2,1)S(1)}, bf16[8,256,128]{2,1,0:T(8,128)(2,1)S(1)}) custom-call(f32[1,2,2,4]{3,2,1,0:T(2,128)S(1)} %bitcast.15, s32[1,2]{1,0:T(1,128)S(1)} %copy-done.6, f32[8,256,128]{2,1,0:T(8,128)S(1)} %bitcast.7, f32[8,256,128]{2,1,0:T(8,128)S(1)} %collective-permute-done.2.other_ref), custom_call_target="tpu_custom_call" | custom-call | flops 5000000000 | bytes 15000000 | tf_op jit(solution)/shard_map/norms/pallas_call | solution.py:415
  20.5 0.6 %collective-permute-done.6.refs_1_ = bf16[4,256,128]{2,1,0:T(8,128)(2,1)S(1)} collective-permute-done((bf16[4,256,128]{2,1,0:T(8,128)(2,1)S(1)}, bf16[4,256,128]{2,1,0:T(8,128)(2,1)S(1)}, u32[]{:S(2)}, u32[]{:S(2)}) %collective-permute-start.6) | collective-permute-done | bytes 262176 | tf_op jit(solution)/shard_map/ppermute | solution.py:393
  21.1 1.3 %collective-permute-done.5.refs_0_ = bf16[4,256,128]{2,1,0:T(8,128)(2,1)S(1)} collective-permute-done((bf16[4,256,128]{2,1,0:T(8,128)(2,1)S(1)}, bf16[4,256,128]{2,1,0:T(8,128)(2,1)S(1)}, u32[]{:S(2)}, u32[]{:S(2)}) %collective-permute-start.5) | collective-permute-done | bytes 262176 | tf_op jit(solution)/shard_map/ppermute | solution.py:392
  22.9 1.5 %multiply.3.refs_6_ = f32[8,256,128]{2,1,0:T(8,128)S(1)} custom-call(s32[1,2,4]{2,1,0:T(2,128)S(1)} %copy-done.5, bf16[4,256,128]{2,1,0:T(8,128)(2,1)S(1)} %collective-permute-done.5.refs_0_, bf16[4,256,128]{2,1,0:T(8,128)(2,1)S(1)} %collective-permute-done.6.refs_1_, ...), custom_call_target="tpu_custom_call", output_to_operand_aliasing={{}: (4, {})} | custom-call | flops 3000000000 | bytes 9000000 | tf_op jit(solution)/shard_map/multiply/pallas_call | solution.py:432
  24.5 2.5 %convolve.1 = (bf16[8,256,128]{2,1,0:T(8,128)(2,1)S(1)}, bf16[4,256,128]{2,1,0:T(8,128)(2,1)S(1)}, f32[4,256,128]{2,1,0:T(8,128)S(1)}, bf16[4,256,128]{2,1,0:T(8...) custom-call(s32[1,2,4]{2,1,0:T(2,128)S(1)} %copy-done.5, ...), custom_call_target="tpu_custom_call" | custom-call | flops 5000000000 | bytes 15000000 | tf_op jit(solution)/shard_map/convolve/pallas_call | solution.py:463
  27.6 2.0 %collective-permute-start.16 = (bf16[2,256,128]{2,1,0:T(8,128)(2,1)S(1)}, bf16[2,256,128]{2,1,0:T(8,128)(2,1)S(1)}, u32[]{:S(2)}, u32[]{:S(2)}) collective-permute-start(bf16[2,256,128]{2,1,0:T(8,128)(2,1)S(1)} %get-tuple-element.41), channel_id=1, source_target_pairs={{4,0},{8,4},{12,8},{28,12},{24,28},{20,24},{16,20},{0,16},{5,1},{9... | collective-permute-start | bytes 393224 | tf_op jit(solution)/shard_map/ppermute | solution.py:393
  29.6 2.0 %collective-permute-start.19 = (bf16[2,256,128]{2,1,0:T(8,128)(2,1)S(1)}, bf16[2,256,128]{2,1,0:T(8,128)(2,1)S(1)}, u32[]{:S(2)}, u32[]{:S(2)}) collective-permute-start(bf16[2,256,128]{2,1,0:T(8,128)(2,1)S(1)} %get-tuple-element.44), channel_id=1, source_target_pairs={{4,0},{8,4},{12,8},{28,12},{24,28},{20,24},{16,20},{0,16},{5,1},{9... | collective-permute-start | bytes 393224 | tf_op jit(solution)/shard_map/ppermute | solution.py:393
  31.7 2.3 %collective-permute-done.15.first_ref = bf16[2,256,128]{2,1,0:T(8,128)(2,1)S(1)} collective-permute-done((bf16[2,256,128]{2,1,0:T(8,128)(2,1)S(1)}, bf16[2,256,128]{2,1,0:T(8,128)(2,1)S(1)}, u32[]{:S(2)}, u32[]{:S(2)}) %collective-permute-start.15) | collective-permute-done | bytes 131104 | tf_op jit(solution)/shard_map/ppermute | solution.py:392
  34.0 2.0 %collective-permute-start.13 = (bf16[4,256,128]{2,1,0:T(8,128)(2,1)S(1)}, bf16[4,256,128]{2,1,0:T(8,128)(2,1)S(1)}, u32[]{:S(2)}, u32[]{:S(2)}) collective-permute-start(bf16[4,256,128]{2,1,0:T(8,128)(2,1)S(1)} %get-tuple-element.34), channel_id=1, source_target_pairs={{4,0},{8,4},{12,8},{28,12},{24,28},{20,24},{16,20},{0,16},{5,1},{9... | collective-permute-start | bytes 786440 | tf_op jit(solution)/shard_map/ppermute | solution.py:393
  36.1 0.6 %collective-permute-done.18.first_ref = bf16[2,256,128]{2,1,0:T(8,128)(2,1)S(1)} collective-permute-done((bf16[2,256,128]{2,1,0:T(8,128)(2,1)S(1)}, bf16[2,256,128]{2,1,0:T(8,128)(2,1)S(1)}, u32[]{:S(2)}, u32[]{:S(2)}) %collective-permute-start.18) | collective-permute-done | bytes 131104 | tf_op jit(solution)/shard_map/ppermute | solution.py:392
  36.7 0.6 %collective-permute-start.17 = (bf16[2,256,128]{2,1,0:T(8,128)(2,1)S(1)}, bf16[2,256,128]{2,1,0:T(8,128)(2,1)S(1)}, u32[]{:S(2)}, u32[]{:S(2)}) collective-permute-start(bf16[2,256,128]{2,1,0:T(8,128)(2,1)S(1)} %merge.3), channel_id=1, source_target_pairs={{0,2},{2,0},{1,3},{3,1},{4,6},{6,4},{5,7},{7,5},{8,10},{10,8},{9,1... | collective-permute-start | bytes 393224 | tf_op jit(solution)/shard_map/ppermute | solution.py:41
  37.4 1.5 %collective-permute-start.20 = (bf16[2,256,128]{2,1,0:T(8,128)(2,1)S(1)}, bf16[2,256,128]{2,1,0:T(8,128)(2,1)S(1)}, u32[]{:S(2)}, u32[]{:S(2)}) collective-permute-start(bf16[2,256,128]{2,1,0:T(8,128)(2,1)S(1)} %merge.4), channel_id=1, source_target_pairs={{0,2},{2,0},{1,3},{3,1},{4,6},{6,4},{5,7},{7,5},{8,10},{10,8},{9,1... | collective-permute-start | bytes 393224 | tf_op jit(solution)/shard_map/ppermute | solution.py:41
  38.9 1.9 %score.1 = f32[8,256,128]{2,1,0:T(8,128)} custom-call(bf16[8,256,128]{2,1,0:T(8,128)(2,1)S(1)} %get-tuple-element.35.low_ref, bf16[8,256,128]{2,1,0:T(8,128)(2,1)S(1)} %collective-permute-done.14.other_ref, bf16[8,256,256]{2,1,0:T(8,128)(2,1)S(1)} %get-tuple-element.36.prow_ref, bf16[8,256,128]{2,1,0:T(8,128)(2,1)S(1)} %get-tuple-element.37.pcol_ref, ...), custom_call_target="tpu_custom_call" | custom-call | flops 5000000000 | bytes 15000000 | tf_op jit(solution)/shard_map/score/pallas_call | solution.py:515
  40.9 2.2 %collective-permute-done.17.refs_0_ = bf16[2,256,128]{2,1,0:T(8,128)(2,1)S(1)} collective-permute-done((bf16[2,256,128]{2,1,0:T(8,128)(2,1)S(1)}, bf16[2,256,128]{2,1,0:T(8,128)(2,1)S(1)}, u32[]{:S(2)}, u32[]{:S(2)}) %collective-permute-start.17) | collective-permute-done | bytes 131104 | tf_op jit(solution)/shard_map/ppermute | solution.py:41
  43.1 1.5 %collective-permute-done.20.refs_1_ = bf16[2,256,128]{2,1,0:T(8,128)(2,1)S(1)} collective-permute-done((bf16[2,256,128]{2,1,0:T(8,128)(2,1)S(1)}, bf16[2,256,128]{2,1,0:T(8,128)(2,1)S(1)}, u32[]{:S(2)}, u32[]{:S(2)}) %collective-permute-start.20) | collective-permute-done | bytes 131104 | tf_op jit(solution)/shard_map/ppermute | solution.py:41
  44.6 0.9 %merge.5 = f32[4,256,128]{2,1,0:T(8,128)} custom-call(f32[4,256,128]{2,1,0:T(8,128)S(1)} %get-tuple-element.32.here_ref, bf16[4,256,128]{2,1,0:T(8,128)(2,1)S(1)} %collective-permute-done.12.first_ref, bf16[4,256,128]{2,1,0:T(8,128)(2,1)S(1)} %collective-permute-done.13.last_ref, bf16[2,256,128]{2,1,0:T(8,128)(2,1)S(1)} %collective-permute-done.17.refs_0_, ...), custom_call_target="tpu_custom_call" | custom-call | flops 500000000 | bytes 1500000 | tf_op jit(solution)/shard_map/merge/pallas_call | solution.py:491
  (41 shorter events, 2.9 us)
Async XLA Ops:
  0.6 13.8 %copy-start.2 = (bf16[1,4,256,128]{3,2,1,0:T(8,128)(2,1)S(1)}, bf16[1,4,256,128]{3,2,1,0:T(8,128)(2,1)}, u32[]{:S(2)}) copy-start(bf16[1,4,256,128]{3,2,1,0:T(8,128)(2,1)} %param.7) | copy-start | bytes 786436
  0.6 17.0 %collective-permute-start.2 = (f32[8,256,128]{2,1,0:T(8,128)}, f32[8,256,128]{2,1,0:T(8,128)S(1)}, u32[]{:S(2)}, u32[]{:S(2)}) collective-permute-start(f32[8,256,128]{2,1,0:T(8,128)} %bitcast.6), channel_id=1, source_target_pairs={{0,1},{1,0},{2,3},{3,2},{4,5},{5,4},{6,7},{7,6},{8,9},{9,8},{10,11... | collective-permute-start | bytes 3145736 | tf_op jit(solution)/shard_map/ppermute | solution.py:41
  1.2 12.7 %collective-permute-start.4 = (bf16[4,256,128]{2,1,0:T(8,128)(2,1)}, bf16[4,256,128]{2,1,0:T(8,128)(2,1)S(1)}, u32[]{:S(2)}, u32[]{:S(2)}) collective-permute-start(bf16[4,256,128]{2,1,0:T(8,128)(2,1)} %bitcast.10), channel_id=1, source_target_pairs={{4,0},{8,4},{12,8},{28,12},{24,28},{20,24},{16,20},{0,16},{5,1},{9... | collective-permute-start | bytes 786440 | tf_op jit(solution)/shard_map/ppermute | solution.py:393
  3.8 8.6 %collective-permute-start.3 = (bf16[4,256,128]{2,1,0:T(8,128)(2,1)}, bf16[4,256,128]{2,1,0:T(8,128)(2,1)S(1)}, u32[]{:S(2)}, u32[]{:S(2)}) collective-permute-start(bf16[4,256,128]{2,1,0:T(8,128)(2,1)} %bitcast.11), channel_id=1, source_target_pairs={{2,0},{0,2},{3,1},{1,3},{6,4},{4,6},{7,5},{5,7},{10,8},{8,10},{11,... | collective-permute-start | bytes 786440 | tf_op jit(solution)/shard_map/ppermute | solution.py:36
  5.3 9.1 %collective-permute-start = (bf16[4,256,128]{2,1,0:T(8,128)(2,1)}, bf16[4,256,128]{2,1,0:T(8,128)(2,1)S(1)}, u32[]{:S(2)}, u32[]{:S(2)}) collective-permute-start(bf16[4,256,128]{2,1,0:T(8,128)(2,1)} %bitcast.12), channel_id=1, source_target_pairs={{0,4},{4,8},{8,12},{12,28},{28,24},{24,20},{20,16},{16,0},{1,5},{5... | collective-permute-start | bytes 786440 | tf_op jit(solution)/shard_map/ppermute | solution.py:392
  8.9 9.3 %copy-start = (f32[1,2,4,256,128]{4,3,2,1,0:T(8,128)S(1)}, f32[1,2,4,256,128]{4,3,2,1,0:T(8,128)}, u32[]{:S(2)}) copy-start(f32[1,2,4,256,128]{4,3,2,1,0:T(8,128)} %param.9) | copy-start | bytes 3145732
  9.0 9.3 %copy-start.4 = (f32[1,2,4,2]{2,3,1,0:T(2,128)S(1)}, f32[1,2,4,2]{2,3,1,0:T(2,128)}, u32[]{:S(2)}) copy-start(f32[1,2,4,2]{2,3,1,0:T(2,128)} %param.11) | copy-start | bytes 196
  12.4 12.1 %collective-permute-start.9 = (bf16[4,256,128]{2,1,0:T(8,128)(2,1)S(1)}, bf16[4,256,128]{2,1,0:T(8,128)(2,1)S(1)}, u32[]{:S(2)}, u32[]{:S(2)}) collective-permute-start(bf16[4,256,128]{2,1,0:T(8,128)(2,1)S(1)} %collective-permute-done.3.refs_2_), channel_id=1, source_target_pairs={{0,1},{1,0},{2,3},{3,2},{4,5},{5,4},{6,7},{7,6},{8,9},{9,8},{10,11... | collective-permute-start | bytes 786440 | tf_op jit(solution)/shard_map/ppermute | solution.py:41
  12.4 8.7 %collective-permute-start.6 = (bf16[4,256,128]{2,1,0:T(8,128)(2,1)S(1)}, bf16[4,256,128]{2,1,0:T(8,128)(2,1)S(1)}, u32[]{:S(2)}, u32[]{:S(2)}) collective-permute-start(bf16[4,256,128]{2,1,0:T(8,128)(2,1)S(1)} %collective-permute-done.3.refs_2_), channel_id=1, source_target_pairs={{4,0},{8,4},{12,8},{28,12},{24,28},{20,24},{16,20},{0,16},{5,1},{9... | collective-permute-start | bytes 786440 | tf_op jit(solution)/shard_map/ppermute | solution.py:393
  13.9 8.4 %collective-permute-start.5 = (bf16[4,256,128]{2,1,0:T(8,128)(2,1)S(1)}, bf16[4,256,128]{2,1,0:T(8,128)(2,1)S(1)}, u32[]{:S(2)}, u32[]{:S(2)}) collective-permute-start(bf16[4,256,128]{2,1,0:T(8,128)(2,1)S(1)} %collective-permute-done.3.refs_2_), channel_id=1, source_target_pairs={{0,4},{4,8},{8,12},{12,28},{28,24},{24,20},{20,16},{16,0},{1,5},{5... | collective-permute-start | bytes 786440 | tf_op jit(solution)/shard_map/ppermute | solution.py:392
  14.4 10.0 %collective-permute-start.8 = (bf16[4,256,128]{2,1,0:T(8,128)(2,1)S(1)}, bf16[4,256,128]{2,1,0:T(8,128)(2,1)S(1)}, u32[]{:S(2)}, u32[]{:S(2)}) collective-permute-start(bf16[4,256,128]{2,1,0:T(8,128)(2,1)S(1)} %bitcast.13), channel_id=1, source_target_pairs={{0,1},{1,0},{2,3},{3,2},{4,5},{5,4},{6,7},{7,6},{8,9},{9,8},{10,11... | collective-permute-start | bytes 786440 | tf_op jit(solution)/shard_map/ppermute | solution.py:41
  17.7 4.7 %collective-permute-start.10 = (bf16[4,256,128]{2,1,0:T(8,128)(2,1)S(1)}, bf16[4,256,128]{2,1,0:T(8,128)(2,1)S(1)}, u32[]{:S(2)}, u32[]{:S(2)}) collective-permute-start(bf16[4,256,128]{2,1,0:T(8,128)(2,1)S(1)} %collective-permute-done.4.refs_3_), channel_id=1, source_target_pairs={{0,1},{1,0},{2,3},{3,2},{4,5},{5,4},{6,7},{7,6},{8,9},{9,8},{10,11... | collective-permute-start | bytes 786440 | tf_op jit(solution)/shard_map/ppermute | solution.py:41
  21.1 3.3 %collective-permute-start.1 = (bf16[4,256,128]{2,1,0:T(8,128)(2,1)S(1)}, bf16[4,256,128]{2,1,0:T(8,128)(2,1)S(1)}, u32[]{:S(2)}, u32[]{:S(2)}) collective-permute-start(bf16[4,256,128]{2,1,0:T(8,128)(2,1)S(1)} %collective-permute-done.refs_0_), channel_id=1, source_target_pairs={{0,1},{1,0},{2,3},{3,2},{4,5},{5,4},{6,7},{7,6},{8,9},{9,8},{10,11... | collective-permute-start | bytes 786440 | tf_op jit(solution)/shard_map/ppermute | solution.py:41
  22.4 2.1 %collective-permute-start.7 = (bf16[4,256,128]{2,1,0:T(8,128)(2,1)S(1)}, bf16[4,256,128]{2,1,0:T(8,128)(2,1)S(1)}, u32[]{:S(2)}, u32[]{:S(2)}) collective-permute-start(bf16[4,256,128]{2,1,0:T(8,128)(2,1)S(1)} %collective-permute-done.5.refs_0_), channel_id=1, source_target_pairs={{0,1},{1,0},{2,3},{3,2},{4,5},{5,4},{6,7},{7,6},{8,9},{9,8},{10,11... | collective-permute-start | bytes 786440 | tf_op jit(solution)/shard_map/ppermute | solution.py:41
  22.4 2.1 %collective-permute-start.11 = (bf16[4,256,128]{2,1,0:T(8,128)(2,1)S(1)}, bf16[4,256,128]{2,1,0:T(8,128)(2,1)S(1)}, u32[]{:S(2)}, u32[]{:S(2)}) collective-permute-start(bf16[4,256,128]{2,1,0:T(8,128)(2,1)S(1)} %collective-permute-done.6.refs_1_), channel_id=1, source_target_pairs={{0,1},{1,0},{2,3},{3,2},{4,5},{5,4},{6,7},{7,6},{8,9},{9,8},{10,11... | collective-permute-start | bytes 786440 | tf_op jit(solution)/shard_map/ppermute | solution.py:41
  27.0 11.9 %collective-permute-start.14 = (bf16[8,256,128]{2,1,0:T(8,128)(2,1)S(1)}, bf16[8,256,128]{2,1,0:T(8,128)(2,1)S(1)}, u32[]{:S(2)}, u32[]{:S(2)}) collective-permute-start(bf16[8,256,128]{2,1,0:T(8,128)(2,1)S(1)} %get-tuple-element.35.low_ref), channel_id=1, source_target_pairs={{0,1},{1,0},{2,3},{3,2},{4,5},{5,4},{6,7},{7,6},{8,9},{9,8},{10,11... | collective-permute-start | bytes 1572872 | tf_op jit(solution)/shard_map/ppermute | solution.py:41
  27.1 6.8 %collective-permute-start.15 = (bf16[2,256,128]{2,1,0:T(8,128)(2,1)S(1)}, bf16[2,256,128]{2,1,0:T(8,128)(2,1)S(1)}, u32[]{:S(2)}, u32[]{:S(2)}) collective-permute-start(bf16[2,256,128]{2,1,0:T(8,128)(2,1)S(1)} %get-tuple-element.40), channel_id=1, source_target_pairs={{0,4},{4,8},{8,12},{12,28},{28,24},{24,20},{20,16},{16,0},{1,5},{5... | collective-permute-start | bytes 393224 | tf_op jit(solution)/shard_map/ppermute | solution.py:392
  27.6 6.4 %collective-permute-start.16 = (bf16[2,256,128]{2,1,0:T(8,128)(2,1)S(1)}, bf16[2,256,128]{2,1,0:T(8,128)(2,1)S(1)}, u32[]{:S(2)}, u32[]{:S(2)}) collective-permute-start(bf16[2,256,128]{2,1,0:T(8,128)(2,1)S(1)} %get-tuple-element.41), channel_id=1, source_target_pairs={{4,0},{8,4},{12,8},{28,12},{24,28},{20,24},{16,20},{0,16},{5,1},{9... | collective-permute-start | bytes 393224 | tf_op jit(solution)/shard_map/ppermute | solution.py:393
  29.6 7.1 %collective-permute-start.18 = (bf16[2,256,128]{2,1,0:T(8,128)(2,1)S(1)}, bf16[2,256,128]{2,1,0:T(8,128)(2,1)S(1)}, u32[]{:S(2)}, u32[]{:S(2)}) collective-permute-start(bf16[2,256,128]{2,1,0:T(8,128)(2,1)S(1)} %get-tuple-element.43), channel_id=1, source_target_pairs={{0,4},{4,8},{8,12},{12,28},{28,24},{24,20},{20,16},{16,0},{1,5},{5... | collective-permute-start | bytes 393224 | tf_op jit(solution)/shard_map/ppermute | solution.py:392
  29.6 7.7 %collective-permute-start.19 = (bf16[2,256,128]{2,1,0:T(8,128)(2,1)S(1)}, bf16[2,256,128]{2,1,0:T(8,128)(2,1)S(1)}, u32[]{:S(2)}, u32[]{:S(2)}) collective-permute-start(bf16[2,256,128]{2,1,0:T(8,128)(2,1)S(1)} %get-tuple-element.44), channel_id=1, source_target_pairs={{4,0},{8,4},{12,8},{28,12},{24,28},{20,24},{16,20},{0,16},{5,1},{9... | collective-permute-start | bytes 393224 | tf_op jit(solution)/shard_map/ppermute | solution.py:393
  33.9 10.6 %collective-permute-start.12 = (bf16[4,256,128]{2,1,0:T(8,128)(2,1)S(1)}, bf16[4,256,128]{2,1,0:T(8,128)(2,1)S(1)}, u32[]{:S(2)}, u32[]{:S(2)}) collective-permute-start(bf16[4,256,128]{2,1,0:T(8,128)(2,1)S(1)} %get-tuple-element.33), channel_id=1, source_target_pairs={{0,4},{4,8},{8,12},{12,28},{28,24},{24,20},{20,16},{16,0},{1,5},{5... | collective-permute-start | bytes 786440 | tf_op jit(solution)/shard_map/ppermute | solution.py:392
  34.0 10.6 %collective-permute-start.13 = (bf16[4,256,128]{2,1,0:T(8,128)(2,1)S(1)}, bf16[4,256,128]{2,1,0:T(8,128)(2,1)S(1)}, u32[]{:S(2)}, u32[]{:S(2)}) collective-permute-start(bf16[4,256,128]{2,1,0:T(8,128)(2,1)S(1)} %get-tuple-element.34), channel_id=1, source_target_pairs={{4,0},{8,4},{12,8},{28,12},{24,28},{20,24},{16,20},{0,16},{5,1},{9... | collective-permute-start | bytes 786440 | tf_op jit(solution)/shard_map/ppermute | solution.py:393
  36.7 6.4 %collective-permute-start.17 = (bf16[2,256,128]{2,1,0:T(8,128)(2,1)S(1)}, bf16[2,256,128]{2,1,0:T(8,128)(2,1)S(1)}, u32[]{:S(2)}, u32[]{:S(2)}) collective-permute-start(bf16[2,256,128]{2,1,0:T(8,128)(2,1)S(1)} %merge.3), channel_id=1, source_target_pairs={{0,2},{2,0},{1,3},{3,1},{4,6},{6,4},{5,7},{7,5},{8,10},{10,8},{9,1... | collective-permute-start | bytes 393224 | tf_op jit(solution)/shard_map/ppermute | solution.py:41
  37.4 7.1 %collective-permute-start.20 = (bf16[2,256,128]{2,1,0:T(8,128)(2,1)S(1)}, bf16[2,256,128]{2,1,0:T(8,128)(2,1)S(1)}, u32[]{:S(2)}, u32[]{:S(2)}) collective-permute-start(bf16[2,256,128]{2,1,0:T(8,128)(2,1)S(1)} %merge.4), channel_id=1, source_target_pairs={{0,2},{2,0},{1,3},{3,1},{4,6},{6,4},{5,7},{7,5},{8,10},{10,8},{9,1... | collective-permute-start | bytes 393224 | tf_op jit(solution)/shard_map/ppermute | solution.py:41
  (4 other events, 21.9 us)

commit v6 on v5

--- a/solution.py
+++ b/solution.py
@@ -126,42 +126,58 @@
     return jnp.where(t % slots < live_ref[0, t // slots], 1.0, 0.0)
 
 
-def norms_kernel(width_ref, live_ref, own_ref, other_ref,
-                 norm_ref, prow_ref, pcol_ref, dist_ref, near_ref):
+def norms_kernel(width_ref, live_ref, own_ref, other_ref, norm_ref, inv_ref, prow_ref, pcol_ref):
     tiles, size, cols = own_ref.shape
-    wide = 2 * cols
-    rows = lax.broadcasted_iota(jnp.int32, (size, size), 0)
-    across = lax.broadcasted_iota(jnp.int32, (size, size), 1)
-    gap = rows - across
-    dist_ref[...] = (gap * gap).astype(jnp.float32)
-    inner = lax.broadcasted_iota(jnp.int32, (wide, cols), 0)
-    outer = lax.broadcasted_iota(jnp.int32, (wide, cols), 1)
-    ring = jnp.abs(inner - outer)
-    ring = jnp.minimum(ring, wide - ring)
-    near_ref[...] = (ring * ring).astype(jnp.float32)
+    blocks = size // cols
     lane = lax.broadcasted_iota(jnp.int32, (size, cols), 1)
     keep = (lane >= cols // 2) == (lax.axis_index("band") == 1)
     slots = width_ref.shape[3]
-    limit = float(PW * PW)
+    down = lax.broadcasted_iota(jnp.int32, (cols, cols), 0)
+    across = lax.broadcasted_iota(jnp.int32, (cols, cols), 1)
+    gaps = (down - across, (down + cols - across)[:8], (down - cols - across)[-8:])
+    squares = [(gap * gap).astype(jnp.float32) for gap in gaps]
     spot = lax.broadcasted_iota(jnp.int32, (8, 128), 1)
     spot_low = spot.astype(jnp.float32) - PW
 
-    def table(width, square):
+    def table(width):
+        width = jnp.full((8, 128), width, jnp.float32)
         rate = -0.5 / (width * width)
         base = jnp.where(spot <= 2 * PW, jnp.exp(spot_low * spot_low * rate), 0.0)
         scale = 1.0 / jnp.sum(base[0:1], axis=1, keepdims=True)
-        return jnp.where(square <= limit, jnp.exp(square * rate[0:1, 0:1]) * scale, 0.0)
+        return [
+            jnp.where(square <= float(PW * PW), jnp.exp(square * rate[0:1, 0:1]) * scale, 0.0)
+            for square in squares
+        ]
+
+    def gap(rows):
+        return jnp.zeros((rows, cols), jnp.float32)
+
+    def row_matrix(main, low, high):
+        up = jnp.concatenate([gap(cols - 8), high], axis=0)
+        under = jnp.concatenate([low, gap(cols - 8)], axis=0)
+        choice = {0: main, 1: up, -1: under}
+        return jnp.concatenate(
+            [
+                jnp.concatenate([choice.get(b - a, gap(cols)) for b in range(blocks)], axis=1)
+                for a in range(blocks)
+            ],
+            axis=0,
+        ).astype(jnp.bfloat16)
+
+    def column_matrix(main, low, high):
+        return jnp.concatenate([main, low, gap(cols - 16), high], axis=0).astype(jnp.bfloat16)
 
     def one(t, carry):
         inv_own = 1.0 / own_ref[t]
+        inv_ref[t] = inv_own
         inv_other = jnp.where(keep, 1.0 / other_ref[t], 0.0)
         inv_low = jnp.concatenate([inv_own, inv_other], axis=1).astype(jnp.bfloat16)
-        prow = table(jnp.full((8, 128), width_ref[0, t // slots, 0, t % slots], jnp.float32), dist_ref[...])
-        prow_ref[t] = prow.astype(jnp.bfloat16)
-        qrow = (prow * prow).astype(jnp.bfloat16)
-        pcol = table(jnp.full((8, 128), width_ref[0, t // slots, 1, t % slots], jnp.float32), near_ref[...])
-        pcol_ref[t] = pcol.astype(jnp.bfloat16)
-        qcol = (pcol * pcol).astype(jnp.bfloat16)
+        prow = table(width_ref[0, t // slots, 0, t % slots])
+        pcol = table(width_ref[0, t // slots, 1, t % slots])
+        prow_ref[t] = row_matrix(*prow)
+        pcol_ref[t] = column_matrix(*pcol)
+        qrow = row_matrix(*[value * value for value in prow])
+        qcol = column_matrix(*[value * value for value in pcol])
         denom = jnp.dot(qrow, inv_low, preferred_element_type=jnp.float32).astype(jnp.bfloat16)
         denom = jnp.dot(denom, qcol, preferred_element_type=jnp.float32)
         norm_ref[t] = alive(live_ref, t, slots) / jnp.sqrt(denom)
@@ -255,7 +271,7 @@
 
 def convolve_kernel(blocks, closed, pieces, ids_ref, live_ref, *refs):
     other_blocks = refs[:blocks]
-    (conv_ref, band_ref, exp_ref, var_ref, low_ref) = refs[blocks : blocks + 5]
+    (conv_ref, band_ref, exp_ref, inv_ref, low_ref) = refs[blocks : blocks + 5]
     out_refs = refs[blocks + 5 : blocks + 5 + len(pieces)]
     tile_ref, padded_ref, lhs_ref, edge_ref, acc_ref = refs[blocks + 5 + len(pieces) :]
     tiles, size, cols = tile_ref.shape
@@ -292,12 +308,12 @@
         edge = jnp.where((lane >= target) & (lane < target + group), edge, 0.0)
         part, slot, present = place(ids_ref, t, owned, closed)
         convolved = (conv_ref[t] + edge) * present
-        own = (exp_ref[t].astype(jnp.float32) - convolved) * (1.0 / var_ref[t])
+        own = (exp_ref[t].astype(jnp.float32) - convolved) * inv_ref[t]
         low_ref[t] = own.astype(jnp.bfloat16)
         acc_ref[part * owned + slot] += alive(live_ref, t, slots) * own
         return carry
 
-    lax.fori_loop(0, tiles, one, 0, unroll=2)
+    lax.fori_loop(0, tiles, one, 0, unroll=8)
     for ref, (b, begin, end) in zip(out_refs, pieces):
         ref[...] = acc_ref[b * owned + begin : b * owned + end].astype(ref.dtype)
 
@@ -385,7 +401,7 @@
     exp_flat = exposures.reshape(-1, size, cols)
     var_flat = variance.reshape(-1, size, cols)
     tiles = exp_flat.shape[0]
-    assert cols % tiles == 0 and cols // tiles >= HW and size % 32 == 0
+    assert cols % tiles == 0 and cols // tiles >= HW and size % cols == 0 and PW < 8
     swap = functools.partial(sent, axis="band", distance=1)
 
     forth, back, closed = neighbours(lax.axis_size("groups"), lax.axis_size("exp"))
@@ -412,17 +428,17 @@
     firsts += [ahead(row[d]) for d in range(1, across)]
     lasts += [behind(row[d]) for d in range(1, across)]
 
-    norm, prow, pcol = pl.pallas_call(
+    norm, inv, prow, pcol = pl.pallas_call(
         norms_kernel,
         name="norms",
         out_shape=(
+            shape((tiles, size, cols), f32),
             shape((tiles, size, cols), f32),
             shape((tiles, size, size), low),
             shape((tiles, 2 * cols, cols), low),
         ),
         in_specs=smem(2) + vmem(2),
-        out_specs=tuple(vmem(3)),
-        scratch_shapes=[VMEM((size, size), f32), VMEM((2 * cols, cols), f32)],
+        out_specs=tuple(vmem(4)),
         compiler_params=params(6),
         cost_estimate=cost(5),
     )(jnp.swapaxes(psf_width, 2, 3), live_count, var_flat, var_other)
@@ -478,7 +494,7 @@
         ],
         compiler_params=params(12),
         cost_estimate=cost(5),
-    )(patch_ids, live_count, *window_other, conv, band, exp_flat, var_flat)
+    )(patch_ids, live_count, *window_other, conv, band, exp_flat, inv)
     weighted_low = outs[0]
     parts = dict(zip(pieces, outs[1:]))
     whole = (0, owned)

time: 45.6 us -> 45.4 us (level)
  Pallas kernels: 15 us -> 14.2 us
  waiting for transfers between devices: 11.9 us -> 12.4 us
    ppermute x5, waiting for transfers between devices: 0.61 us -> 1.19 us  [on_device(): behind = lambda block: lax.ppermute(block, ('groups', 'exp'), back)]
    pallas_call x1, Pallas kernels: 2.21 us -> 1.72 us  [on_device(): pl.pallas_call(norms_kernel, name='norms', out_shape=(shape((tiles, size,...]
  transfers between devices with their start and end apart: 21 -> 21, of which waited for: 7 -> 7; matrix products, arithmetic and copies ran while one was open for 0% -> 0% of each run, Pallas kernels for 26% -> 24%
where the time goes in v6:
time: 45.4 us; the launch traced here: 45.2 us
  starting transfers between devices  17 us (37%)
  Pallas kernels  14.2 us (31%)
  waiting for transfers between devices  12.4 us (27%)
  between operations  0.82 us (2%)
  local copies, waits for them, and re-layouts  0.72 us (2%)
    ppermute x5, starting transfers between devices, on_device(): behind = lambda block: lax.ppermute(block, ('groups', 'exp'), back)  10.1 us
    pallas_call x2, Pallas kernels, multiply(): pl.pallas_call(functools.partial(multiply_kernel, members, closed, len(ca...  4.65 us
    ppermute x5, waiting for transfers between devices, on_device(): ahead = lambda block: lax.ppermute(block, ('groups', 'exp'), forth)  4.17 us
    ppermute x10, starting transfers between devices, sent(): lax.ppermute(block, axis, [(i, (i + distance) % devices) for i in range(d...  3.8 us
    ppermute x10, waiting for transfers between devices, sent(): lax.ppermute(block, axis, [(i, (i + distance) % devices) for i in range(d...  3.71 us
    ppermute x1, waiting for transfers between devices, fetched(): lax.ppermute(block, axis, [((i + distance) % devices, i) for i in range(d...  3.37 us
    pallas_call x1, Pallas kernels, on_device(): pl.pallas_call(taps_kernel, name='taps', out_shape=shape((tiles + 1, (cou...  2.48 us
    pallas_call x1, Pallas kernels, on_device(): pl.pallas_call(functools.partial(convolve_kernel, blocks, closed, pieces)...  2.35 us
  transfers between devices with their start and end apart: 21, of which 7 were waited for; matrix products, arithmetic and copies ran while one was open for 0% of the time, Pallas kernels for 24%

profile of v6, /device:TPU:0, one launch (start us, length us, event | category | flops | bytes accessed | tf_op | source)
XLA Modules:
  0.0 45.2 jit_solution(1708699184029820901)
XLA Ops:
  1.2 2.6 %collective-permute-start.4 = (bf16[4,256,128]{2,1,0:T(8,128)(2,1)}, bf16[4,256,128]{2,1,0:T(8,128)(2,1)S(1)}, u32[]{:S(2)}, u32[]{:S(2)}) collective-permute-start(bf16[4,256,128]{2,1,0:T(8,128)(2,1)} %bitcast.9), channel_id=1, source_target_pairs={{4,0},{8,4},{12,8},{28,12},{24,28},{20,24},{16,20},{0,16},{5,1},{9... | collective-permute-start | bytes 786440 | tf_op jit(solution)/shard_map/ppermute | solution.py:409
  3.8 1.5 %collective-permute-start.3 = (bf16[4,256,128]{2,1,0:T(8,128)(2,1)}, bf16[4,256,128]{2,1,0:T(8,128)(2,1)S(1)}, u32[]{:S(2)}, u32[]{:S(2)}) collective-permute-start(bf16[4,256,128]{2,1,0:T(8,128)(2,1)} %bitcast.10), channel_id=1, source_target_pairs={{2,0},{0,2},{3,1},{1,3},{6,4},{4,6},{7,5},{5,7},{10,8},{8,10},{11,... | collective-permute-start | bytes 786440 | tf_op jit(solution)/shard_map/ppermute | solution.py:36
  5.8 0.7 %copy-done.3 = f32[1,2,4,27]{3,2,1,0:T(4,128)S(1)} copy-done((f32[1,2,4,27]{3,2,1,0:T(4,128)S(1)}, f32[1,2,4,27]{3,2,1,0:T(4,128)}, u32[]{:S(2)}) %copy-start.3) | copy-done | bytes 888
  6.5 2.5 %taps.1.refs_4_.refs_2_.refs_7_ = bf16[9,2944,128]{2,1,0:T(8,128)(2,1)S(1)} custom-call(f32[1,2,4,27]{3,2,1,0:T(4,128)S(1)} %copy-done.3), custom_call_target="tpu_custom_call" | custom-call | flops 3000000000 | bytes 9000000 | tf_op jit(solution)/shard_map/taps/pallas_call | solution.py:417
  9.0 3.4 %collective-permute-done.3.refs_2_ = bf16[4,256,128]{2,1,0:T(8,128)(2,1)S(1)} collective-permute-done((bf16[4,256,128]{2,1,0:T(8,128)(2,1)}, bf16[4,256,128]{2,1,0:T(8,128)(2,1)S(1)}, u32[]{:S(2)}, u32[]{:S(2)}) %collective-permute-start.3) | collective-permute-done | bytes 262176 | tf_op jit(solution)/shard_map/ppermute | solution.py:36
  12.4 1.6 %collective-permute-start.6 = (bf16[4,256,128]{2,1,0:T(8,128)(2,1)S(1)}, bf16[4,256,128]{2,1,0:T(8,128)(2,1)S(1)}, u32[]{:S(2)}, u32[]{:S(2)}) collective-permute-start(bf16[4,256,128]{2,1,0:T(8,128)(2,1)S(1)} %collective-permute-done.3.refs_2_), channel_id=1, source_target_pairs={{4,0},{8,4},{12,8},{28,12},{24,28},{20,24},{16,20},{0,16},{5,1},{9... | collective-permute-start | bytes 786440 | tf_op jit(solution)/shard_map/ppermute | solution.py:409
  14.4 3.2 %multiply.2.refs_3_ = f32[8,256,128]{2,1,0:T(8,128)S(1)} custom-call(s32[1,2,4]{2,1,0:T(2,128)S(1)} %copy-done.5, bf16[4,256,128]{2,1,0:T(8,128)(2,1)S(1)} %collective-permute-done.refs_0_, bf16[4,256,128]{2,1,0:T(8,128)(2,1)S(1)} %bitcast.13, bf16[4,256,128]{2,1,0:T(8,128)(2,1)S(1)} %collective-permute-done.3.refs_2_, ...), custom_call_target="tpu_custom_call" | custom-call | flops 3000000000 | bytes 9000000 | tf_op jit(solution)/shard_map/multiply/pallas_call | solution.py:448
  17.6 0.6 %collective-permute-start.10 = (bf16[4,256,128]{2,1,0:T(8,128)(2,1)S(1)}, bf16[4,256,128]{2,1,0:T(8,128)(2,1)S(1)}, u32[]{:S(2)}, u32[]{:S(2)}) collective-permute-start(bf16[4,256,128]{2,1,0:T(8,128)(2,1)S(1)} %collective-permute-done.4.refs_3_), channel_id=1, source_target_pairs={{0,1},{1,0},{2,3},{3,2},{4,5},{5,4},{6,7},{7,6},{8,9},{9,8},{10,11... | collective-permute-start | bytes 786440 | tf_op jit(solution)/shard_map/ppermute | solution.py:41
  18.2 1.7 %norms.1 = (f32[8,256,128]{2,1,0:T(8,128)S(1)}, f32[8,256,128]{2,1,0:T(8,128)S(1)}, bf16[8,256,256]{2,1,0:T(8,128)(2,1)S(1)}, bf16[8,256,128]{2,1,0:T(8,128)(2,1)S(1)}) custom-call(f32[1,2,2,4]{3,2,1,0:T(2,128)S(1)} %bitcast.14, s32[1,2]{1,0:T(1,128)S(1)} %copy-done.6, f32[8,256,128]{2,1,0:T(8,128)S(1)} %bitcast.7, ...), custom_call_target="tpu_custom_call" | custom-call | flops 5000000000 | bytes 15000000 | tf_op jit(solution)/shard_map/norms/pallas_call | solution.py:431
  19.9 1.2 %collective-permute-done.6.refs_1_ = bf16[4,256,128]{2,1,0:T(8,128)(2,1)S(1)} collective-permute-done((bf16[4,256,128]{2,1,0:T(8,128)(2,1)S(1)}, bf16[4,256,128]{2,1,0:T(8,128)(2,1)S(1)}, u32[]{:S(2)}, u32[]{:S(2)}) %collective-permute-start.6) | collective-permute-done | bytes 262176 | tf_op jit(solution)/shard_map/ppermute | solution.py:409
  21.1 1.3 %collective-permute-done.5.refs_0_ = bf16[4,256,128]{2,1,0:T(8,128)(2,1)S(1)} collective-permute-done((bf16[4,256,128]{2,1,0:T(8,128)(2,1)S(1)}, bf16[4,256,128]{2,1,0:T(8,128)(2,1)S(1)}, u32[]{:S(2)}, u32[]{:S(2)}) %collective-permute-start.5) | collective-permute-done | bytes 262176 | tf_op jit(solution)/shard_map/ppermute | solution.py:408
  22.9 1.5 %multiply.3.refs_6_ = f32[8,256,128]{2,1,0:T(8,128)S(1)} custom-call(s32[1,2,4]{2,1,0:T(2,128)S(1)} %copy-done.5, bf16[4,256,128]{2,1,0:T(8,128)(2,1)S(1)} %collective-permute-done.5.refs_0_, bf16[4,256,128]{2,1,0:T(8,128)(2,1)S(1)} %collective-permute-done.6.refs_1_, ...), custom_call_target="tpu_custom_call", output_to_operand_aliasing={{}: (4, {})} | custom-call | flops 3000000000 | bytes 9000000 | tf_op jit(solution)/shard_map/multiply/pallas_call | solution.py:448
  24.4 2.4 %convolve.1 = (bf16[8,256,128]{2,1,0:T(8,128)(2,1)S(1)}, bf16[4,256,128]{2,1,0:T(8,128)(2,1)S(1)}, f32[4,256,128]{2,1,0:T(8,128)S(1)}, bf16[4,256,128]{2,1,0:T(8...) custom-call(s32[1,2,4]{2,1,0:T(2,128)S(1)} %copy-done.5, ...), custom_call_target="tpu_custom_call" | custom-call | flops 5000000000 | bytes 15000000 | tf_op jit(solution)/shard_map/convolve/pallas_call | solution.py:479
  27.4 2.0 %collective-permute-start.16 = (bf16[2,256,128]{2,1,0:T(8,128)(2,1)S(1)}, bf16[2,256,128]{2,1,0:T(8,128)(2,1)S(1)}, u32[]{:S(2)}, u32[]{:S(2)}) collective-permute-start(bf16[2,256,128]{2,1,0:T(8,128)(2,1)S(1)} %get-tuple-element.43), channel_id=1, source_target_pairs={{4,0},{8,4},{12,8},{28,12},{24,28},{20,24},{16,20},{0,16},{5,1},{9... | collective-permute-start | bytes 393224 | tf_op jit(solution)/shard_map/ppermute | solution.py:409
  29.4 2.0 %collective-permute-start.19 = (bf16[2,256,128]{2,1,0:T(8,128)(2,1)S(1)}, bf16[2,256,128]{2,1,0:T(8,128)(2,1)S(1)}, u32[]{:S(2)}, u32[]{:S(2)}) collective-permute-start(bf16[2,256,128]{2,1,0:T(8,128)(2,1)S(1)} %get-tuple-element.46), channel_id=1, source_target_pairs={{4,0},{8,4},{12,8},{28,12},{24,28},{20,24},{16,20},{0,16},{5,1},{9... | collective-permute-start | bytes 393224 | tf_op jit(solution)/shard_map/ppermute | solution.py:409
  31.4 2.3 %collective-permute-done.15.first_ref = bf16[2,256,128]{2,1,0:T(8,128)(2,1)S(1)} collective-permute-done((bf16[2,256,128]{2,1,0:T(8,128)(2,1)S(1)}, bf16[2,256,128]{2,1,0:T(8,128)(2,1)S(1)}, u32[]{:S(2)}, u32[]{:S(2)}) %collective-permute-start.15) | collective-permute-done | bytes 131104 | tf_op jit(solution)/shard_map/ppermute | solution.py:408
  33.8 2.0 %collective-permute-start.13 = (bf16[4,256,128]{2,1,0:T(8,128)(2,1)S(1)}, bf16[4,256,128]{2,1,0:T(8,128)(2,1)S(1)}, u32[]{:S(2)}, u32[]{:S(2)}) collective-permute-start(bf16[4,256,128]{2,1,0:T(8,128)(2,1)S(1)} %get-tuple-element.36), channel_id=1, source_target_pairs={{4,0},{8,4},{12,8},{28,12},{24,28},{20,24},{16,20},{0,16},{5,1},{9... | collective-permute-start | bytes 786440 | tf_op jit(solution)/shard_map/ppermute | solution.py:409
  35.9 0.6 %collective-permute-done.18.first_ref = bf16[2,256,128]{2,1,0:T(8,128)(2,1)S(1)} collective-permute-done((bf16[2,256,128]{2,1,0:T(8,128)(2,1)S(1)}, bf16[2,256,128]{2,1,0:T(8,128)(2,1)S(1)}, u32[]{:S(2)}, u32[]{:S(2)}) %collective-permute-start.18) | collective-permute-done | bytes 131104 | tf_op jit(solution)/shard_map/ppermute | solution.py:408
  36.5 0.6 %collective-permute-start.17 = (bf16[2,256,128]{2,1,0:T(8,128)(2,1)S(1)}, bf16[2,256,128]{2,1,0:T(8,128)(2,1)S(1)}, u32[]{:S(2)}, u32[]{:S(2)}) collective-permute-start(bf16[2,256,128]{2,1,0:T(8,128)(2,1)S(1)} %merge.3), channel_id=1, source_target_pairs={{0,2},{2,0},{1,3},{3,1},{4,6},{6,4},{5,7},{7,5},{8,10},{10,8},{9,1... | collective-permute-start | bytes 393224 | tf_op jit(solution)/shard_map/ppermute | solution.py:41
  37.2 1.5 %collective-permute-start.20 = (bf16[2,256,128]{2,1,0:T(8,128)(2,1)S(1)}, bf16[2,256,128]{2,1,0:T(8,128)(2,1)S(1)}, u32[]{:S(2)}, u32[]{:S(2)}) collective-permute-start(bf16[2,256,128]{2,1,0:T(8,128)(2,1)S(1)} %merge.4), channel_id=1, source_target_pairs={{0,2},{2,0},{1,3},{3,1},{4,6},{6,4},{5,7},{7,5},{8,10},{10,8},{9,1... | collective-permute-start | bytes 393224 | tf_op jit(solution)/shard_map/ppermute | solution.py:41
  38.7 1.9 %score.1 = f32[8,256,128]{2,1,0:T(8,128)} custom-call(bf16[8,256,128]{2,1,0:T(8,128)(2,1)S(1)} %get-tuple-element.37.low_ref, bf16[8,256,128]{2,1,0:T(8,128)(2,1)S(1)} %collective-permute-done.14.other_ref, bf16[8,256,256]{2,1,0:T(8,128)(2,1)S(1)} %get-tuple-element.38.prow_ref, bf16[8,256,128]{2,1,0:T(8,128)(2,1)S(1)} %get-tuple-element.39.pcol_ref, ...), custom_call_target="tpu_custom_call" | custom-call | flops 5000000000 | bytes 15000000 | tf_op jit(solution)/shard_map/score/pallas_call | solution.py:531
  40.6 2.2 %collective-permute-done.17.refs_0_ = bf16[2,256,128]{2,1,0:T(8,128)(2,1)S(1)} collective-permute-done((bf16[2,256,128]{2,1,0:T(8,128)(2,1)S(1)}, bf16[2,256,128]{2,1,0:T(8,128)(2,1)S(1)}, u32[]{:S(2)}, u32[]{:S(2)}) %collective-permute-start.17) | collective-permute-done | bytes 131104 | tf_op jit(solution)/shard_map/ppermute | solution.py:41
  42.8 1.5 %collective-permute-done.20.refs_1_ = bf16[2,256,128]{2,1,0:T(8,128)(2,1)S(1)} collective-permute-done((bf16[2,256,128]{2,1,0:T(8,128)(2,1)S(1)}, bf16[2,256,128]{2,1,0:T(8,128)(2,1)S(1)}, u32[]{:S(2)}, u32[]{:S(2)}) %collective-permute-start.20) | collective-permute-done | bytes 131104 | tf_op jit(solution)/shard_map/ppermute | solution.py:41
  44.3 0.9 %merge.5 = f32[4,256,128]{2,1,0:T(8,128)} custom-call(f32[4,256,128]{2,1,0:T(8,128)S(1)} %get-tuple-element.34.here_ref, bf16[4,256,128]{2,1,0:T(8,128)(2,1)S(1)} %collective-permute-done.12.first_ref, bf16[4,256,128]{2,1,0:T(8,128)(2,1)S(1)} %collective-permute-done.13.last_ref, bf16[2,256,128]{2,1,0:T(8,128)(2,1)S(1)} %collective-permute-done.17.refs_0_, ...), custom_call_target="tpu_custom_call" | custom-call | flops 500000000 | bytes 1500000 | tf_op jit(solution)/shard_map/merge/pallas_call | solution.py:507
  (41 shorter events, 3.0 us)
Async XLA Ops:
  0.6 13.8 %copy-start.2 = (bf16[1,4,256,128]{3,2,1,0:T(8,128)(2,1)S(1)}, bf16[1,4,256,128]{3,2,1,0:T(8,128)(2,1)}, u32[]{:S(2)}) copy-start(bf16[1,4,256,128]{3,2,1,0:T(8,128)(2,1)} %param.7) | copy-start | bytes 786436
  0.6 16.9 %collective-permute-start.2 = (f32[8,256,128]{2,1,0:T(8,128)}, f32[8,256,128]{2,1,0:T(8,128)S(1)}, u32[]{:S(2)}, u32[]{:S(2)}) collective-permute-start(f32[8,256,128]{2,1,0:T(8,128)} %bitcast.6), channel_id=1, source_target_pairs={{0,1},{1,0},{2,3},{3,2},{4,5},{5,4},{6,7},{7,6},{8,9},{9,8},{10,11... | collective-permute-start | bytes 3145736 | tf_op jit(solution)/shard_map/ppermute | solution.py:41
  1.2 12.7 %collective-permute-start.4 = (bf16[4,256,128]{2,1,0:T(8,128)(2,1)}, bf16[4,256,128]{2,1,0:T(8,128)(2,1)S(1)}, u32[]{:S(2)}, u32[]{:S(2)}) collective-permute-start(bf16[4,256,128]{2,1,0:T(8,128)(2,1)} %bitcast.9), channel_id=1, source_target_pairs={{4,0},{8,4},{12,8},{28,12},{24,28},{20,24},{16,20},{0,16},{5,1},{9... | collective-permute-start | bytes 786440 | tf_op jit(solution)/shard_map/ppermute | solution.py:409
  3.8 8.6 %collective-permute-start.3 = (bf16[4,256,128]{2,1,0:T(8,128)(2,1)}, bf16[4,256,128]{2,1,0:T(8,128)(2,1)S(1)}, u32[]{:S(2)}, u32[]{:S(2)}) collective-permute-start(bf16[4,256,128]{2,1,0:T(8,128)(2,1)} %bitcast.10), channel_id=1, source_target_pairs={{2,0},{0,2},{3,1},{1,3},{6,4},{4,6},{7,5},{5,7},{10,8},{8,10},{11,... | collective-permute-start | bytes 786440 | tf_op jit(solution)/shard_map/ppermute | solution.py:36
  5.3 9.1 %collective-permute-start = (bf16[4,256,128]{2,1,0:T(8,128)(2,1)}, bf16[4,256,128]{2,1,0:T(8,128)(2,1)S(1)}, u32[]{:S(2)}, u32[]{:S(2)}) collective-permute-start(bf16[4,256,128]{2,1,0:T(8,128)(2,1)} %bitcast.11), channel_id=1, source_target_pairs={{0,4},{4,8},{8,12},{12,28},{28,24},{24,20},{20,16},{16,0},{1,5},{5... | collective-permute-start | bytes 786440 | tf_op jit(solution)/shard_map/ppermute | solution.py:408
  8.9 9.2 %copy-start = (f32[1,2,4,256,128]{4,3,2,1,0:T(8,128)S(1)}, f32[1,2,4,256,128]{4,3,2,1,0:T(8,128)}, u32[]{:S(2)}) copy-start(f32[1,2,4,256,128]{4,3,2,1,0:T(8,128)} %param.9) | copy-start | bytes 3145732
  9.0 9.2 %copy-start.4 = (f32[1,2,4,2]{2,3,1,0:T(2,128)S(1)}, f32[1,2,4,2]{2,3,1,0:T(2,128)}, u32[]{:S(2)}) copy-start(f32[1,2,4,2]{2,3,1,0:T(2,128)} %param.11) | copy-start | bytes 196
  12.4 12.1 %collective-permute-start.9 = (bf16[4,256,128]{2,1,0:T(8,128)(2,1)S(1)}, bf16[4,256,128]{2,1,0:T(8,128)(2,1)S(1)}, u32[]{:S(2)}, u32[]{:S(2)}) collective-permute-start(bf16[4,256,128]{2,1,0:T(8,128)(2,1)S(1)} %collective-permute-done.3.refs_2_), channel_id=1, source_target_pairs={{0,1},{1,0},{2,3},{3,2},{4,5},{5,4},{6,7},{7,6},{8,9},{9,8},{10,11... | collective-permute-start | bytes 786440 | tf_op jit(solution)/shard_map/ppermute | solution.py:41
  12.4 8.7 %collective-permute-start.6 = (bf16[4,256,128]{2,1,0:T(8,128)(2,1)S(1)}, bf16[4,256,128]{2,1,0:T(8,128)(2,1)S(1)}, u32[]{:S(2)}, u32[]{:S(2)}) collective-permute-start(bf16[4,256,128]{2,1,0:T(8,128)(2,1)S(1)} %collective-permute-done.3.refs_2_), channel_id=1, source_target_pairs={{4,0},{8,4},{12,8},{28,12},{24,28},{20,24},{16,20},{0,16},{5,1},{9... | collective-permute-start | bytes 786440 | tf_op jit(solution)/shard_map/ppermute | solution.py:409
  13.9 8.4 %collective-permute-start.5 = (bf16[4,256,128]{2,1,0:T(8,128)(2,1)S(1)}, bf16[4,256,128]{2,1,0:T(8,128)(2,1)S(1)}, u32[]{:S(2)}, u32[]{:S(2)}) collective-permute-start(bf16[4,256,128]{2,1,0:T(8,128)(2,1)S(1)} %collective-permute-done.3.refs_2_), channel_id=1, source_target_pairs={{0,4},{4,8},{8,12},{12,28},{28,24},{24,20},{20,16},{16,0},{1,5},{5... | collective-permute-start | bytes 786440 | tf_op jit(solution)/shard_map/ppermute | solution.py:408
  14.4 10.0 %collective-permute-start.8 = (bf16[4,256,128]{2,1,0:T(8,128)(2,1)S(1)}, bf16[4,256,128]{2,1,0:T(8,128)(2,1)S(1)}, u32[]{:S(2)}, u32[]{:S(2)}) collective-permute-start(bf16[4,256,128]{2,1,0:T(8,128)(2,1)S(1)} %bitcast.12), channel_id=1, source_target_pairs={{0,1},{1,0},{2,3},{3,2},{4,5},{5,4},{6,7},{7,6},{8,9},{9,8},{10,11... | collective-permute-start | bytes 786440 | tf_op jit(solution)/shard_map/ppermute | solution.py:41
  17.6 4.8 %collective-permute-start.10 = (bf16[4,256,128]{2,1,0:T(8,128)(2,1)S(1)}, bf16[4,256,128]{2,1,0:T(8,128)(2,1)S(1)}, u32[]{:S(2)}, u32[]{:S(2)}) collective-permute-start(bf16[4,256,128]{2,1,0:T(8,128)(2,1)S(1)} %collective-permute-done.4.refs_3_), channel_id=1, source_target_pairs={{0,1},{1,0},{2,3},{3,2},{4,5},{5,4},{6,7},{7,6},{8,9},{9,8},{10,11... | collective-permute-start | bytes 786440 | tf_op jit(solution)/shard_map/ppermute | solution.py:41
  21.1 3.3 %collective-permute-start.1 = (bf16[4,256,128]{2,1,0:T(8,128)(2,1)S(1)}, bf16[4,256,128]{2,1,0:T(8,128)(2,1)S(1)}, u32[]{:S(2)}, u32[]{:S(2)}) collective-permute-start(bf16[4,256,128]{2,1,0:T(8,128)(2,1)S(1)} %collective-permute-done.refs_0_), channel_id=1, source_target_pairs={{0,1},{1,0},{2,3},{3,2},{4,5},{5,4},{6,7},{7,6},{8,9},{9,8},{10,11... | collective-permute-start | bytes 786440 | tf_op jit(solution)/shard_map/ppermute | solution.py:41
  22.4 2.0 %collective-permute-start.7 = (bf16[4,256,128]{2,1,0:T(8,128)(2,1)S(1)}, bf16[4,256,128]{2,1,0:T(8,128)(2,1)S(1)}, u32[]{:S(2)}, u32[]{:S(2)}) collective-permute-start(bf16[4,256,128]{2,1,0:T(8,128)(2,1)S(1)} %collective-permute-done.5.refs_0_), channel_id=1, source_target_pairs={{0,1},{1,0},{2,3},{3,2},{4,5},{5,4},{6,7},{7,6},{8,9},{9,8},{10,11... | collective-permute-start | bytes 786440 | tf_op jit(solution)/shard_map/ppermute | solution.py:41
  22.4 2.0 %collective-permute-start.11 = (bf16[4,256,128]{2,1,0:T(8,128)(2,1)S(1)}, bf16[4,256,128]{2,1,0:T(8,128)(2,1)S(1)}, u32[]{:S(2)}, u32[]{:S(2)}) collective-permute-start(bf16[4,256,128]{2,1,0:T(8,128)(2,1)S(1)} %collective-permute-done.6.refs_1_), channel_id=1, source_target_pairs={{0,1},{1,0},{2,3},{3,2},{4,5},{5,4},{6,7},{7,6},{8,9},{9,8},{10,11... | collective-permute-start | bytes 786440 | tf_op jit(solution)/shard_map/ppermute | solution.py:41
  26.8 11.9 %collective-permute-start.14 = (bf16[8,256,128]{2,1,0:T(8,128)(2,1)S(1)}, bf16[8,256,128]{2,1,0:T(8,128)(2,1)S(1)}, u32[]{:S(2)}, u32[]{:S(2)}) collective-permute-start(bf16[8,256,128]{2,1,0:T(8,128)(2,1)S(1)} %get-tuple-element.37.low_ref), channel_id=1, source_target_pairs={{0,1},{1,0},{2,3},{3,2},{4,5},{5,4},{6,7},{7,6},{8,9},{9,8},{10,11... | collective-permute-start | bytes 1572872 | tf_op jit(solution)/shard_map/ppermute | solution.py:41
  26.9 6.8 %collective-permute-start.15 = (bf16[2,256,128]{2,1,0:T(8,128)(2,1)S(1)}, bf16[2,256,128]{2,1,0:T(8,128)(2,1)S(1)}, u32[]{:S(2)}, u32[]{:S(2)}) collective-permute-start(bf16[2,256,128]{2,1,0:T(8,128)(2,1)S(1)} %get-tuple-element.42), channel_id=1, source_target_pairs={{0,4},{4,8},{8,12},{12,28},{28,24},{24,20},{20,16},{16,0},{1,5},{5... | collective-permute-start | bytes 393224 | tf_op jit(solution)/shard_map/ppermute | solution.py:408
  27.4 6.4 %collective-permute-start.16 = (bf16[2,256,128]{2,1,0:T(8,128)(2,1)S(1)}, bf16[2,256,128]{2,1,0:T(8,128)(2,1)S(1)}, u32[]{:S(2)}, u32[]{:S(2)}) collective-permute-start(bf16[2,256,128]{2,1,0:T(8,128)(2,1)S(1)} %get-tuple-element.43), channel_id=1, source_target_pairs={{4,0},{8,4},{12,8},{28,12},{24,28},{20,24},{16,20},{0,16},{5,1},{9... | collective-permute-start | bytes 393224 | tf_op jit(solution)/shard_map/ppermute | solution.py:409
  29.4 7.1 %collective-permute-start.18 = (bf16[2,256,128]{2,1,0:T(8,128)(2,1)S(1)}, bf16[2,256,128]{2,1,0:T(8,128)(2,1)S(1)}, u32[]{:S(2)}, u32[]{:S(2)}) collective-permute-start(bf16[2,256,128]{2,1,0:T(8,128)(2,1)S(1)} %get-tuple-element.45), channel_id=1, source_target_pairs={{0,4},{4,8},{8,12},{12,28},{28,24},{24,20},{20,16},{16,0},{1,5},{5... | collective-permute-start | bytes 393224 | tf_op jit(solution)/shard_map/ppermute | solution.py:408
  29.4 7.7 %collective-permute-start.19 = (bf16[2,256,128]{2,1,0:T(8,128)(2,1)S(1)}, bf16[2,256,128]{2,1,0:T(8,128)(2,1)S(1)}, u32[]{:S(2)}, u32[]{:S(2)}) collective-permute-start(bf16[2,256,128]{2,1,0:T(8,128)(2,1)S(1)} %get-tuple-element.46), channel_id=1, source_target_pairs={{4,0},{8,4},{12,8},{28,12},{24,28},{20,24},{16,20},{0,16},{5,1},{9... | collective-permute-start | bytes 393224 | tf_op jit(solution)/shard_map/ppermute | solution.py:409
  33.7 10.6 %collective-permute-start.12 = (bf16[4,256,128]{2,1,0:T(8,128)(2,1)S(1)}, bf16[4,256,128]{2,1,0:T(8,128)(2,1)S(1)}, u32[]{:S(2)}, u32[]{:S(2)}) collective-permute-start(bf16[4,256,128]{2,1,0:T(8,128)(2,1)S(1)} %get-tuple-element.35), channel_id=1, source_target_pairs={{0,4},{4,8},{8,12},{12,28},{28,24},{24,20},{20,16},{16,0},{1,5},{5... | collective-permute-start | bytes 786440 | tf_op jit(solution)/shard_map/ppermute | solution.py:408
  33.8 10.6 %collective-permute-start.13 = (bf16[4,256,128]{2,1,0:T(8,128)(2,1)S(1)}, bf16[4,256,128]{2,1,0:T(8,128)(2,1)S(1)}, u32[]{:S(2)}, u32[]{:S(2)}) collective-permute-start(bf16[4,256,128]{2,1,0:T(8,128)(2,1)S(1)} %get-tuple-element.36), channel_id=1, source_target_pairs={{4,0},{8,4},{12,8},{28,12},{24,28},{20,24},{16,20},{0,16},{5,1},{9... | collective-permute-start | bytes 786440 | tf_op jit(solution)/shard_map/ppermute | solution.py:409
  36.5 6.4 %collective-permute-start.17 = (bf16[2,256,128]{2,1,0:T(8,128)(2,1)S(1)}, bf16[2,256,128]{2,1,0:T(8,128)(2,1)S(1)}, u32[]{:S(2)}, u32[]{:S(2)}) collective-permute-start(bf16[2,256,128]{2,1,0:T(8,128)(2,1)S(1)} %merge.3), channel_id=1, source_target_pairs={{0,2},{2,0},{1,3},{3,1},{4,6},{6,4},{5,7},{7,5},{8,10},{10,8},{9,1... | collective-permute-start | bytes 393224 | tf_op jit(solution)/shard_map/ppermute | solution.py:41
  37.2 7.1 %collective-permute-start.20 = (bf16[2,256,128]{2,1,0:T(8,128)(2,1)S(1)}, bf16[2,256,128]{2,1,0:T(8,128)(2,1)S(1)}, u32[]{:S(2)}, u32[]{:S(2)}) collective-permute-start(bf16[2,256,128]{2,1,0:T(8,128)(2,1)S(1)} %merge.4), channel_id=1, source_target_pairs={{0,2},{2,0},{1,3},{3,1},{4,6},{6,4},{5,7},{7,5},{8,10},{10,8},{9,1... | collective-permute-start | bytes 393224 | tf_op jit(solution)/shard_map/ppermute | solution.py:41
  (4 other events, 22.4 us)

commit v7 on v6

--- a/solution.py
+++ b/solution.py
@@ -236,7 +236,7 @@
     conv_ref, padded_ref, lhs_ref, list_ref = refs[len(members) + 1 + carried :]
     tiles, size, cols = conv_ref.shape
     owned = blocks[0].shape[0]
-    side, pairs, _ = lhs_ref.shape
+    side, pairs = lhs_ref.shape[0] // 2, lhs_ref.shape[1]
     clear_ends(padded_ref)
 
     count = 0
@@ -250,23 +250,45 @@
 
         count = count + jnp.where(here, 1, 0)
 
-    def some(i, carry):
-        names = [list_ref[jnp.minimum(i * side + n, count - 1)] for n in range(side)]
-        for n, t in enumerate(names):
-            part, slot, _ = place(ids_ref, t, owned, closed)
+    groups = (count + side - 1) // side
+
+    def named_tile(i, n):
+        return list_ref[jnp.minimum(i * side + n, count - 1)]
+
+    def pick(i, base):
+        for n in range(side):
+            part, slot, _ = place(ids_ref, named_tile(i, n), owned, closed)
             for b, ref in zip(members, blocks):
                 @pl.when(part == b)
                 def _(n=n, ref=ref, slot=slot):
-                    padded_ref[n, PAD : PAD + size, :] = ref[slot].astype(jnp.float32)
+                    padded_ref[base + n, PAD : PAD + size, :] = ref[slot].astype(jnp.float32)
+
+    def work(i, base, following):
+        for n in range(side):
+            t = named_tile(i, n)
+            both = spread(lhs_ref, band_ref, base + n, t)
+            build(padded_ref, lhs_ref, following + n)
+            for s in range(2):
+                conv_ref[t, pl.ds(s, pairs, stride=2), :] = both[:, s * cols : (s + 1) * cols]
+
+    @pl.when(count > 0)
+    def _():
+        pick(0, 0)
         for n in range(side):
             build(padded_ref, lhs_ref, n)
-        both = [spread(lhs_ref, band_ref, n, t) for n, t in enumerate(names)]
-        for n, t in enumerate(names):
-            for s in range(2):
-                conv_ref[t, pl.ds(s, pairs, stride=2), :] = both[n][:, s * cols : (s + 1) * cols]
+
+    def some(i, carry):
+        pick(2 * i + 1, side)
+        work(2 * i, 0, side)
+
+        @pl.when(2 * i + 1 < groups)
+        def _():
+            pick(2 * i + 2, 0)
+            work(2 * i + 1, side, 0)
+
         return carry
 
-    lax.fori_loop(0, (count + side - 1) // side, some, 0)
+    lax.fori_loop(0, (groups + 1) // 2, some, 0)
 
 
 def convolve_kernel(blocks, closed, pieces, ids_ref, live_ref, *refs):
@@ -442,7 +464,7 @@
         compiler_params=params(6),
         cost_estimate=cost(5),
     )(jnp.swapaxes(psf_width, 2, 3), live_count, var_flat, var_other)
-    side = 2 if tiles % 2 == 0 else 1
+    side = 1
 
     def multiply(members, sources, *carried):
         return pl.pallas_call(
@@ -453,8 +475,8 @@
             out_specs=vmem(1)[0],
             input_output_aliases={len(sources) + 2: 0} if carried else {},
             scratch_shapes=[
-                VMEM((side, size + 2 * PAD, cols), f32),
-                VMEM((side, size // 2, (count + 1) * cols), low),
+                VMEM((2 * side, size + 2 * PAD, cols), f32),
+                VMEM((2 * side, size // 2, (count + 1) * cols), low),
                 SMEM((tiles,), jnp.int32),
             ],
             compiler_params=params(8),

time: 45.4 us -> 45.7 us (level)
  Pallas kernels: 14.2 us -> 14.9 us
    pallas_call x2, Pallas kernels: 4.65 us -> 5.33 us  [multiply(): pl.pallas_call(functools.partial(multiply_kernel, members, closed, len(ca...]
  transfers between devices with their start and end apart: 21 -> 21, of which waited for: 7 -> 7; matrix products, arithmetic and copies ran while one was open for 0% -> 0% of each run, Pallas kernels for 24% -> 26%
where the time goes in v7:
time: 45.7 us; the launch traced here: 45.5 us
  starting transfers between devices  17.1 us (37%)
  Pallas kernels  14.9 us (33%)
  waiting for transfers between devices  12 us (26%)
  between operations  0.82 us (2%)
  local copies, waits for them, and re-layouts  0.72 us (2%)
    ppermute x5, starting transfers between devices, on_device(): behind = lambda block: lax.ppermute(block, ('groups', 'exp'), back)  10.3 us
    pallas_call x2, Pallas kernels, multiply(): pl.pallas_call(functools.partial(multiply_kernel, members, closed, len(ca...  5.33 us
    ppermute x5, waiting for transfers between devices, on_device(): ahead = lambda block: lax.ppermute(block, ('groups', 'exp'), forth)  4.17 us
    ppermute x10, starting transfers between devices, sent(): lax.ppermute(block, axis, [(i, (i + distance) % devices) for i in range(d...  3.8 us
    ppermute x10, waiting for transfers between devices, sent(): lax.ppermute(block, axis, [(i, (i + distance) % devices) for i in range(d...  3.71 us
    ppermute x1, waiting for transfers between devices, fetched(): lax.ppermute(block, axis, [((i + distance) % devices, i) for i in range(d...  3.37 us
    pallas_call x1, Pallas kernels, on_device(): pl.pallas_call(taps_kernel, name='taps', out_shape=shape((tiles + 1, (cou...  2.48 us
    pallas_call x1, Pallas kernels, on_device(): pl.pallas_call(functools.partial(convolve_kernel, blocks, closed, pieces)...  2.35 us
  transfers between devices with their start and end apart: 21, of which 7 were waited for; matrix products, arithmetic and copies ran while one was open for 0% of the time, Pallas kernels for 26%

profile of v7, /device:TPU:0, one launch (start us, length us, event | category | flops | bytes accessed | tf_op | source)
XLA Modules:
  0.0 45.5 jit_solution(1304854885655793048)
XLA Ops:
  0.6 0.6 %collective-permute-start.2 = (f32[8,256,128]{2,1,0:T(8,128)}, f32[8,256,128]{2,1,0:T(8,128)S(1)}, u32[]{:S(2)}, u32[]{:S(2)}) collective-permute-start(f32[8,256,128]{2,1,0:T(8,128)} %bitcast.6), channel_id=1, source_target_pairs={{0,1},{1,0},{2,3},{3,2},{4,5},{5,4},{6,7},{7,6},{8,9},{9,8},{10,11... | collective-permute-start | bytes 3145736 | tf_op jit(solution)/shard_map/ppermute | solution.py:41
  1.2 2.6 %collective-permute-start.4 = (bf16[4,256,128]{2,1,0:T(8,128)(2,1)}, bf16[4,256,128]{2,1,0:T(8,128)(2,1)S(1)}, u32[]{:S(2)}, u32[]{:S(2)}) collective-permute-start(bf16[4,256,128]{2,1,0:T(8,128)(2,1)} %bitcast.9), channel_id=1, source_target_pairs={{4,0},{8,4},{12,8},{28,12},{24,28},{20,24},{16,20},{0,16},{5,1},{9... | collective-permute-start | bytes 786440 | tf_op jit(solution)/shard_map/ppermute | solution.py:431
  3.8 1.5 %collective-permute-start.3 = (bf16[4,256,128]{2,1,0:T(8,128)(2,1)}, bf16[4,256,128]{2,1,0:T(8,128)(2,1)S(1)}, u32[]{:S(2)}, u32[]{:S(2)}) collective-permute-start(bf16[4,256,128]{2,1,0:T(8,128)(2,1)} %bitcast.10), channel_id=1, source_target_pairs={{2,0},{0,2},{3,1},{1,3},{6,4},{4,6},{7,5},{5,7},{10,8},{8,10},{11,... | collective-permute-start | bytes 786440 | tf_op jit(solution)/shard_map/ppermute | solution.py:36
  5.8 0.7 %copy-done.3 = f32[1,2,4,27]{3,2,1,0:T(4,128)S(1)} copy-done((f32[1,2,4,27]{3,2,1,0:T(4,128)S(1)}, f32[1,2,4,27]{3,2,1,0:T(4,128)}, u32[]{:S(2)}) %copy-start.3) | copy-done | bytes 888
  6.5 2.5 %taps.1.refs_4_.refs_2_.refs_7_ = bf16[9,2944,128]{2,1,0:T(8,128)(2,1)S(1)} custom-call(f32[1,2,4,27]{3,2,1,0:T(4,128)S(1)} %copy-done.3), custom_call_target="tpu_custom_call" | custom-call | flops 3000000000 | bytes 9000000 | tf_op jit(solution)/shard_map/taps/pallas_call | solution.py:439
  9.0 3.4 %collective-permute-done.3.refs_2_ = bf16[4,256,128]{2,1,0:T(8,128)(2,1)S(1)} collective-permute-done((bf16[4,256,128]{2,1,0:T(8,128)(2,1)}, bf16[4,256,128]{2,1,0:T(8,128)(2,1)S(1)}, u32[]{:S(2)}, u32[]{:S(2)}) %collective-permute-start.3) | collective-permute-done | bytes 262176 | tf_op jit(solution)/shard_map/ppermute | solution.py:36
  12.4 1.6 %collective-permute-start.6 = (bf16[4,256,128]{2,1,0:T(8,128)(2,1)S(1)}, bf16[4,256,128]{2,1,0:T(8,128)(2,1)S(1)}, u32[]{:S(2)}, u32[]{:S(2)}) collective-permute-start(bf16[4,256,128]{2,1,0:T(8,128)(2,1)S(1)} %collective-permute-done.3.refs_2_), channel_id=1, source_target_pairs={{4,0},{8,4},{12,8},{28,12},{24,28},{20,24},{16,20},{0,16},{5,1},{9... | collective-permute-start | bytes 786440 | tf_op jit(solution)/shard_map/ppermute | solution.py:431
  14.4 3.6 %multiply.2.refs_3_ = f32[8,256,128]{2,1,0:T(8,128)S(1)} custom-call(s32[1,2,4]{2,1,0:T(2,128)S(1)} %copy-done.5, bf16[4,256,128]{2,1,0:T(8,128)(2,1)S(1)} %collective-permute-done.refs_0_, bf16[4,256,128]{2,1,0:T(8,128)(2,1)S(1)} %bitcast.13, bf16[4,256,128]{2,1,0:T(8,128)(2,1)S(1)} %collective-permute-done.3.refs_2_, ...), custom_call_target="tpu_custom_call" | custom-call | flops 3000000000 | bytes 9000000 | tf_op jit(solution)/shard_map/multiply/pallas_call | solution.py:470
  18.0 0.6 %collective-permute-start.10 = (bf16[4,256,128]{2,1,0:T(8,128)(2,1)S(1)}, bf16[4,256,128]{2,1,0:T(8,128)(2,1)S(1)}, u32[]{:S(2)}, u32[]{:S(2)}) collective-permute-start(bf16[4,256,128]{2,1,0:T(8,128)(2,1)S(1)} %collective-permute-done.4.refs_3_), channel_id=1, source_target_pairs={{0,1},{1,0},{2,3},{3,2},{4,5},{5,4},{6,7},{7,6},{8,9},{9,8},{10,11... | collective-permute-start | bytes 786440 | tf_op jit(solution)/shard_map/ppermute | solution.py:41
  18.6 1.7 %norms.1 = (f32[8,256,128]{2,1,0:T(8,128)S(1)}, f32[8,256,128]{2,1,0:T(8,128)S(1)}, bf16[8,256,256]{2,1,0:T(8,128)(2,1)S(1)}, bf16[8,256,128]{2,1,0:T(8,128)(2,1)S(1)}) custom-call(f32[1,2,2,4]{3,2,1,0:T(2,128)S(1)} %bitcast.14, s32[1,2]{1,0:T(1,128)S(1)} %copy-done.6, f32[8,256,128]{2,1,0:T(8,128)S(1)} %bitcast.7, ...), custom_call_target="tpu_custom_call" | custom-call | flops 5000000000 | bytes 15000000 | tf_op jit(solution)/shard_map/norms/pallas_call | solution.py:453
  20.3 0.8 %collective-permute-done.6.refs_1_ = bf16[4,256,128]{2,1,0:T(8,128)(2,1)S(1)} collective-permute-done((bf16[4,256,128]{2,1,0:T(8,128)(2,1)S(1)}, bf16[4,256,128]{2,1,0:T(8,128)(2,1)S(1)}, u32[]{:S(2)}, u32[]{:S(2)}) %collective-permute-start.6) | collective-permute-done | bytes 262176 | tf_op jit(solution)/shard_map/ppermute | solution.py:431
  21.1 1.3 %collective-permute-done.5.refs_0_ = bf16[4,256,128]{2,1,0:T(8,128)(2,1)S(1)} collective-permute-done((bf16[4,256,128]{2,1,0:T(8,128)(2,1)S(1)}, bf16[4,256,128]{2,1,0:T(8,128)(2,1)S(1)}, u32[]{:S(2)}, u32[]{:S(2)}) %collective-permute-start.5) | collective-permute-done | bytes 262176 | tf_op jit(solution)/shard_map/ppermute | solution.py:430
  22.9 1.7 %multiply.3.refs_6_ = f32[8,256,128]{2,1,0:T(8,128)S(1)} custom-call(s32[1,2,4]{2,1,0:T(2,128)S(1)} %copy-done.5, bf16[4,256,128]{2,1,0:T(8,128)(2,1)S(1)} %collective-permute-done.5.refs_0_, bf16[4,256,128]{2,1,0:T(8,128)(2,1)S(1)} %collective-permute-done.6.refs_1_, ...), custom_call_target="tpu_custom_call", output_to_operand_aliasing={{}: (4, {})} | custom-call | flops 3000000000 | bytes 9000000 | tf_op jit(solution)/shard_map/multiply/pallas_call | solution.py:470
  24.7 2.4 %convolve.1 = (bf16[8,256,128]{2,1,0:T(8,128)(2,1)S(1)}, bf16[4,256,128]{2,1,0:T(8,128)(2,1)S(1)}, f32[4,256,128]{2,1,0:T(8,128)S(1)}, bf16[4,256,128]{2,1,0:T(8...) custom-call(s32[1,2,4]{2,1,0:T(2,128)S(1)} %copy-done.5, ...), custom_call_target="tpu_custom_call" | custom-call | flops 5000000000 | bytes 15000000 | tf_op jit(solution)/shard_map/convolve/pallas_call | solution.py:501
  27.6 2.1 %collective-permute-start.16 = (bf16[2,256,128]{2,1,0:T(8,128)(2,1)S(1)}, bf16[2,256,128]{2,1,0:T(8,128)(2,1)S(1)}, u32[]{:S(2)}, u32[]{:S(2)}) collective-permute-start(bf16[2,256,128]{2,1,0:T(8,128)(2,1)S(1)} %get-tuple-element.43), channel_id=1, source_target_pairs={{4,0},{8,4},{12,8},{28,12},{24,28},{20,24},{16,20},{0,16},{5,1},{9... | collective-permute-start | bytes 393224 | tf_op jit(solution)/shard_map/ppermute | solution.py:431
  29.7 2.0 %collective-permute-start.19 = (bf16[2,256,128]{2,1,0:T(8,128)(2,1)S(1)}, bf16[2,256,128]{2,1,0:T(8,128)(2,1)S(1)}, u32[]{:S(2)}, u32[]{:S(2)}) collective-permute-start(bf16[2,256,128]{2,1,0:T(8,128)(2,1)S(1)} %get-tuple-element.46), channel_id=1, source_target_pairs={{4,0},{8,4},{12,8},{28,12},{24,28},{20,24},{16,20},{0,16},{5,1},{9... | collective-permute-start | bytes 393224 | tf_op jit(solution)/shard_map/ppermute | solution.py:431
  31.7 2.3 %collective-permute-done.15.first_ref = bf16[2,256,128]{2,1,0:T(8,128)(2,1)S(1)} collective-permute-done((bf16[2,256,128]{2,1,0:T(8,128)(2,1)S(1)}, bf16[2,256,128]{2,1,0:T(8,128)(2,1)S(1)}, u32[]{:S(2)}, u32[]{:S(2)}) %collective-permute-start.15) | collective-permute-done | bytes 131104 | tf_op jit(solution)/shard_map/ppermute | solution.py:430
  34.0 2.1 %collective-permute-start.13 = (bf16[4,256,128]{2,1,0:T(8,128)(2,1)S(1)}, bf16[4,256,128]{2,1,0:T(8,128)(2,1)S(1)}, u32[]{:S(2)}, u32[]{:S(2)}) collective-permute-start(bf16[4,256,128]{2,1,0:T(8,128)(2,1)S(1)} %get-tuple-element.36), channel_id=1, source_target_pairs={{4,0},{8,4},{12,8},{28,12},{24,28},{20,24},{16,20},{0,16},{5,1},{9... | collective-permute-start | bytes 786440 | tf_op jit(solution)/shard_map/ppermute | solution.py:431
  36.2 0.6 %collective-permute-done.18.first_ref = bf16[2,256,128]{2,1,0:T(8,128)(2,1)S(1)} collective-permute-done((bf16[2,256,128]{2,1,0:T(8,128)(2,1)S(1)}, bf16[2,256,128]{2,1,0:T(8,128)(2,1)S(1)}, u32[]{:S(2)}, u32[]{:S(2)}) %collective-permute-start.18) | collective-permute-done | bytes 131104 | tf_op jit(solution)/shard_map/ppermute | solution.py:430
  37.4 1.6 %collective-permute-start.20 = (bf16[2,256,128]{2,1,0:T(8,128)(2,1)S(1)}, bf16[2,256,128]{2,1,0:T(8,128)(2,1)S(1)}, u32[]{:S(2)}, u32[]{:S(2)}) collective-permute-start(bf16[2,256,128]{2,1,0:T(8,128)(2,1)S(1)} %merge.4), channel_id=1, source_target_pairs={{0,2},{2,0},{1,3},{3,1},{4,6},{6,4},{5,7},{7,5},{8,10},{10,8},{9,1... | collective-permute-start | bytes 393224 | tf_op jit(solution)/shard_map/ppermute | solution.py:41
  39.0 1.9 %score.1 = f32[8,256,128]{2,1,0:T(8,128)} custom-call(bf16[8,256,128]{2,1,0:T(8,128)(2,1)S(1)} %get-tuple-element.37.low_ref, bf16[8,256,128]{2,1,0:T(8,128)(2,1)S(1)} %collective-permute-done.14.other_ref, bf16[8,256,256]{2,1,0:T(8,128)(2,1)S(1)} %get-tuple-element.38.prow_ref, bf16[8,256,128]{2,1,0:T(8,128)(2,1)S(1)} %get-tuple-element.39.pcol_ref, ...), custom_call_target="tpu_custom_call" | custom-call | flops 5000000000 | bytes 15000000 | tf_op jit(solution)/shard_map/score/pallas_call | solution.py:553
  41.0 2.2 %collective-permute-done.17.refs_0_ = bf16[2,256,128]{2,1,0:T(8,128)(2,1)S(1)} collective-permute-done((bf16[2,256,128]{2,1,0:T(8,128)(2,1)S(1)}, bf16[2,256,128]{2,1,0:T(8,128)(2,1)S(1)}, u32[]{:S(2)}, u32[]{:S(2)}) %collective-permute-start.17) | collective-permute-done | bytes 131104 | tf_op jit(solution)/shard_map/ppermute | solution.py:41
  43.2 1.5 %collective-permute-done.20.refs_1_ = bf16[2,256,128]{2,1,0:T(8,128)(2,1)S(1)} collective-permute-done((bf16[2,256,128]{2,1,0:T(8,128)(2,1)S(1)}, bf16[2,256,128]{2,1,0:T(8,128)(2,1)S(1)}, u32[]{:S(2)}, u32[]{:S(2)}) %collective-permute-start.20) | collective-permute-done | bytes 131104 | tf_op jit(solution)/shard_map/ppermute | solution.py:41
  44.6 0.9 %merge.5 = f32[4,256,128]{2,1,0:T(8,128)} custom-call(f32[4,256,128]{2,1,0:T(8,128)S(1)} %get-tuple-element.34.here_ref, bf16[4,256,128]{2,1,0:T(8,128)(2,1)S(1)} %collective-permute-done.12.first_ref, bf16[4,256,128]{2,1,0:T(8,128)(2,1)S(1)} %collective-permute-done.13.last_ref, bf16[2,256,128]{2,1,0:T(8,128)(2,1)S(1)} %collective-permute-done.17.refs_0_, ...), custom_call_target="tpu_custom_call" | custom-call | flops 500000000 | bytes 1500000 | tf_op jit(solution)/shard_map/merge/pallas_call | solution.py:529
  (41 shorter events, 2.8 us)
Async XLA Ops:
  0.6 13.8 %copy-start.2 = (bf16[1,4,256,128]{3,2,1,0:T(8,128)(2,1)S(1)}, bf16[1,4,256,128]{3,2,1,0:T(8,128)(2,1)}, u32[]{:S(2)}) copy-start(bf16[1,4,256,128]{3,2,1,0:T(8,128)(2,1)} %param.7) | copy-start | bytes 786436
  0.6 17.4 %collective-permute-start.2 = (f32[8,256,128]{2,1,0:T(8,128)}, f32[8,256,128]{2,1,0:T(8,128)S(1)}, u32[]{:S(2)}, u32[]{:S(2)}) collective-permute-start(f32[8,256,128]{2,1,0:T(8,128)} %bitcast.6), channel_id=1, source_target_pairs={{0,1},{1,0},{2,3},{3,2},{4,5},{5,4},{6,7},{7,6},{8,9},{9,8},{10,11... | collective-permute-start | bytes 3145736 | tf_op jit(solution)/shard_map/ppermute | solution.py:41
  1.2 12.7 %collective-permute-start.4 = (bf16[4,256,128]{2,1,0:T(8,128)(2,1)}, bf16[4,256,128]{2,1,0:T(8,128)(2,1)S(1)}, u32[]{:S(2)}, u32[]{:S(2)}) collective-permute-start(bf16[4,256,128]{2,1,0:T(8,128)(2,1)} %bitcast.9), channel_id=1, source_target_pairs={{4,0},{8,4},{12,8},{28,12},{24,28},{20,24},{16,20},{0,16},{5,1},{9... | collective-permute-start | bytes 786440 | tf_op jit(solution)/shard_map/ppermute | solution.py:431
  3.8 8.6 %collective-permute-start.3 = (bf16[4,256,128]{2,1,0:T(8,128)(2,1)}, bf16[4,256,128]{2,1,0:T(8,128)(2,1)S(1)}, u32[]{:S(2)}, u32[]{:S(2)}) collective-permute-start(bf16[4,256,128]{2,1,0:T(8,128)(2,1)} %bitcast.10), channel_id=1, source_target_pairs={{2,0},{0,2},{3,1},{1,3},{6,4},{4,6},{7,5},{5,7},{10,8},{8,10},{11,... | collective-permute-start | bytes 786440 | tf_op jit(solution)/shard_map/ppermute | solution.py:36
  5.3 9.1 %collective-permute-start = (bf16[4,256,128]{2,1,0:T(8,128)(2,1)}, bf16[4,256,128]{2,1,0:T(8,128)(2,1)S(1)}, u32[]{:S(2)}, u32[]{:S(2)}) collective-permute-start(bf16[4,256,128]{2,1,0:T(8,128)(2,1)} %bitcast.11), channel_id=1, source_target_pairs={{0,4},{4,8},{8,12},{12,28},{28,24},{24,20},{20,16},{16,0},{1,5},{5... | collective-permute-start | bytes 786440 | tf_op jit(solution)/shard_map/ppermute | solution.py:430
  8.9 9.6 %copy-start = (f32[1,2,4,256,128]{4,3,2,1,0:T(8,128)S(1)}, f32[1,2,4,256,128]{4,3,2,1,0:T(8,128)}, u32[]{:S(2)}) copy-start(f32[1,2,4,256,128]{4,3,2,1,0:T(8,128)} %param.9) | copy-start | bytes 3145732
  9.0 9.6 %copy-start.4 = (f32[1,2,4,2]{2,3,1,0:T(2,128)S(1)}, f32[1,2,4,2]{2,3,1,0:T(2,128)}, u32[]{:S(2)}) copy-start(f32[1,2,4,2]{2,3,1,0:T(2,128)} %param.11) | copy-start | bytes 196
  12.4 12.3 %collective-permute-start.9 = (bf16[4,256,128]{2,1,0:T(8,128)(2,1)S(1)}, bf16[4,256,128]{2,1,0:T(8,128)(2,1)S(1)}, u32[]{:S(2)}, u32[]{:S(2)}) collective-permute-start(bf16[4,256,128]{2,1,0:T(8,128)(2,1)S(1)} %collective-permute-done.3.refs_2_), channel_id=1, source_target_pairs={{0,1},{1,0},{2,3},{3,2},{4,5},{5,4},{6,7},{7,6},{8,9},{9,8},{10,11... | collective-permute-start | bytes 786440 | tf_op jit(solution)/shard_map/ppermute | solution.py:41
  12.4 8.7 %collective-permute-start.6 = (bf16[4,256,128]{2,1,0:T(8,128)(2,1)S(1)}, bf16[4,256,128]{2,1,0:T(8,128)(2,1)S(1)}, u32[]{:S(2)}, u32[]{:S(2)}) collective-permute-start(bf16[4,256,128]{2,1,0:T(8,128)(2,1)S(1)} %collective-permute-done.3.refs_2_), channel_id=1, source_target_pairs={{4,0},{8,4},{12,8},{28,12},{24,28},{20,24},{16,20},{0,16},{5,1},{9... | collective-permute-start | bytes 786440 | tf_op jit(solution)/shard_map/ppermute | solution.py:431
  13.9 8.4 %collective-permute-start.5 = (bf16[4,256,128]{2,1,0:T(8,128)(2,1)S(1)}, bf16[4,256,128]{2,1,0:T(8,128)(2,1)S(1)}, u32[]{:S(2)}, u32[]{:S(2)}) collective-permute-start(bf16[4,256,128]{2,1,0:T(8,128)(2,1)S(1)} %collective-permute-done.3.refs_2_), channel_id=1, source_target_pairs={{0,4},{4,8},{8,12},{12,28},{28,24},{24,20},{20,16},{16,0},{1,5},{5... | collective-permute-start | bytes 786440 | tf_op jit(solution)/shard_map/ppermute | solution.py:430
  14.4 10.3 %collective-permute-start.8 = (bf16[4,256,128]{2,1,0:T(8,128)(2,1)S(1)}, bf16[4,256,128]{2,1,0:T(8,128)(2,1)S(1)}, u32[]{:S(2)}, u32[]{:S(2)}) collective-permute-start(bf16[4,256,128]{2,1,0:T(8,128)(2,1)S(1)} %bitcast.12), channel_id=1, source_target_pairs={{0,1},{1,0},{2,3},{3,2},{4,5},{5,4},{6,7},{7,6},{8,9},{9,8},{10,11... | collective-permute-start | bytes 786440 | tf_op jit(solution)/shard_map/ppermute | solution.py:41
  18.0 4.4 %collective-permute-start.10 = (bf16[4,256,128]{2,1,0:T(8,128)(2,1)S(1)}, bf16[4,256,128]{2,1,0:T(8,128)(2,1)S(1)}, u32[]{:S(2)}, u32[]{:S(2)}) collective-permute-start(bf16[4,256,128]{2,1,0:T(8,128)(2,1)S(1)} %collective-permute-done.4.refs_3_), channel_id=1, source_target_pairs={{0,1},{1,0},{2,3},{3,2},{4,5},{5,4},{6,7},{7,6},{8,9},{9,8},{10,11... | collective-permute-start | bytes 786440 | tf_op jit(solution)/shard_map/ppermute | solution.py:41
  21.1 3.6 %collective-permute-start.1 = (bf16[4,256,128]{2,1,0:T(8,128)(2,1)S(1)}, bf16[4,256,128]{2,1,0:T(8,128)(2,1)S(1)}, u32[]{:S(2)}, u32[]{:S(2)}) collective-permute-start(bf16[4,256,128]{2,1,0:T(8,128)(2,1)S(1)} %collective-permute-done.refs_0_), channel_id=1, source_target_pairs={{0,1},{1,0},{2,3},{3,2},{4,5},{5,4},{6,7},{7,6},{8,9},{9,8},{10,11... | collective-permute-start | bytes 786440 | tf_op jit(solution)/shard_map/ppermute | solution.py:41
  22.4 2.3 %collective-permute-start.7 = (bf16[4,256,128]{2,1,0:T(8,128)(2,1)S(1)}, bf16[4,256,128]{2,1,0:T(8,128)(2,1)S(1)}, u32[]{:S(2)}, u32[]{:S(2)}) collective-permute-start(bf16[4,256,128]{2,1,0:T(8,128)(2,1)S(1)} %collective-permute-done.5.refs_0_), channel_id=1, source_target_pairs={{0,1},{1,0},{2,3},{3,2},{4,5},{5,4},{6,7},{7,6},{8,9},{9,8},{10,11... | collective-permute-start | bytes 786440 | tf_op jit(solution)/shard_map/ppermute | solution.py:41
  22.4 2.3 %collective-permute-start.11 = (bf16[4,256,128]{2,1,0:T(8,128)(2,1)S(1)}, bf16[4,256,128]{2,1,0:T(8,128)(2,1)S(1)}, u32[]{:S(2)}, u32[]{:S(2)}) collective-permute-start(bf16[4,256,128]{2,1,0:T(8,128)(2,1)S(1)} %collective-permute-done.6.refs_1_), channel_id=1, source_target_pairs={{0,1},{1,0},{2,3},{3,2},{4,5},{5,4},{6,7},{7,6},{8,9},{9,8},{10,11... | collective-permute-start | bytes 786440 | tf_op jit(solution)/shard_map/ppermute | solution.py:41
  27.1 12.0 %collective-permute-start.14 = (bf16[8,256,128]{2,1,0:T(8,128)(2,1)S(1)}, bf16[8,256,128]{2,1,0:T(8,128)(2,1)S(1)}, u32[]{:S(2)}, u32[]{:S(2)}) collective-permute-start(bf16[8,256,128]{2,1,0:T(8,128)(2,1)S(1)} %get-tuple-element.37.low_ref), channel_id=1, source_target_pairs={{0,1},{1,0},{2,3},{3,2},{4,5},{5,4},{6,7},{7,6},{8,9},{9,8},{10,11... | collective-permute-start | bytes 1572872 | tf_op jit(solution)/shard_map/ppermute | solution.py:41
  27.1 6.9 %collective-permute-start.15 = (bf16[2,256,128]{2,1,0:T(8,128)(2,1)S(1)}, bf16[2,256,128]{2,1,0:T(8,128)(2,1)S(1)}, u32[]{:S(2)}, u32[]{:S(2)}) collective-permute-start(bf16[2,256,128]{2,1,0:T(8,128)(2,1)S(1)} %get-tuple-element.42), channel_id=1, source_target_pairs={{0,4},{4,8},{8,12},{12,28},{28,24},{24,20},{20,16},{16,0},{1,5},{5... | collective-permute-start | bytes 393224 | tf_op jit(solution)/shard_map/ppermute | solution.py:430
  27.6 6.4 %collective-permute-start.16 = (bf16[2,256,128]{2,1,0:T(8,128)(2,1)S(1)}, bf16[2,256,128]{2,1,0:T(8,128)(2,1)S(1)}, u32[]{:S(2)}, u32[]{:S(2)}) collective-permute-start(bf16[2,256,128]{2,1,0:T(8,128)(2,1)S(1)} %get-tuple-element.43), channel_id=1, source_target_pairs={{4,0},{8,4},{12,8},{28,12},{24,28},{20,24},{16,20},{0,16},{5,1},{9... | collective-permute-start | bytes 393224 | tf_op jit(solution)/shard_map/ppermute | solution.py:431
  29.7 7.1 %collective-permute-start.18 = (bf16[2,256,128]{2,1,0:T(8,128)(2,1)S(1)}, bf16[2,256,128]{2,1,0:T(8,128)(2,1)S(1)}, u32[]{:S(2)}, u32[]{:S(2)}) collective-permute-start(bf16[2,256,128]{2,1,0:T(8,128)(2,1)S(1)} %get-tuple-element.45), channel_id=1, source_target_pairs={{0,4},{4,8},{8,12},{12,28},{28,24},{24,20},{20,16},{16,0},{1,5},{5... | collective-permute-start | bytes 393224 | tf_op jit(solution)/shard_map/ppermute | solution.py:430
  29.7 7.5 %collective-permute-start.19 = (bf16[2,256,128]{2,1,0:T(8,128)(2,1)S(1)}, bf16[2,256,128]{2,1,0:T(8,128)(2,1)S(1)}, u32[]{:S(2)}, u32[]{:S(2)}) collective-permute-start(bf16[2,256,128]{2,1,0:T(8,128)(2,1)S(1)} %get-tuple-element.46), channel_id=1, source_target_pairs={{4,0},{8,4},{12,8},{28,12},{24,28},{20,24},{16,20},{0,16},{5,1},{9... | collective-permute-start | bytes 393224 | tf_op jit(solution)/shard_map/ppermute | solution.py:431
  34.0 10.6 %collective-permute-start.12 = (bf16[4,256,128]{2,1,0:T(8,128)(2,1)S(1)}, bf16[4,256,128]{2,1,0:T(8,128)(2,1)S(1)}, u32[]{:S(2)}, u32[]{:S(2)}) collective-permute-start(bf16[4,256,128]{2,1,0:T(8,128)(2,1)S(1)} %get-tuple-element.35), channel_id=1, source_target_pairs={{0,4},{4,8},{8,12},{12,28},{28,24},{24,20},{20,16},{16,0},{1,5},{5... | collective-permute-start | bytes 786440 | tf_op jit(solution)/shard_map/ppermute | solution.py:430
  34.0 10.6 %collective-permute-start.13 = (bf16[4,256,128]{2,1,0:T(8,128)(2,1)S(1)}, bf16[4,256,128]{2,1,0:T(8,128)(2,1)S(1)}, u32[]{:S(2)}, u32[]{:S(2)}) collective-permute-start(bf16[4,256,128]{2,1,0:T(8,128)(2,1)S(1)} %get-tuple-element.36), channel_id=1, source_target_pairs={{4,0},{8,4},{12,8},{28,12},{24,28},{20,24},{16,20},{0,16},{5,1},{9... | collective-permute-start | bytes 786440 | tf_op jit(solution)/shard_map/ppermute | solution.py:431
  36.8 6.4 %collective-permute-start.17 = (bf16[2,256,128]{2,1,0:T(8,128)(2,1)S(1)}, bf16[2,256,128]{2,1,0:T(8,128)(2,1)S(1)}, u32[]{:S(2)}, u32[]{:S(2)}) collective-permute-start(bf16[2,256,128]{2,1,0:T(8,128)(2,1)S(1)} %merge.3), channel_id=1, source_target_pairs={{0,2},{2,0},{1,3},{3,1},{4,6},{6,4},{5,7},{7,5},{8,10},{10,8},{9,1... | collective-permute-start | bytes 393224 | tf_op jit(solution)/shard_map/ppermute | solution.py:41
  37.4 7.3 %collective-permute-start.20 = (bf16[2,256,128]{2,1,0:T(8,128)(2,1)S(1)}, bf16[2,256,128]{2,1,0:T(8,128)(2,1)S(1)}, u32[]{:S(2)}, u32[]{:S(2)}) collective-permute-start(bf16[2,256,128]{2,1,0:T(8,128)(2,1)S(1)} %merge.4), channel_id=1, source_target_pairs={{0,2},{2,0},{1,3},{3,1},{4,6},{6,4},{5,7},{7,5},{8,10},{10,8},{9,1... | collective-permute-start | bytes 393224 | tf_op jit(solution)/shard_map/ppermute | solution.py:41
  (4 other events, 22.6 us)
